TPU v7x, 32 devices: a whole 2x2x4 slice. The times are simulated.
32 devices in a mesh: seq: 8 (over z, y), tp: 4 (over x, core).
Axes of the slice: x: 2, y: 2, z: 4, core: 2. Of those that a mesh axis runs over, the one named last changes fastest.
Arguments:
- inputs: bfloat16 [16, 1024, 768], P(None, 'seq'), may hold values from -6 to 6
- lengths: int32 [16], replicated, may hold values from 256 to 1024, as said below
- first_gain: float32 [768], replicated, may hold values from 0.5 to 1.5
- query_weight: bfloat16 [768, 768], P(None, 'tp'), may hold values from -0.21875 to 0.21875
- key_weight: bfloat16 [768, 768], P(None, 'tp'), may hold values from -0.21875 to 0.21875
- value_weight: bfloat16 [768, 768], P(None, 'tp'), may hold values from -0.21875 to 0.21875
- shift_taps: float32 [4, 768], P(None, 'tp'), may hold values from -3 to 3
- state_coef: float32 [768, 64], P('tp'), may hold values from -0.1875 to 0.1875
- state_rate: float32 [768, 64], P('tp'), may hold values from 0.00048828125 to 0.2
- skip_gain: float32 [768], P('tp'), may hold values from -3 to 3
- project_weight: bfloat16 [768, 768], P('tp'), may hold values from -0.21875 to 0.21875
- second_gain: float32 [768], replicated, may hold values from 0.5 to 1.5
- up_weight: bfloat16 [768, 3072], P(None, 'tp'), may hold values from -0.21875 to 0.21875
- down_weight: bfloat16 [3072, 768], P('tp'), may hold values from -0.109375 to 0.109375
- cotangent: bfloat16 [16, 1024, 768], P(None, 'seq'), may hold values from -6 to 6
Outputs:
- block_out: float32 [16, 1024, 768], P(None, 'seq')
- grad_inputs: float32 [16, 1024, 768], P(None, 'seq')
- grad_first: float32 [768], replicated
- grad_query: float32 [768, 768], P(None, 'tp')
- grad_key: float32 [768, 768], P(None, 'tp')
- grad_value: float32 [768, 768], P(None, 'tp')
- grad_taps: float32 [4, 768], P(None, 'tp')
- grad_coef: float32 [768, 64], P('tp')
- grad_rate: float32 [768, 64], P('tp')
- grad_skip: float32 [768], P('tp')
- grad_project: float32 [768, 768], P('tp')
- grad_second: float32 [768], replicated
- grad_up: float32 [768, 3072], P(None, 'tp')
- grad_down: float32 [3072, 768], P('tp')
Inputs may be any that keep to these rules, and one draw needn't show every extreme that they name: `lengths`: one of the 16 sequences, which one drawn from the seed, has exactly 1024 tokens; positions from a sequence's length on are padding.
All inputs are finite; a program needn't handle non-finite values.
Results may differ from a plain program's by a relative error of at most 0.0075.
Values sent between devices are 32-bit elements; how exact they have to be, the bound alone decides.
No kernel may reach another device: no remote copies, remote signals or barrier semaphores. Data moves between devices by JAX's collectives and lax.ppermute only.
A program may use at most 192 MiB of HBM per device.

v0:
```python
import jax
import jax.numpy as jnp
from jax import lax
from jax.sharding import PartitionSpec as P

exact_mode = lax.Precision.HIGHEST


def passed_along(x, axis, by):
    count = lax.axis_size(axis)
    pairs = [(i, i + by) for i in range(count) if 0 <= i + by < count]
    return lax.ppermute(x, axis, pairs)


def layer_norm(rows, gain):
    center = rows - jnp.mean(rows, axis=-1, keepdims=True)
    spread = jnp.mean(center * center, axis=-1, keepdims=True)
    return center * lax.rsqrt(spread + 1e-05) * gain


def kernel_values(coef, rate, freq, parity, total, length):
    half = jnp.pi * freq / total
    below = jnp.sin(half)
    square = (below * below)[:, None, None]
    whole = jnp.sin(2.0 * half)[:, None, None]
    decay = jnp.exp(-rate)
    gap = -jnp.expm1(-rate)
    ending = jnp.exp(-rate * length)
    numer = 1.0 - parity[:, None, None] * ending
    denom = gap * gap + 4.0 * decay * square
    real_term = numer * (gap + 2.0 * decay * square) / denom
    imag_term = -numer * decay * whole / denom
    return (jnp.sum(coef * real_term, axis=-1), jnp.sum(coef * imag_term, axis=-1))


def angles(left, right, modulus):
    return 2.0 * jnp.pi / modulus * (left[:, None] * right[None, :] % modulus).astype(jnp.float32)


def project(left, right):
    return jnp.einsum("btd,de->bte", left, right, preferred_element_type=jnp.float32)


def to_bins(signal, num_dev, place):
    num_seqs, block_len, channels = signal.shape
    per_dev = block_len // num_dev
    span_len = 2 * num_dev
    total = span_len * block_len
    parted = lax.all_to_all(
        signal.reshape(num_seqs, 1, block_len, channels),
        "seq",
        split_axis=2,
        concat_axis=1,
        tiled=True,
    )
    outer = angles(jnp.arange(num_dev), jnp.arange(span_len), span_len)
    first_re = jnp.einsum("bpmc,pq->bqmc", parted, jnp.cos(outer), precision=exact_mode)
    first_im = -jnp.einsum("bpmc,pq->bqmc", parted, jnp.sin(outer), precision=exact_mode)
    twist = angles(jnp.arange(span_len), place * per_dev + jnp.arange(per_dev), total)
    twist_cos = jnp.cos(twist)[None, :, :, None]
    twist_sin = jnp.sin(twist)[None, :, :, None]
    turned_re = first_re * twist_cos + first_im * twist_sin
    turned_im = first_im * twist_cos - first_re * twist_sin
    joined = lax.all_to_all(
        jnp.stack([turned_re, turned_im]), "seq", split_axis=2, concat_axis=3, tiled=True
    )
    wave = angles(jnp.arange(block_len), jnp.arange(block_len), block_len)
    wave_cos = jnp.cos(wave)
    wave_sin = jnp.sin(wave)
    spec_re = jnp.einsum("bqmc,mj->bqjc", joined[0], wave_cos, precision=exact_mode) + jnp.einsum(
        "bqmc,mj->bqjc", joined[1], wave_sin, precision=exact_mode
    )
    spec_im = jnp.einsum("bqmc,mj->bqjc", joined[1], wave_cos, precision=exact_mode) - jnp.einsum(
        "bqmc,mj->bqjc", joined[0], wave_sin, precision=exact_mode
    )
    return (spec_re, spec_im)


def from_bins(spec_re, spec_im, num_dev, place):
    num_seqs, bin_rows, block_len, channels = spec_re.shape
    span_len = 2 * num_dev
    total = span_len * block_len
    wave = angles(jnp.arange(block_len), jnp.arange(block_len), block_len)
    wave_cos = jnp.cos(wave)
    wave_sin = jnp.sin(wave)
    back_re = jnp.einsum("bqjc,jm->bqmc", spec_re, wave_cos, precision=exact_mode) - jnp.einsum(
        "bqjc,jm->bqmc", spec_im, wave_sin, precision=exact_mode
    )
    back_im = jnp.einsum("bqjc,jm->bqmc", spec_re, wave_sin, precision=exact_mode) + jnp.einsum(
        "bqjc,jm->bqmc", spec_im, wave_cos, precision=exact_mode
    )
    twist = angles(place * bin_rows + jnp.arange(bin_rows), jnp.arange(block_len), total)
    twist_cos = jnp.cos(twist)[None, :, :, None]
    twist_sin = jnp.sin(twist)[None, :, :, None]
    turned_re = back_re * twist_cos - back_im * twist_sin
    turned_im = back_re * twist_sin + back_im * twist_cos
    parted = lax.all_to_all(
        jnp.stack([turned_re, turned_im]), "seq", split_axis=3, concat_axis=2, tiled=True
    )
    outer = angles(jnp.arange(span_len), jnp.arange(num_dev), span_len)
    times_re = (
        jnp.einsum("bqmc,qp->bpmc", parted[0], jnp.cos(outer), precision=exact_mode)
        - jnp.einsum("bqmc,qp->bpmc", parted[1], jnp.sin(outer), precision=exact_mode)
    ) / total
    joined = lax.all_to_all(times_re, "seq", split_axis=1, concat_axis=2, tiled=True)
    return joined.reshape(num_seqs, block_len, channels)


def local(
    inputs,
    lengths,
    first_gain,
    query_weight,
    key_weight,
    value_weight,
    shift_taps,
    state_coef,
    state_rate,
    skip_gain,
    project_weight,
    second_gain,
    up_weight,
    down_weight,
    cotangent,
):
    num_dev = lax.axis_size("seq")
    place = lax.axis_index("seq")
    num_seqs, block_len, width_all = inputs.shape
    tap_count = shift_taps.shape[0]
    seq_len = num_dev * block_len
    total = 2 * seq_len
    source = inputs.astype(jnp.float32)
    positions = place * block_len + jnp.arange(block_len)
    validity = (positions[None, :] < lengths[:, None]).astype(jnp.float32)[:, :, None]
    normed = layer_norm(source, first_gain).astype(jnp.bfloat16)
    queries = project(normed, query_weight)
    key_rows = project(normed, key_weight)
    values = project(normed, value_weight)
    tail = key_rows[:, block_len - (tap_count - 1) :, :]
    before = passed_along(tail, "seq", 1)
    extended = jnp.concatenate([before, key_rows], axis=1)
    shifted = jnp.zeros_like(key_rows)
    for offset in range(tap_count):
        shifted = (
            shifted
            + shift_taps[offset]
            * extended[:, tap_count - 1 - offset : tap_count - 1 - offset + block_len, :]
        )
    mixed_in = shifted * values
    channels = state_coef.shape[0]
    bin_index = place * 2 + jnp.arange(2)
    freq_int = (bin_index[:, None] + 2 * num_dev * jnp.arange(block_len)[None, :]).reshape(-1)
    freq = freq_int.astype(jnp.float32)
    parity = (1 - 2 * (freq_int % 2)).astype(jnp.float32)

    def kernel_part(coef, rate):
        part_re, part_im = kernel_values(coef, rate, freq, parity, total, seq_len)
        return (part_re.reshape(2, block_len, channels), part_im.reshape(2, block_len, channels))

    (kernel_re, kernel_im), kernel_pull = jax.vjp(kernel_part, state_coef, state_rate)
    spec_re, spec_im = to_bins(mixed_in, num_dev, place)
    conv = from_bins(
        spec_re * kernel_re - spec_im * kernel_im,
        spec_re * kernel_im + spec_im * kernel_re,
        num_dev,
        place,
    )
    state_out = conv + skip_gain * mixed_in
    gated_out = (queries * state_out).astype(jnp.bfloat16)
    mixer = lax.psum(project(gated_out, project_weight), "tp")
    residual = source + mixer
    second = layer_norm(residual, second_gain).astype(jnp.bfloat16)
    up_act = project(second, up_weight)
    hidden = jax.nn.gelu(up_act).astype(jnp.bfloat16)
    lowered = lax.psum(project(hidden, down_weight), "tp")
    block_out = validity * (residual + lowered)
    d_mlp = validity * cotangent.astype(jnp.float32)
    d_mlp_low = d_mlp.astype(jnp.bfloat16)
    grad_down = jnp.einsum("btf,btd->fd", hidden, d_mlp_low, preferred_element_type=jnp.float32)
    d_hidden = jnp.einsum("btd,fd->btf", d_mlp_low, down_weight, preferred_element_type=jnp.float32)
    gelu_value, gelu_pull = jax.vjp(jax.nn.gelu, up_act)
    d_up = gelu_pull(d_hidden)[0].astype(jnp.bfloat16)
    grad_up = jnp.einsum("btd,btf->df", second, d_up, preferred_element_type=jnp.float32)
    d_second = lax.psum(
        jnp.einsum("btf,df->btd", d_up, up_weight, preferred_element_type=jnp.float32), "tp"
    )
    norm_value, second_pull = jax.vjp(layer_norm, residual, second_gain)
    d_resid_norm, grad_second = second_pull(d_second)
    d_residual = d_mlp + d_resid_norm
    d_resid_low = d_residual.astype(jnp.bfloat16)
    grad_project = jnp.einsum(
        "btc,btd->cd", gated_out, d_resid_low, preferred_element_type=jnp.float32
    )
    d_gated = jnp.einsum(
        "btd,cd->btc", d_resid_low, project_weight, preferred_element_type=jnp.float32
    )
    d_queries = (d_gated * state_out).astype(jnp.bfloat16)
    d_state = d_gated * queries
    back_re, back_im = to_bins(d_state, num_dev, place)
    fore_re, fore_im = to_bins(lax.optimization_barrier(mixed_in), num_dev, place)
    grad_kernel_re = jnp.sum(back_re * fore_re + back_im * fore_im, axis=0) / total
    grad_kernel_im = jnp.sum(back_im * fore_re - back_re * fore_im, axis=0) / total
    grad_coef, grad_rate = kernel_pull((grad_kernel_re, grad_kernel_im))
    corr = from_bins(
        back_re * kernel_re + back_im * kernel_im,
        back_im * kernel_re - back_re * kernel_im,
        num_dev,
        place,
    )
    d_mixed = corr + skip_gain * d_state
    grad_skip = jnp.sum(d_state * mixed_in, axis=(0, 1))
    d_values = (d_mixed * shifted).astype(jnp.bfloat16)
    d_shifted = d_mixed * values
    d_extended = jnp.zeros_like(extended)
    tap_sums = []
    for offset in range(tap_count):
        d_extended = d_extended + jnp.pad(
            shift_taps[offset] * d_shifted, ((0, 0), (tap_count - 1 - offset, offset), (0, 0))
        )
        tap_sums.append(
            jnp.sum(
                d_shifted
                * extended[:, tap_count - 1 - offset : tap_count - 1 - offset + block_len, :],
                axis=(0, 1),
            )
        )
    grad_taps = jnp.stack(tap_sums)
    spill = passed_along(d_extended[:, : tap_count - 1, :], "seq", -1)
    d_keys = (
        d_extended[:, tap_count - 1 :, :]
        + jnp.pad(spill, ((0, 0), (block_len - tap_count + 1, 0), (0, 0)))
    ).astype(jnp.bfloat16)
    grad_query = jnp.einsum("btd,btc->dc", normed, d_queries, preferred_element_type=jnp.float32)
    grad_key = jnp.einsum("btd,btc->dc", normed, d_keys, preferred_element_type=jnp.float32)
    grad_value = jnp.einsum("btd,btc->dc", normed, d_values, preferred_element_type=jnp.float32)
    d_first_part = jnp.einsum(
        "btc,dc->btd", d_queries, query_weight, preferred_element_type=jnp.float32
    )
    d_first_part = d_first_part + jnp.einsum(
        "btc,dc->btd", d_keys, key_weight, preferred_element_type=jnp.float32
    )
    d_first_part = d_first_part + jnp.einsum(
        "btc,dc->btd", d_values, value_weight, preferred_element_type=jnp.float32
    )
    d_first = lax.psum(d_first_part, "tp")
    first_value, first_pull = jax.vjp(layer_norm, source, first_gain)
    d_input_norm, grad_first = first_pull(d_first)
    grad_inputs = d_residual + d_input_norm
    (
        grad_first,
        grad_query,
        grad_key,
        grad_value,
        grad_taps,
        grad_coef,
        grad_rate,
        grad_skip,
        grad_project,
        grad_second,
        grad_up,
        grad_down,
    ) = lax.psum(
        (
            grad_first,
            grad_query,
            grad_key,
            grad_value,
            grad_taps,
            grad_coef,
            grad_rate,
            grad_skip,
            grad_project,
            grad_second,
            grad_up,
            grad_down,
        ),
        "seq",
    )
    return (
        block_out,
        grad_inputs,
        grad_first,
        grad_query,
        grad_key,
        grad_value,
        grad_taps,
        grad_coef,
        grad_rate,
        grad_skip,
        grad_project,
        grad_second,
        grad_up,
        grad_down,
    )


def solution(mesh):
    return jax.shard_map(
        local,
        mesh=mesh,
        in_specs=(
            P(None, "seq", None),
            P(),
            P(),
            P(None, "tp"),
            P(None, "tp"),
            P(None, "tp"),
            P(None, "tp"),
            P("tp", None),
            P("tp", None),
            P("tp"),
            P("tp", None),
            P(),
            P(None, "tp"),
            P("tp", None),
            P(None, "seq", None),
        ),
        out_specs=(
            P(None, "seq", None),
            P(None, "seq", None),
            P(),
            P(None, "tp"),
            P(None, "tp"),
            P(None, "tp"),
            P(None, "tp"),
            P("tp", None),
            P("tp", None),
            P("tp"),
            P("tp", None),
            P(),
            P(None, "tp"),
            P("tp", None),
        ),
        check_vma=False,
    )
```

profile of v0, /device:TPU:0, one launch (start us, length us, event | category | flops | bytes accessed | tf_op | source)
XLA Modules:
  0.0 2281.5 jit_solution(13198516228330018810)
XLA Ops:
  23.4 9.7 fusion.355
  35.1 7.1 all-to-all-start
  42.4 46.5 %all-to-all-done = f32[16,1,128,192]{3,0,1,2:T(8,128)S(1)} async-done(((f32[16,1,128,192]{3,0,1,2:T(8,128)}), f32[16,1,128,192]{3,0,1,2:T(8,128)S(1)}, u32[]{:S(2)}, u32[]{:S(2)}) %all-to-all-start) | async-done | bytes 1572896 | tf_op jit(solution)/shard_map/all_to_all | solution.py:49
  93.2 5.3 add_bitcast_fusion.2
  100.1 8.3 copy.229
  108.4 5.1 all-to-all-start.1
  114.4 14.0 multiply_reduce_fusion.7
  128.5 167.1 %all-to-all-done.1 = f32[2,16,16,16,192]{4,3,1,0,2:T(8,128)} async-done(((f32[2,16,16,16,192]{4,3,1,0,2:T(8,128)}), f32[2,16,16,16,192]{4,3,1,0,2:T(8,128)}, u32[]{:S(2)}, u32[]{:S(2)}) %all-to-all-start.1) | async-done | bytes 6291488 | tf_op jit(solution)/shard_map/all_to_all | solution.py:64
  301.7 6.8 fusion.137
  308.6 7.2 fusion.135
  315.8 6.8 convolution_add_fusion.4
  322.6 7.0 convolution_subtract_fusion.4
  347.2 12.7 copy.239
  359.9 186.8 %all_to_all.129 = f32[2,16,2,128,192]{4,2,1,0,3:T(2,128)S(1)} all-to-all(f32[2,16,2,128,192]{4,2,1,0,3:T(2,128)} %copy.239), channel_id=1, replica_groups=mesh['seq'=8,'tp'=4] {'seq'}, dimensions={3} | all-to-all | bytes 12582912 | tf_op jit(solution)/shard_map/all_to_all | solution.py:97
  554.9 5.3 copy.241
  560.2 6.0 squeeze.38
  570.5 5.3 copy.242
  575.8 6.0 squeeze.39
  586.6 51.4 %all_to_all.130 = f32[16,8,16,192]{3,2,0,1:T(8,128)S(1)} all-to-all(f32[16,8,16,192]{3,2,0,1:T(8,128)S(1)} %copy.243), channel_id=1, replica_groups=mesh['seq'=8,'tp'=4] {'seq'}, dimensions={1} | all-to-all | bytes 3145728 | tf_op jit(solution)/shard_map/all_to_all | solution.py:105
  642.3 5.2 multiply_convert_fusion.4
  652.8 117.9 %all-reduce.14.cloned.1.call-done = f32[16,128,768]{2,1,0:T(8,128)} async-done(((f32[16,128,768]{2,1,0:T(8,128)}), f32[16,128,768]{2,1,0:T(8,128)}) %all-reduce.14.cloned.1.call-update) | async-done | bytes 6291472 | tf_op jit(solution)/shard_map/psum | solution.py:170
  779.6 6.1 fusion.26
  793.9 5.5 all-to-all-start.8
  799.4 112.5 %all-reduce.16.cloned.1.call-done = f32[16,128,768]{2,1,0:T(8,128)} async-done(((f32[16,128,768]{2,1,0:T(8,128)}), f32[16,128,768]{2,1,0:T(8,128)}) %all-reduce.16.cloned.1.call-update) | async-done | bytes 6291472 | tf_op jit(solution)/shard_map/psum | solution.py:184
  911.9 6.4 multiply_reduce_fusion.8
  934.5 6.0 all-to-all-start.4
  940.5 6.4 fusion.52
  946.9 6.4 fusion.54
  953.3 35.3 %all-to-all-done.4 = f32[16,1,128,192]{3,0,1,2:T(8,128)} async-done(((f32[16,1,128,192]{3,0,1,2:T(8,128)}), f32[16,1,128,192]{3,0,1,2:T(8,128)}, u32[]{:S(2)}, u32[]{:S(2)}) %all-to-all-start.4) | async-done | bytes 1572896 | tf_op jit(solution)/shard_map/all_to_all | solution.py:49
  988.6 6.2 fusion.56
  994.8 10.9 add_bitcast_fusion
  1007.3 8.2 copy.250
  1024.9 8.2 copy.269
  1033.1 169.4 %all-to-all-done.5 = f32[2,16,16,16,192]{4,3,1,0,2:T(8,128)} async-done(((f32[2,16,16,16,192]{4,3,1,0,2:T(8,128)}), f32[2,16,16,16,192]{4,3,1,0,2:T(8,128)}, u32[]{:S(2)}, u32[]{:S(2)}) %all-to-all-start.5) | async-done | bytes 6291488 | tf_op jit(solution)/shard_map/all_to_all | solution.py:64
  1202.5 5.4 all-to-all-start.9
  1214.0 6.8 fusion.131
  1220.8 7.0 fusion.129
  1227.8 6.8 convolution_add_fusion.2
  1234.7 7.0 convolution_subtract_fusion.2
  1259.4 12.7 copy.256
  1272.1 117.5 %all-to-all-done.9 = f32[2,16,16,16,192]{4,3,1,0,2:T(8,128)} async-done(((f32[2,16,16,16,192]{4,3,1,0,2:T(8,128)}), f32[2,16,16,16,192]{4,3,1,0,2:T(8,128)}, u32[]{:S(2)}, u32[]{:S(2)}) %all-to-all-start.9) | async-done | bytes 6291488 | tf_op jit(solution)/shard_map/all_to_all | solution.py:64
  1389.6 5.1 all-to-all-start.6
  1394.7 8.2 convolution_bitcast_fusion
  1402.9 5.8 fusion.71
  1408.7 5.0 fusion.64
  1421.4 8.1 copy.334
  1429.5 147.4 %all-to-all-done.6 = f32[2,16,2,128,192]{4,2,1,0,3:T(2,128)} async-done(((f32[2,16,2,128,192]{4,2,1,0,3:T(2,128)}), f32[2,16,2,128,192]{4,2,1,0,3:T(2,128)}, u32[]{:S(2)}, u32[]{:S(2)}) %all-to-all-start.6) | async-done | bytes 6291488 | tf_op jit(solution)/shard_map/all_to_all | solution.py:97
  1576.9 8.6 copy.257
  1588.9 5.3 copy.258
  1594.2 6.0 squeeze.42
  1604.3 5.3 copy.259
  1609.6 6.1 squeeze.43
  1630.8 7.0 fusion.125
  1637.8 7.0 fusion.123
  1644.8 6.9 convolution_add_fusion
  1651.8 8.3 fusion.35
  1661.4 12.7 all-to-all-done.7
  1680.2 8.6 multiply_reduce_fusion.14
  1703.7 8.2 add_add_fusion.3
  1713.3 35.0 %fusion.30 = (f32[192,64]{1,0:T(8,128)S(1)}, f32[192,64]{1,0:T(8,128)S(1)}, f32[192,64]{1,0:T(8,128)S(1)}, f32[192,64]{1,0:T(8,128)S(1)}, f32[192,64]{1,0:T(8,12...) fusion(f32[192,64]{1,0:T(8,128)S(1)} %copy-done.44, f32[192,64]{1,0:T(8,128)S(1)} %copy-done.48, ...), kind=kLoop, calls=%fused_computation.71 | loop fusion | flops 144605184 | bytes 1133568 | tf_op jit(solution)/shard_map/transpose(jvp())/reduce_sum | solution.py:30
  1755.2 178.1 %all-reduce.22.cloned.1.call-done = (f32[16,128,768]{2,1,0:T(8,128)}, f32[16,128,768]{2,1,0:T(8,128)}) async-done(((f32[16,128,768]{2,1,0:T(8,128)}, f32[16,128,768]{2,1,0:T(8,128)}), (f32[16,128,768]{2,1,0:T(8,128)}, f32[16,128,768]{2,1,0:T(8,128)})) %all-reduce.22.cloned.1.call-update) | async-done | bytes 12582928 | tf_op jit(solution)/shard_map/psum | solution.py:175
  1948.5 15.6 add_add_fusion.2
  1964.1 51.2 %all-reduce.18.cloned.1.call-done = (f32[768]{0:T(1024)}, f32[4,192]{1,0:T(4,128)}, f32[192,64]{1,0:T(8,128)}, f32[192,64]{1,0:T(8,128)}, f32[192]{0:T(256)}, /*index=5*/f32[768]{0:T(1024)}) async-done(((f32[768]{0:T(1024)}, f32[4,192]{1,0:T(4,128)}, f32[192,64]{1,0:T(8,128)}, f32[192,64]{1,0:T(8,128)}, f32[192]{0:T(256)}, /*index=5*/f32[768]{0:T(1024)}), (f32[768]{0:T(1024)}, f32[4,192]{1,0:T(4,128)}, ...) | async-done | bytes 108304 | tf_op jit(solution)/shard_map/psum | solution.py:262
  2018.5 241.1 %all-reduce.20.cloned.1.call-done = (f32[768,192]{0,1:T(8,128)}, f32[768,192]{0,1:T(8,128)}, f32[768,192]{0,1:T(8,128)}, f32[192,768]{1,0:T(8,128)}, f32[768,768]{1,0:T(8,128)}, /*index=5*/f32[768,768]{1,0:T(8,128)}) async-done(((f32[768,192]{0,1:T(8,128)}, f32[768,192]{0,1:T(8,128)}, f32[768,192]{0,1:T(8,128)}, f32[192,768]{1,0:T(8,128)}, f32[768,768]{1,0:T(8,128)}, /*index=5*/f32[768,768]{1,0:T(8,128)}), ...) | async-done | bytes 7077904 | tf_op jit(solution)/shard_map/psum | solution.py:262
  (328 shorter events, 237.0 us)
Async XLA Ops:
  7.2 768.8 %copy-start = (bf16[768,768]{1,0:T(8,128)(2,1)S(1)}, bf16[768,768]{1,0:T(8,128)(2,1)}, u32[]{:S(2)}) copy-start(bf16[768,768]{1,0:T(8,128)(2,1)} %param.27) | copy-start | bytes 3538948
  10.1 632.1 %copy-start.63 = (f32[16,128]{1,0:T(8,128)}, f32[16,128]{1,0:T(8,128)S(1)}, u32[]{:S(2)}) copy-start(f32[16,128]{1,0:T(8,128)S(1)} %broadcast_multiply_fusion.7) | copy-start | bytes 24580
  11.3 631.0 %copy-start.69 = (f32[16,128]{1,0:T(8,128)}, f32[16,128]{1,0:T(8,128)S(1)}, u32[]{:S(2)}) copy-start(f32[16,128]{1,0:T(8,128)S(1)} %fusion.170) | copy-start | bytes 24580
  14.0 9.4 copy-start.59
  15.1 6.6 collective-permute-start
  20.0 13.1 copy-start.87
  20.0 13.1 copy-start.89
  20.0 13.1 copy-start.91
  20.1 13.1 copy-start.93
  35.1 53.7 %all-to-all-start = ((f32[16,1,128,192]{3,0,1,2:T(8,128)}), f32[16,1,128,192]{3,0,1,2:T(8,128)S(1)}, u32[]{:S(2)}, u32[]{:S(2)}) async-start(f32[16,1,128,192]{3,0,1,2:T(8,128)} %copy.225), calls=%async_computation | async-start | bytes 4194304 | tf_op jit(solution)/shard_map/all_to_all | solution.py:49
  108.4 187.1 %all-to-all-start.1 = ((f32[2,16,16,16,192]{4,3,1,0,2:T(8,128)}), f32[2,16,16,16,192]{4,3,1,0,2:T(8,128)}, u32[]{:S(2)}, u32[]{:S(2)}) async-start(f32[2,16,16,16,192]{4,3,1,0,2:T(8,128)} %copy.229), calls=%async_computation.1 | async-start | bytes 16777216 | tf_op jit(solution)/shard_map/all_to_all | solution.py:64
  113.6 657.2 %all-reduce.14.cloned.1.call-start = ((), (), s32[]{:S(2)}) async-start(), calls=%async_computation.10 | async-start | bytes 12582912 | tf_op jit(solution)/shard_map/psum | solution.py:170
  113.7 14.6 copy-start.53
  113.8 14.5 copy-start.39
  113.9 14.4 copy-start.80
  114.1 225.7 %copy-start.81 = (f32[2,128]{1,0:T(2,128)}, f32[2,128]{1,0:T(2,128)S(1)}, u32[]{:S(2)}) copy-start(f32[2,128]{1,0:T(2,128)S(1)} %get-tuple-element.113) | copy-start | bytes 3076
  114.1 225.7 %copy-start.83 = (f32[2,128]{1,0:T(2,128)}, f32[2,128]{1,0:T(2,128)S(1)}, u32[]{:S(2)}) copy-start(f32[2,128]{1,0:T(2,128)S(1)} %get-tuple-element.114) | copy-start | bytes 3076
  114.2 14.1 copy-start.78
  114.2 14.1 copy-start.79
  114.3 14.1 copy-start.41
  114.3 14.1 copy-start.43
  114.3 14.1 copy-start.45
  114.3 14.1 copy-start.47
  114.3 14.1 copy-start.49
  114.3 14.1 copy-start.51
  128.5 211.3 %copy-start.18 = (f32[2,128,192]{1,2,0:T(8,128)}, f32[2,128,192]{1,2,0:T(8,128)S(1)}, u32[]{:S(2)}) copy-start(f32[2,128,192]{1,2,0:T(8,128)S(1)} %get-tuple-element.120) | copy-start | bytes 589828
  128.5 211.3 %copy-start.20 = (f32[2,128,192]{1,2,0:T(8,128)}, f32[2,128,192]{1,2,0:T(8,128)S(1)}, u32[]{:S(2)}) copy-start(f32[2,128,192]{1,2,0:T(8,128)S(1)} %get-tuple-element.121) | copy-start | bytes 589828
  642.3 6.1 copy-start.37
  652.1 259.8 %all-reduce.16.cloned.1.call-start = ((), (), s32[]{:S(2)}) async-start(), calls=%async_computation.11 | async-start | bytes 12582912 | tf_op jit(solution)/shard_map/psum | solution.py:184
  779.6 6.1 copy-start.100
  793.9 140.6 %all-to-all-start.8 = ((f32[16,1,128,192]{3,0,1,2:T(8,128)}), f32[16,1,128,192]{3,0,1,2:T(8,128)S(1)}, u32[]{:S(2)}, u32[]{:S(2)}) async-start(f32[16,1,128,192]{3,0,1,2:T(8,128)} %copy.265), calls=%async_computation.8 | async-start | bytes 4194304 | tf_op jit(solution)/shard_map/all_to_all | solution.py:49
  911.9 6.4 copy-start.14
  934.5 54.1 %all-to-all-start.4 = ((f32[16,1,128,192]{3,0,1,2:T(8,128)}), f32[16,1,128,192]{3,0,1,2:T(8,128)}, u32[]{:S(2)}, u32[]{:S(2)}) async-start(f32[16,1,128,192]{3,0,1,2:T(8,128)} %copy.246), calls=%async_computation.4 | async-start | bytes 4194304 | tf_op jit(solution)/shard_map/all_to_all | solution.py:49
  988.6 6.2 copy-start.15
  1015.5 187.0 %all-to-all-start.5 = ((f32[2,16,16,16,192]{4,3,1,0,2:T(8,128)}), f32[2,16,16,16,192]{4,3,1,0,2:T(8,128)}, u32[]{:S(2)}, u32[]{:S(2)}) async-start(f32[2,16,16,16,192]{4,3,1,0,2:T(8,128)} %copy.250), calls=%async_computation.5 | async-start | bytes 16777216 | tf_op jit(solution)/shard_map/all_to_all | solution.py:64
  1202.5 187.1 %all-to-all-start.9 = ((f32[2,16,16,16,192]{4,3,1,0,2:T(8,128)}), f32[2,16,16,16,192]{4,3,1,0,2:T(8,128)}, u32[]{:S(2)}, u32[]{:S(2)}) async-start(f32[2,16,16,16,192]{4,3,1,0,2:T(8,128)} %copy.269), calls=%async_computation.9 | async-start | bytes 16777216 | tf_op jit(solution)/shard_map/all_to_all | solution.py:64
  1234.7 17.3 copy-start.6
  1234.7 7.1 copy-start.19
  1234.7 7.1 copy-start.21
  1241.7 10.2 copy-start.8
  1389.6 13.3 slice-start
  1389.6 187.3 %all-to-all-start.6 = ((f32[2,16,2,128,192]{4,2,1,0,3:T(2,128)}), f32[2,16,2,128,192]{4,2,1,0,3:T(2,128)}, u32[]{:S(2)}, u32[]{:S(2)}) async-start(f32[2,16,2,128,192]{4,2,1,0,3:T(2,128)} %copy.256), calls=%async_computation.6 | async-start | bytes 16777216 | tf_op jit(solution)/shard_map/all_to_all | solution.py:97
  1394.6 8.2 copy-start.99
  1394.7 8.2 slice-start.1
  1621.8 52.4 %all-to-all-start.7 = ((f32[16,8,16,192]{3,2,0,1:T(8,128)}), f32[16,8,16,192]{3,2,0,1:T(8,128)}, u32[]{:S(2)}, u32[]{:S(2)}) async-start(f32[16,8,16,192]{3,2,0,1:T(8,128)} %copy.260), calls=%async_computation.7 | async-start | bytes 4194304 | tf_op jit(solution)/shard_map/all_to_all | solution.py:105
  1626.1 307.2 %all-reduce.22.cloned.1.call-start = ((), (), s32[]{:S(2)}) async-start(), calls=%async_computation.14 | async-start | bytes 25165824 | tf_op jit(solution)/shard_map/psum | solution.py:175
  1644.8 6.9 copy-start.7
  1644.8 6.9 copy-start.9
  1660.7 19.4 copy-start.25
  1660.7 19.4 copy-start.86
  1680.1 8.6 copy-start.88
  1680.1 8.6 copy-start.90
  1680.1 8.6 copy-start.92
  1680.1 8.6 copy-start.94
  1694.4 6.0 collective-permute-start.1
  1712.0 37.0 %copy-start.54 = (f32[192,64]{1,0:T(8,128)S(1)}, f32[192,64]{1,0:T(8,128)}, u32[]{:S(2)}) copy-start(f32[192,64]{1,0:T(8,128)} %copy-done.53) | copy-start | bytes 147460
  1712.1 303.3 %all-reduce.18.cloned.1.call-start = ((), (), s32[]{:S(2)}) async-start(), calls=%async_computation.12 | async-start | bytes 419840 | tf_op jit(solution)/shard_map/psum | solution.py:262
  1751.0 182.3 %copy-start.76 = (f32[768]{0:T(1024)S(1)}, f32[768]{0:T(1024)}, u32[]{:S(2)}) copy-start(f32[768]{0:T(1024)} %param.17) | copy-start | bytes 9220
  1933.3 6.5 copy-start.11
  1933.3 6.5 copy-start.71
  1943.7 316.0 %all-reduce.20.cloned.1.call-start = ((), (), s32[]{:S(2)}) async-start(), calls=%async_computation.13 | async-start | bytes 14155776 | tf_op jit(solution)/shard_map/psum | solution.py:262
  2015.3 256.1 %copy-start.96 = (f32[768]{0:T(1024)S(1)}, f32[768]{0:T(1024)}, u32[]{:S(2)}) copy-start(f32[768]{0:T(1024)} %get-tuple-element.133) | copy-start | bytes 9220
  2259.7 12.3 copy-start.35
  2263.0 10.4 copy-start.34
  (55 other events, 174.6 us)
Sparse Core Ops, SparseCore 0:
  652.2 118.4 all-reduce.13
  792.1 119.7 all-reduce.15
  1712.2 221.1 all-reduce.21
  1943.8 71.4 all-reduce.17
  2022.2 237.4 all-reduce.19
where the time goes:
time: 2290 us; the launch traced here: 2280 us
  waiting for transfers between devices  1400 us (61%)
  matrix products  252 us (11%)
  blocking collectives  238 us (10%)
  local copies, waits for them, and re-layouts  198 us (9%)
  other arithmetic  128 us (6%)
  starting transfers between devices  50.5 us (2%)
    all_to_all x3, waiting for transfers between devices, to_bins(): lax.all_to_all(jnp.stack([turned_re, turned_im]), 'seq', split_axis=2, co...  454 us
    psum x2, waiting for transfers between devices, local(): lax.psum((grad_first, grad_query, grad_key, grad_value, grad_taps, grad_c...  292 us
    all_to_all x1, blocking collectives, from_bins(): lax.all_to_all(jnp.stack([turned_re, turned_im]), 'seq', split_axis=3, co...  187 us
    psum x1, waiting for transfers between devices, local(): lowered = lax.psum(project(hidden, down_weight), 'tp')  178 us
    all_to_all x1, waiting for transfers between devices, from_bins(): lax.all_to_all(jnp.stack([turned_re, turned_im]), 'seq', split_axis=3, co...  147 us
    psum x1, waiting for transfers between devices, local(): mixer = lax.psum(project(gated_out, project_weight), 'tp')  118 us
    psum x1, waiting for transfers between devices, local(): lax.psum(jnp.einsum('btf,df->btd', d_up, up_weight, preferred_element_typ...  113 us
    all_to_all x3, waiting for transfers between devices, to_bins(): lax.all_to_all(signal.reshape(num_seqs, 1, block_len, channels), 'seq', s...  81.8 us
  transfers between devices with their start and end apart: 15, of which 14 were waited for; matrix products, arithmetic and copies ran while one was open for 11% of the time, Pallas kernels for 0%

commit v1 on v0

v1 whole, which is shorter than its diff:
```python
import jax
import jax.numpy as jnp
from jax import lax
from jax.experimental import pallas as pl
from jax.experimental.pallas import tpu as pltpu
from jax.sharding import PartitionSpec as P

LANES = 128
GROUP = 16
BF = jnp.bfloat16
F32 = jnp.float32


def iota2(axis):
    return lax.broadcasted_iota(jnp.int32, (LANES, LANES), axis)


def strided(ref, c, rows):
    return ref[pl.ds(c, rows, stride=GROUP), :]


def lag_rows(block, edge, offset, lane):
    return pltpu.roll(jnp.where(lane < LANES - offset, block, edge), offset, 1)


def unpack_tail(tail, b, taps):
    return pltpu.roll(tail, (LANES - (taps - 1) * (b + 1)) % LANES, 1)


def shift_sum(block, tail, b, taps_ref, taps, lane):
    edge = unpack_tail(tail, b, taps)
    total = taps_ref[:, 0:1] * block
    for offset in range(1, taps):
        total = total + taps_ref[:, offset : offset + 1] * lag_rows(block, edge, offset, lane)
    return total


def fwd_local_kernel(
    k_ref, v_ref, tail_ref, taps_ref, rate_ref, kern_ref, y_ref, h_ref, h1_ref, mix_ref, out_ref
):
    batch = k_ref.shape[0]
    taps = taps_ref.shape[1]
    lane = lax.broadcasted_iota(jnp.int32, (GROUP, LANES), 1)
    tail = tail_ref[...]
    for b in range(batch):
        mixed = shift_sum(k_ref[b], tail, b, taps_ref, taps, lane) * v_ref[b]
        mix_ref[b * GROUP : (b + 1) * GROUP, :] = mixed
    row = iota2(0)
    col = iota2(1)
    away = (LANES - 1 - row).astype(F32)
    low_half = lax.broadcasted_iota(jnp.int32, (batch, LANES), 1) < LANES // 2
    for p in range(GROUP // 2):
        xs = []
        for c in (2 * p, 2 * p + 1):
            x = strided(mix_ref, c, batch).astype(BF)
            xs.append(x)
            spread = jnp.broadcast_to(kern_ref[c : c + 1, :], (LANES, LANES))
            toep = pltpu.roll(spread, 0, 1, stride=1, stride_axis=0)
            toep = jnp.where(col >= row, toep, 0.0).astype(BF)
            out_ref[pl.ds(c, batch, stride=GROUP), :] = jnp.dot(
                x, toep, preferred_element_type=F32
            )
        decay = jnp.exp(-rate_ref[p : p + 1, :] * away)
        both = jnp.concatenate(xs, axis=0)
        grown = jnp.dot(both, decay.astype(BF), preferred_element_type=F32)
        h_ref[p] = jnp.where(low_half, grown[:batch], grown[batch:])
        grown = jnp.dot(both, (decay * away).astype(BF), preferred_element_type=F32)
        h1_ref[p] = jnp.where(low_half, grown[:batch], grown[batch:])
    for b in range(batch):
        y_ref[b] = out_ref[b * GROUP : (b + 1) * GROUP, :]


def fwd_post_kernel(
    y_ref, hin_ref, coef_ref, rate_ref, k_ref, v_ref, tail_ref, taps_ref, q_ref, skip_ref,
    state_ref, gated_ref, out_ref,
):
    batch = k_ref.shape[0]
    taps = taps_ref.shape[1]
    ahead = (iota2(0) + 1).astype(F32)
    low_half = lax.broadcasted_iota(jnp.int32, (batch, LANES), 1) < LANES // 2
    for p in range(GROUP // 2):
        grow = jnp.exp(-rate_ref[p : p + 1, :] * ahead).astype(BF)
        h = hin_ref[p] * coef_ref[p : p + 1, :]
        both = jnp.concatenate([jnp.where(low_half, h, 0.0), jnp.where(low_half, 0.0, h)], axis=0)
        cross = lax.dot_general(
            both.astype(BF), grow, (((1,), (1,)), ((), ())), preferred_element_type=F32
        )
        out_ref[pl.ds(2 * p, batch, stride=GROUP), :] = cross[:batch]
        out_ref[pl.ds(2 * p + 1, batch, stride=GROUP), :] = cross[batch:]
    lane = lax.broadcasted_iota(jnp.int32, (GROUP, LANES), 1)
    tail = tail_ref[...]
    for b in range(batch):
        mixed = shift_sum(k_ref[b], tail, b, taps_ref, taps, lane) * v_ref[b]
        state = y_ref[b] + out_ref[b * GROUP : (b + 1) * GROUP, :] + skip_ref[...] * mixed
        state_ref[b] = state
        gated_ref[b] = (q_ref[b] * state).astype(BF)


def bwd_local_kernel(
    dg_ref, q_ref, state_ref, k_ref, v_ref, tail_ref, taps_ref, skip_ref, rate_ref, kern_ref,
    dq_ref, dx_ref, g_ref, g1_ref, lag_ref, s0_ref, s1_ref, x_scr, d_scr, out_ref,
):
    batch = k_ref.shape[0]
    taps = taps_ref.shape[1]
    lane = lax.broadcasted_iota(jnp.int32, (GROUP, LANES), 1)
    tail = tail_ref[...]
    for b in range(batch):
        x_scr[b * GROUP : (b + 1) * GROUP, :] = (
            shift_sum(k_ref[b], tail, b, taps_ref, taps, lane) * v_ref[b]
        )
        dg = dg_ref[b]
        dq_ref[b] = (dg * state_ref[b]).astype(BF)
        d_scr[b * GROUP : (b + 1) * GROUP, :] = dg * q_ref[b]
    row = iota2(0)
    col = iota2(1)
    mirror = jnp.where(row + col == LANES - 1, 1.0, 0.0).astype(BF)
    ahead = (row + 1).astype(F32)
    low_half = lax.broadcasted_iota(jnp.int32, (batch, LANES), 1) < LANES // 2
    low_row = lax.broadcasted_iota(jnp.int32, (1, LANES), 1) < LANES // 2
    for p in range(GROUP // 2):
        ds = []
        lags = []
        for c in (2 * p, 2 * p + 1):
            x = strided(x_scr, c, batch).astype(BF)
            d = strided(d_scr, c, batch).astype(BF)
            ds.append(d)
            spread = jnp.broadcast_to(kern_ref[c : c + 1, :], (LANES, LANES))
            toep = pltpu.roll(spread, 0, 1, stride=1, stride_axis=0)
            toep = jnp.where(col >= row, toep, 0.0).astype(BF)
            out_ref[pl.ds(c, batch, stride=GROUP), :] = lax.dot_general(
                d, toep, (((1,), (1,)), ((), ())), preferred_element_type=F32
            )
            x = jnp.dot(x, mirror, preferred_element_type=F32).astype(BF)
            pairs = lax.dot_general(x, d, (((0,), (0,)), ((), ())), preferred_element_type=F32)
            pairs = jnp.where(col + row >= LANES - 1, pairs, 0.0)
            pairs = pltpu.roll(pairs, 1, 1, stride=1, stride_axis=0)
            lag = jnp.sum(pairs, axis=0, keepdims=True)
            lag_ref[c : c + 1, :] = lag
            lags.append(lag)
        grow = jnp.exp(-rate_ref[p : p + 1, :] * ahead)
        grow_low = grow.astype(BF)
        grow1_low = (grow * ahead).astype(BF)
        both = jnp.concatenate(ds, axis=0)
        got = jnp.dot(both, grow_low, preferred_element_type=F32)
        g_ref[p] = jnp.where(low_half, got[:batch], got[batch:])
        got = jnp.dot(both, grow1_low, preferred_element_type=F32)
        g1_ref[p] = jnp.where(low_half, got[:batch], got[batch:])
        high = [lag.astype(BF).astype(F32) for lag in lags]
        lagrow = lax.broadcasted_iota(jnp.int32, (8, LANES), 0)
        stack = jnp.where(
            lagrow == 0, high[0], jnp.where(lagrow == 1, high[1],
            jnp.where(lagrow == 2, lags[0] - high[0], jnp.where(lagrow == 3, lags[1] - high[1], 0.0)))
        ).astype(BF)
        got = jnp.dot(stack, grow_low, preferred_element_type=F32)
        s0_ref[p : p + 1, :] = jnp.where(low_row, got[0:1] + got[2:3], got[1:2] + got[3:4])
        got = jnp.dot(stack, grow1_low, preferred_element_type=F32)
        s1_ref[p : p + 1, :] = jnp.where(low_row, got[0:1] + got[2:3], got[1:2] + got[3:4])
    for b in range(batch):
        sl = slice(b * GROUP, (b + 1) * GROUP)
        dx_ref[b] = out_ref[sl, :] + skip_ref[...] * d_scr[sl, :]


def bwd_post_kernel(
    dx_ref, gin_ref, coef_ref, rate_ref, k_ref, v_ref, tail_ref, taps_ref,
    dv_ref, ds_ref, head_ref, gtap_ref, out_ref,
):
    batch = k_ref.shape[0]
    taps = taps_ref.shape[1]
    away = (LANES - 1 - iota2(0)).astype(F32)
    low_half = lax.broadcasted_iota(jnp.int32, (batch, LANES), 1) < LANES // 2
    for p in range(GROUP // 2):
        decay = jnp.exp(-rate_ref[p : p + 1, :] * away).astype(BF)
        g = gin_ref[p] * coef_ref[p : p + 1, :]
        both = jnp.concatenate([jnp.where(low_half, g, 0.0), jnp.where(low_half, 0.0, g)], axis=0)
        cross = lax.dot_general(
            both.astype(BF), decay, (((1,), (1,)), ((), ())), preferred_element_type=F32
        )
        out_ref[pl.ds(2 * p, batch, stride=GROUP), :] = cross[:batch]
        out_ref[pl.ds(2 * p + 1, batch, stride=GROUP), :] = cross[batch:]
    lane = lax.broadcasted_iota(jnp.int32, (GROUP, LANES), 1)
    tail = tail_ref[...]
    head = jnp.zeros((GROUP, LANES), F32)
    sums = [jnp.zeros((GROUP, LANES), F32) for _ in range(taps)]
    for b in range(batch):
        block = k_ref[b]
        edge = unpack_tail(tail, b, taps)
        lagged = [block] + [lag_rows(block, edge, i, lane) for i in range(1, taps)]
        shifted = taps_ref[:, 0:1] * block
        for i in range(1, taps):
            shifted = shifted + taps_ref[:, i : i + 1] * lagged[i]
        d_mixed = dx_ref[b] + out_ref[b * GROUP : (b + 1) * GROUP, :]
        dv_ref[b] = (d_mixed * shifted).astype(BF)
        d_shifted = d_mixed * v_ref[b]
        ds_ref[b] = d_shifted
        for i in range(taps):
            sums[i] = sums[i] + d_shifted * lagged[i]
        start = (taps - 1) * b
        head = jnp.where(
            (lane >= start) & (lane < start + taps - 1), pltpu.roll(d_shifted, start, 1), head
        )
    head_ref[...] = head
    packed = jnp.zeros((GROUP, LANES), F32)
    for i in range(taps):
        packed = jnp.where(lane == i, jnp.sum(sums[i], axis=1, keepdims=True), packed)
    gtap_ref[...] = packed


def specs(batch, taps):
    return dict(
        act=pl.BlockSpec((batch, GROUP, LANES), lambda i: (0, i, 0)),
        row=pl.BlockSpec((GROUP, LANES), lambda i: (i, 0)),
        pair=pl.BlockSpec((GROUP // 2, LANES), lambda i: (i, 0)),
        state=pl.BlockSpec((GROUP // 2, batch, LANES), lambda i: (i, 0, 0)),
        taps=pl.BlockSpec((GROUP, taps), lambda i: (i, 0)),
        one=pl.BlockSpec((GROUP, 1), lambda i: (i, 0)),
    )


def shape(*dims, dtype=F32):
    return jax.ShapeDtypeStruct(dims, dtype)


def call(kernel, ins, outs, out_shapes, scratch, channels, args):
    return pl.pallas_call(
        kernel,
        grid=(channels // GROUP,),
        in_specs=ins,
        out_specs=outs,
        out_shape=out_shapes,
        scratch_shapes=scratch,
    )(*args)


def conv_calls(batch, channels, taps):
    s = specs(batch, taps)
    act, row, pair, state, tap, one = (s[n] for n in ("act", "row", "pair", "state", "taps", "one"))
    a = shape(batch, channels, LANES)
    alow = shape(batch, channels, LANES, dtype=BF)
    st = shape(channels // 2, batch, LANES)
    rows = shape(channels, LANES)
    pairs = shape(channels // 2, LANES)
    scr = pltpu.VMEM((batch * GROUP, LANES), F32)

    def fwd_local(k, v, tail, tap_rows, rate, kern):
        return call(fwd_local_kernel, [act, act, row, tap, pair, row], [act, state, state],
                    [a, st, st], [scr, scr], channels, (k, v, tail, tap_rows, rate, kern))

    def fwd_post(y, hin, coef, rate, k, v, tail, tap_rows, q, skip):
        return call(fwd_post_kernel, [act, state, pair, pair, act, act, row, tap, act, one],
                    [act, act], [a, alow], [scr], channels,
                    (y, hin, coef, rate, k, v, tail, tap_rows, q, skip))

    def bwd_local(dg, q, so, k, v, tail, tap_rows, skip, rate, kern):
        return call(bwd_local_kernel, [act, act, act, act, act, row, tap, one, pair, row],
                    [act, act, state, state, row, pair, pair], [alow, a, st, st, rows, pairs, pairs],
                    [scr, scr, scr], channels, (dg, q, so, k, v, tail, tap_rows, skip, rate, kern))

    def bwd_post(dx, gin, coef, rate, k, v, tail, tap_rows):
        return call(bwd_post_kernel, [act, state, pair, pair, act, act, row, tap],
                    [act, act, row, row], [alow, a, rows, rows], [scr], channels,
                    (dx, gin, coef, rate, k, v, tail, tap_rows))

    return fwd_local, fwd_post, bwd_local, bwd_post


def passed_along(x, axis, by):
    count = lax.axis_size(axis)
    pairs = [(i, i + by) for i in range(count) if 0 <= i + by < count]
    return lax.ppermute(x, axis, pairs)


def carried(own, decay, sign):
    count = lax.axis_size("seq")
    got = passed_along(own, "seq", sign)
    reach = 1
    while reach < count - 1:
        whole = own + decay(1) * got
        got = got + decay(reach) * passed_along(whole, "seq", sign * (reach + 1))
        reach = 2 * reach + 1
    return got


def layer_norm(rows, gain):
    center = rows - jnp.mean(rows, axis=-1, keepdims=True)
    spread = jnp.mean(center * center, axis=-1, keepdims=True)
    return center * lax.rsqrt(spread + 1e-05) * gain


def product(form, left, right):
    return jnp.einsum(form, left, right, preferred_element_type=F32)


def pack_edges(rows, lanes):
    num_seqs, channels, count = rows.shape
    flat = jnp.transpose(rows, (1, 0, 2)).reshape(channels, num_seqs * count)
    return jnp.pad(flat, ((0, 0), (0, lanes - num_seqs * count)))


def local(
    inputs,
    lengths,
    first_gain,
    query_weight,
    key_weight,
    value_weight,
    shift_taps,
    state_coef,
    state_rate,
    skip_gain,
    project_weight,
    second_gain,
    up_weight,
    down_weight,
    cotangent,
):
    num_dev = lax.axis_size("seq")
    place = lax.axis_index("seq")
    num_seqs, block_len, width_all = inputs.shape
    taps = shift_taps.shape[0]
    channels, states = state_coef.shape
    assert block_len == LANES and 2 * states == LANES and channels % GROUP == 0
    edge = taps - 1
    source = inputs.astype(F32)
    positions = place * block_len + jnp.arange(block_len)
    validity = (positions[None, :] < lengths[:, None]).astype(F32)[:, :, None]
    fwd_local, fwd_post, bwd_local, bwd_post = conv_calls(num_seqs, channels, taps)
    rate = state_rate.reshape(channels // 2, LANES)
    coef = state_coef.reshape(channels // 2, LANES)
    tap_rows = shift_taps.T
    skip = skip_gain[:, None]
    lag = jnp.arange(LANES).astype(F32)
    kern = jnp.sum(
        state_coef[:, :, None] * jnp.exp(-state_rate[:, :, None] * lag[None, None, :]), axis=1
    )

    def block_decay(count):
        return jnp.exp(-rate * (LANES * count))[:, None, :]

    normed = layer_norm(source, first_gain).astype(BF)
    queries = product("btd,dc->bct", normed, query_weight)
    keys = product("btd,dc->bct", normed, key_weight)
    values = product("btd,dc->bct", normed, value_weight)
    tail = passed_along(pack_edges(keys[:, :, block_len - edge :], LANES), "seq", 1)
    conv, own, own_lag = fwd_local(keys, values, tail, tap_rows, rate, kern)
    before = carried(own, block_decay, 1)
    state_out, gated_out = fwd_post(
        conv, before, coef, rate, keys, values, tail, tap_rows, queries, skip
    )
    mixer = lax.psum(product("bct,cd->btd", gated_out, project_weight), "tp")
    residual = source + mixer
    second = layer_norm(residual, second_gain).astype(BF)
    up_act = product("btd,df->btf", second, up_weight)
    hidden = jax.nn.gelu(up_act).astype(BF)
    lowered = lax.psum(product("btf,fd->btd", hidden, down_weight), "tp")
    block_out = validity * (residual + lowered)
    d_mlp = validity * cotangent.astype(F32)
    d_mlp_low = d_mlp.astype(BF)
    grad_down = product("btf,btd->fd", hidden, d_mlp_low)
    d_hidden = product("btd,fd->btf", d_mlp_low, down_weight)
    gelu_value, gelu_pull = jax.vjp(jax.nn.gelu, up_act)
    d_up = gelu_pull(d_hidden)[0].astype(BF)
    grad_up = product("btd,btf->df", second, d_up)
    d_second = lax.psum(product("btf,df->btd", d_up, up_weight), "tp")
    norm_value, second_pull = jax.vjp(layer_norm, residual, second_gain)
    d_resid_norm, grad_second = second_pull(d_second)
    d_residual = d_mlp + d_resid_norm
    d_resid_low = d_residual.astype(BF)
    grad_project = product("bct,btd->cd", gated_out, d_resid_low)
    d_gated = product("btd,cd->bct", d_resid_low, project_weight)
    d_queries, d_part, back, back_lag, lags, near, near_lag = bwd_local(
        d_gated, queries, state_out, keys, values, tail, tap_rows, skip, rate, kern
    )
    after = carried(back, block_decay, -1)
    d_values, d_shifted, head, grad_taps = bwd_post(
        d_part, after, coef, rate, keys, values, tail, tap_rows
    )
    grow = jnp.exp(rate)
    grad_coef = jnp.sum(before * back, axis=1) + grow * near
    grad_rate = -coef * (
        jnp.sum(
            back_lag * before + after * (own_lag + LANES * block_decay(1) * before), axis=1
        )
        + grow * (near_lag - near)
    )
    grad_coef = grad_coef.reshape(channels, states)
    grad_rate = grad_rate.reshape(channels, states)
    grad_skip = lags[:, 0]
    grad_taps = grad_taps[:, :taps].T
    spill = passed_along(head, "seq", -1)
    spill = spill[:, : num_seqs * edge].reshape(channels, num_seqs, edge)
    ahead = jnp.concatenate([d_shifted, jnp.transpose(spill, (1, 0, 2))], axis=2)
    d_keys = sum(
        tap_rows[:, i][None, :, None] * ahead[:, :, i : i + block_len] for i in range(taps)
    ).astype(BF)
    grad_query = product("btd,bct->dc", normed, d_queries)
    grad_key = product("btd,bct->dc", normed, d_keys)
    grad_value = product("btd,bct->dc", normed, d_values)
    d_first_part = product("bct,dc->btd", d_queries, query_weight)
    d_first_part = d_first_part + product("bct,dc->btd", d_keys, key_weight)
    d_first_part = d_first_part + product("bct,dc->btd", d_values, value_weight)
    d_first = lax.psum(d_first_part, "tp")
    first_value, first_pull = jax.vjp(layer_norm, source, first_gain)
    d_input_norm, grad_first = first_pull(d_first)
    grad_inputs = d_residual + d_input_norm
    grads = lax.psum(
        (
            grad_first,
            grad_query,
            grad_key,
            grad_value,
            grad_taps,
            grad_coef,
            grad_rate,
            grad_skip,
            grad_project,
            grad_second,
            grad_up,
            grad_down,
        ),
        "seq",
    )
    return (block_out, grad_inputs, *grads)


def solution(mesh):
    return jax.shard_map(
        local,
        mesh=mesh,
        in_specs=(
            P(None, "seq", None),
            P(),
            P(),
            P(None, "tp"),
            P(None, "tp"),
            P(None, "tp"),
            P(None, "tp"),
            P("tp", None),
            P("tp", None),
            P("tp"),
            P("tp", None),
            P(),
            P(None, "tp"),
            P("tp", None),
            P(None, "seq", None),
        ),
        out_specs=(
            P(None, "seq", None),
            P(None, "seq", None),
            P(),
            P(None, "tp"),
            P(None, "tp"),
            P(None, "tp"),
            P(None, "tp"),
            P("tp", None),
            P("tp", None),
            P("tp"),
            P("tp", None),
            P(),
            P(None, "tp"),
            P("tp", None),
        ),
        check_vma=False,
    )
```

time: 2290 us -> 1190 us (0.52)
  waiting for transfers between devices: 1400 us -> 848 us
  blocking collectives: 238 us -> 0 us
  matrix products: 252 us -> 77.5 us
  local copies, waits for them, and re-layouts: 198 us -> 40.2 us
  Pallas kernels: 0 us -> 102 us
  other arithmetic: 128 us -> 68.2 us
  starting transfers between devices: 50.5 us -> 26.6 us
    all_to_all x8 -> x0, waiting for transfers between devices: 696 us -> none  [the longest x3 454 us: to_bins(): lax.all_to_all(jnp.stack([turned_re, turned_im]), 'seq', split_axis=2, co...]
    all_to_all x2 -> x0, blocking collectives: 238 us -> none  [the longest x1 187 us: from_bins(): lax.all_to_all(jnp.stack([turned_re, turned_im]), 'seq', split_axis=3, co...]
    dot_general x48 -> x18, matrix products: 252 us -> 77.5 us  [product(): return jnp.einsum(form, left, right, preferred_element_type=F32)]
    ppermute x2 -> x8, waiting for transfers between devices: 2.55 us -> 106 us  [passed_along(): return lax.ppermute(x, axis, pairs)]
    pallas_call x0 -> x4, Pallas kernels: none -> 102 us  [call(): pl.pallas_call(kernel, grid=(channels // GROUP,), in_specs=ins, out_specs...]
    reduce_sum x3 -> x2, other arithmetic: 57.6 us -> 6.62 us  [the longest x1 4.56 us: local(): jnp.sum(state_coef[:, :, None] * jnp.exp(-state_rate[:, :, None] * lag[No...]
    another operation x5 -> x0, local copies, waits for them, and re-layouts: 50.1 us -> none  [the longest x2 25.5 us: from_bins(): jnp.stack([turned_re, turned_im])]
    all_to_all x8 -> x0, starting transfers between devices: 43.5 us -> none  [the longest x3 18.7 us: to_bins(): lax.all_to_all(signal.reshape(num_seqs, 1, block_len, channels), 'seq', s...]
  transfers between devices with their start and end apart: 15 -> 13, of which waited for: 14 -> 12; matrix products, arithmetic and copies ran while one was open for 11% -> 7% of each run, Pallas kernels for 0% -> 0%
where the time goes in v1:
time: 1190 us; the launch traced here: 1180 us
  waiting for transfers between devices  848 us (71%)
  Pallas kernels  102 us (9%)
  matrix products  77.5 us (7%)
  other arithmetic  68.2 us (6%)
  local copies, waits for them, and re-layouts  40.2 us (3%)
  starting transfers between devices  26.6 us (2%)
  between operations  15.1 us (1%)
    psum x2, waiting for transfers between devices, local(): lax.psum((grad_first, grad_query, grad_key, grad_value, grad_taps, grad_c...  292 us
    psum x1, waiting for transfers between devices, local(): lowered = lax.psum(product('btf,fd->btd', hidden, down_weight), 'tp')  194 us
    psum x1, waiting for transfers between devices, local(): mixer = lax.psum(product('bct,cd->btd', gated_out, project_weight), 'tp')  137 us
    psum x1, waiting for transfers between devices, local(): d_second = lax.psum(product('btf,df->btd', d_up, up_weight), 'tp')  120 us
    ppermute x8, waiting for transfers between devices, passed_along(): return lax.ppermute(x, axis, pairs)  106 us
    pallas_call x4, Pallas kernels, call(): pl.pallas_call(kernel, grid=(channels // GROUP,), in_specs=ins, out_specs...  102 us
    dot_general x18, matrix products, product(): return jnp.einsum(form, left, right, preferred_element_type=F32)  77.5 us
    unnamed x143, local copies, waits for them, and re-layouts  28.6 us
  transfers between devices with their start and end apart: 13, of which 12 were waited for; matrix products, arithmetic and copies ran while one was open for 7% of the time, Pallas kernels for 0%

profile of v1, /device:TPU:0, one launch (start us, length us, event | category | flops | bytes accessed | tf_op | source)
XLA Modules:
  0.0 1177.5 jit_solution(4956676574753722849)
XLA Ops:
  7.3 2.5 convert_reduce_fusion
  9.8 3.0 fusion.15
  13.4 1.5 convolution_bitcast_fusion.4.k_ref
  15.0 1.7 slice_bitcast_fusion
  16.6 2.0 copy.57
  19.5 4.9 collective-permute-start
  26.1 4.5 convolution_bitcast_fusion.3.v_ref
  30.6 4.6 multiply_reduce_fusion.3.kern_ref
  37.4 16.8 %shard_map.254 = (f32[16,192,128]{2,1,0:T(8,128)}, f32[96,16,128]{2,1,0:T(8,128)}, f32[96,16,128]{2,1,0:T(8,128)}) custom-call(f32[16,192,128]{2,1,0:T(8,128)} %copy-done.8, f32[16,192,128]{2,1,0:T(8,128)} %convolution_bitcast_fusion.3.v_ref, f32[192,128]{1,0:T(8,128)} %copy-done.23, f32[192,4]{1,0:T(8,128)} %bitcast.76, f32[96,128]{1,0:T(8,128)} %reshape.164.rate_ref, ...), custom_call_target="tpu_custom_call" | custom-call | tf_op jit(solution)/shard_map/pallas_call | solution.py:224
  54.2 3.5 collective-permute-start.1
  58.5 15.9 %collective-permute-done.1 = f32[96,16,128]{2,1,0:T(8,128)S(1)} collective-permute-done((f32[96,16,128]{2,1,0:T(8,128)}, f32[96,16,128]{2,1,0:T(8,128)S(1)}, u32[]{:S(2)}, u32[]{:S(2)}) %collective-permute-start.1) | collective-permute-done | bytes 786464 | tf_op jit(solution)/shard_map/ppermute | solution.py:269
  75.7 5.3 collective-permute-start.2
  81.0 15.5 %collective-permute-done.2 = f32[96,16,128]{2,1,0:T(8,128)S(1)} collective-permute-done((f32[96,16,128]{2,1,0:T(8,128)S(1)}, f32[96,16,128]{2,1,0:T(8,128)S(1)}, u32[]{:S(2)}, u32[]{:S(2)}) %collective-permute-start.2) | collective-permute-done | bytes 786464 | tf_op jit(solution)/shard_map/ppermute | solution.py:269
  96.5 2.2 multiply_add_fusion.5
  98.7 6.3 collective-permute-start.3
  106.4 4.5 convolution_bitcast_fusion.2.q_ref
  110.9 8.2 collective-permute-done.3
  119.1 2.2 multiply_add_fusion.4.hin_ref
  121.3 18.1 %shard_map.255 = (f32[16,192,128]{2,1,0:T(8,128)}, bf16[16,192,128]{2,1,0:T(8,128)(2,1)}) custom-call(f32[16,192,128]{2,1,0:T(8,128)} %get-tuple-element.30.y_ref, f32[96,16,128]{2,1,0:T(8,128)} %multiply_add_fusion.4.hin_ref, f32[96,128]{1,0:T(8,128)} %reshape.165.coef_ref, f32[96,128]{1,0:T(8,128)} %reshape.164.rate_ref, f32[16,192,128]{2,1,0:T(8,128)} %copy-done.8, ...), custom_call_target="tpu_custom_call" | custom-call | tf_op jit(solution)/shard_map/pallas_call | solution.py:224
  139.4 4.9 fusion.43
  144.9 136.9 %all-reduce.10.cloned.1.call-done = f32[16,128,768]{2,1,0:T(8,128)} async-done(((f32[16,128,768]{2,1,0:T(8,128)}), f32[16,128,768]{2,1,0:T(8,128)}) %all-reduce.10.cloned.1.call-update) | async-done | bytes 6291472 | tf_op jit(solution)/shard_map/psum | solution.py:349
  281.8 4.4 fusion.65
  287.1 2.9 fusion.40
  290.7 6.1 fusion.14
  296.8 1.7 copy-done.63
  298.5 4.5 fusion.38
  303.1 119.9 %all-reduce.12.cloned.1.call-done = f32[16,128,768]{2,1,0:T(8,128)} async-done(((f32[16,128,768]{2,1,0:T(8,128)}), f32[16,128,768]{2,1,0:T(8,128)}) %all-reduce.12.cloned.1.call-update) | async-done | bytes 6291472 | tf_op jit(solution)/shard_map/psum | solution.py:363
  423.0 6.4 multiply_reduce_fusion
  429.4 4.3 fusion.64
  434.9 1.5 copy-done.6
  436.4 2.3 convolution_bitcast_fusion.1.dg_ref
  438.7 51.8 %shard_map.256 = (bf16[16,192,128]{2,1,0:T(8,128)(2,1)}, f32[16,192,128]{2,1,0:T(8,128)}, f32[96,16,128]{2,1,0:T(8,128)}, f32[96,16,128]{2,1,0:T(8,128)}, f32[19...) custom-call(f32[16,192,128]{2,1,0:T(8,128)} %convolution_bitcast_fusion.1.dg_ref, ...), custom_call_target="tpu_custom_call" | custom-call | tf_op jit(solution)/shard_map/pallas_call | solution.py:224
  490.5 1.5 collective-permute-start.4
  492.0 19.8 %collective-permute-done.4 = f32[96,16,128]{2,1,0:T(8,128)S(1)} collective-permute-done((f32[96,16,128]{2,1,0:T(8,128)}, f32[96,16,128]{2,1,0:T(8,128)S(1)}, u32[]{:S(2)}, u32[]{:S(2)}) %collective-permute-start.4) | collective-permute-done | bytes 786464 | tf_op jit(solution)/shard_map/ppermute | solution.py:269
  515.3 17.8 %collective-permute-done.5 = f32[96,16,128]{2,1,0:T(8,128)S(1)} collective-permute-done((f32[96,16,128]{2,1,0:T(8,128)S(1)}, f32[96,16,128]{2,1,0:T(8,128)S(1)}, u32[]{:S(2)}, u32[]{:S(2)}) %collective-permute-start.5) | collective-permute-done | bytes 786464 | tf_op jit(solution)/shard_map/ppermute | solution.py:269
  534.5 1.6 collective-permute-start.6
  536.0 9.5 fusion.36
  545.6 26.0 %collective-permute-done.6 = f32[96,16,128]{2,1,0:T(8,128)S(1)} collective-permute-done((f32[96,16,128]{2,1,0:T(8,128)S(1)}, f32[96,16,128]{2,1,0:T(8,128)S(1)}, u32[]{:S(2)}, u32[]{:S(2)}) %collective-permute-start.6) | collective-permute-done | bytes 786464 | tf_op jit(solution)/shard_map/ppermute | solution.py:269
  571.6 2.1 add_reduce_fusion
  573.7 15.3 %shard_map.257 = (bf16[16,192,128]{2,1,0:T(8,128)(2,1)}, f32[16,192,128]{2,1,0:T(8,128)}, f32[192,128]{1,0:T(8,128)}, f32[192,128]{1,0:T(8,128)}) custom-call(f32[16,192,128]{2,1,0:T(8,128)} %get-tuple-element.35.dx_ref, f32[96,16,128]{2,1,0:T(8,128)} %get-tuple-element.112.gin_ref, f32[96,128]{1,0:T(8,128)} %reshape.165.coef_ref, ...), custom_call_target="tpu_custom_call" | custom-call | tf_op jit(solution)/shard_map/pallas_call | solution.py:224
  590.3 3.6 fusion.45
  594.0 2.1 collective-permute-done.7
  596.8 5.8 fusion.30
  603.7 3.9 add_add_fusion.3
  608.3 8.2 convolution_bitcast_fusion
  616.5 8.0 fusion.23
  625.3 1.6 convolution_bitcast_fusion.8
  626.9 2.3 convolution_bitcast_fusion.7
  631.3 4.0 convolution_bitcast_fusion.5
  635.4 193.8 %all-reduce.18.cloned.1.call-done = (f32[16,128,768]{2,1,0:T(8,128)}, f32[16,128,768]{2,1,0:T(8,128)}) async-done(((f32[16,128,768]{2,1,0:T(8,128)}, f32[16,128,768]{2,1,0:T(8,128)}), (f32[16,128,768]{2,1,0:T(8,128)}, f32[16,128,768]{2,1,0:T(8,128)})) %all-reduce.18.cloned.1.call-update) | async-done | bytes 12582928 | tf_op jit(solution)/shard_map/psum | solution.py:354
  829.1 4.6 fusion.16
  833.8 1.8 copy-done.7
  835.6 3.8 fusion.7
  839.8 4.0 convolution_bitcast_fusion.6
  843.9 15.7 %add_add_fusion.2 = (f32[16,128,768]{2,1,0:T(8,128)}, f32[16,128,768]{2,1,0:T(8,128)}) fusion(f32[16,128,768]{2,1,0:T(8,128)} %copy-done.6, bf16[16,128,768]{2,1,0:T(8,128)(2,1)} %param.29, f32[16,128]{1,0:T(8,128)S(1)} %negate_multiply_fusion, f32[16,128]{1,0:T(8,128)S(1)} %copy-done.45, f32[16,128]{1,0:T(8,128)S(1)} %copy-done.43, ...), kind=kLoop, calls=%fused_computation.25 | loop fusion | flops 23592960 | bytes 44092416 | tf_op jit(solution)/shard_map/add | solution.py:404
  859.5 52.7 %all-reduce.14.cloned.1.call-done = (f32[768]{0:T(1024)}, f32[4,192]{0,1:T(8,128)}, f32[192,64]{1,0:T(8,128)}, f32[192,64]{1,0:T(8,128)}, f32[192]{0:T(256)}, /*index=5*/f32[768]{0:T(1024)}) async-done(((f32[768]{0:T(1024)}, f32[4,192]{0,1:T(8,128)}, f32[192,64]{1,0:T(8,128)}, f32[192,64]{1,0:T(8,128)}, f32[192]{0:T(256)}, /*index=5*/f32[768]{0:T(1024)}), (f32[768]{0:T(1024)}, f32[4,192]{0,1:T(8,128)}, ...) | async-done | bytes 108304 | tf_op jit(solution)/shard_map/psum | solution.py:405
  912.3 1.6 copy.70
  913.9 1.6 copy.71
  915.5 1.6 copy.72
  917.1 239.0 %all-reduce.16.cloned.1.call-done = (f32[768,192]{0,1:T(8,128)}, f32[768,192]{0,1:T(8,128)}, f32[768,192]{0,1:T(8,128)}, f32[192,768]{1,0:T(8,128)}, f32[768,768]{1,0:T(8,128)}, /*index=5*/f32[768,768]{1,0:T(8,128)}) async-done(((f32[768,192]{0,1:T(8,128)}, f32[768,192]{0,1:T(8,128)}, f32[768,192]{0,1:T(8,128)}, f32[192,768]{1,0:T(8,128)}, f32[768,768]{1,0:T(8,128)}, /*index=5*/f32[768,768]{1,0:T(8,128)}), ...) | async-done | bytes 7077904 | tf_op jit(solution)/shard_map/psum | solution.py:405
  1157.5 2.0 copy.92
  1159.5 1.9 copy.93
  1161.4 1.9 copy.94
  1164.5 1.9 copy.96
  (181 shorter events, 30.6 us)
Async XLA Ops:
  7.2 279.9 %copy-start = (bf16[768,768]{1,0:T(8,128)(2,1)S(1)}, bf16[768,768]{1,0:T(8,128)(2,1)}, u32[]{:S(2)}) copy-start(bf16[768,768]{1,0:T(8,128)(2,1)} %param.27) | copy-start | bytes 3538948
  7.2 6.2 copy-start.54
  7.2 6.2 copy-start.32
  7.2 274.6 %all-reduce.10.cloned.1.call-start = ((), (), s32[]{:S(2)}) async-start(), calls=%async_computation | async-start | bytes 12582912 | tf_op jit(solution)/shard_map/psum | solution.py:349
  7.3 6.1 copy-start.3
  13.4 93.0 %copy-start.50 = (f32[16,128]{1,0:T(8,128)}, f32[16,128]{1,0:T(8,128)S(1)}, u32[]{:S(2)}) copy-start(f32[16,128]{1,0:T(8,128)S(1)} %fusion.56) | copy-start | bytes 24580
  13.4 10.9 copy-start.36
  13.4 12.6 %copy-start.34 = (bf16[768,192]{0,1:T(8,128)(2,1)S(1)}, bf16[768,192]{0,1:T(8,128)(2,1)}, u32[]{:S(2)}) copy-start(bf16[768,192]{0,1:T(8,128)(2,1)} %param.20) | copy-start | bytes 884740
  15.0 15.6 %copy-start.8 = (f32[16,192,128]{2,1,0:T(8,128)}, f32[16,192,128]{2,1,0:T(8,128)S(1)}, u32[]{:S(2)}) copy-start(f32[16,192,128]{2,1,0:T(8,128)S(1)} %convolution_bitcast_fusion.4.k_ref) | copy-start | bytes 4718596
  18.8 16.4 %copy-start.58 = (f32[4,192]{1,0:T(4,128)S(1)}, f32[4,192]{1,0:T(4,128)}, u32[]{:S(2)}) copy-start(f32[4,192]{1,0:T(4,128)} %param.21) | copy-start | bytes 9220
  19.5 17.2 %collective-permute-start = (f32[192,128]{1,0:T(8,128)}, f32[192,128]{1,0:T(8,128)S(1)}, u32[]{:S(2)}, u32[]{:S(2)}) collective-permute-start(f32[192,128]{1,0:T(8,128)} %pad.4), channel_id=1, source_target_pairs={{0,4},{4,8},{8,12},{12,16},{16,20},{20,24},{24,28},{1,5},{5,9},{9,... | collective-permute-start | bytes 294920 | tf_op jit(solution)/shard_map/ppermute | solution.py:269
  26.1 4.5 copy-start.41
  30.6 75.1 %copy-start.59 = (f32[192]{0:T(256)S(1)}, f32[192]{0:T(256)}, u32[]{:S(2)}) copy-start(f32[192]{0:T(256)} %param.24) | copy-start | bytes 2308
  30.6 75.8 %copy-start.31 = (bf16[768,192]{0,1:T(8,128)(2,1)S(1)}, bf16[768,192]{0,1:T(8,128)(2,1)}, u32[]{:S(2)}) copy-start(bf16[768,192]{0,1:T(8,128)(2,1)} %param.18) | copy-start | bytes 884740
  54.2 20.2 %collective-permute-start.1 = (f32[96,16,128]{2,1,0:T(8,128)}, f32[96,16,128]{2,1,0:T(8,128)S(1)}, u32[]{:S(2)}, u32[]{:S(2)}) collective-permute-start(f32[96,16,128]{2,1,0:T(8,128)} %get-tuple-element.31), channel_id=1, source_target_pairs={{0,4},{4,8},{8,12},{12,16},{16,20},{20,24},{24,28},{1,5},{5,9},{9,... | collective-permute-start | bytes 2359304 | tf_op jit(solution)/shard_map/ppermute | solution.py:269
  75.7 20.8 %collective-permute-start.2 = (f32[96,16,128]{2,1,0:T(8,128)S(1)}, f32[96,16,128]{2,1,0:T(8,128)S(1)}, u32[]{:S(2)}, u32[]{:S(2)}) collective-permute-start(f32[96,16,128]{2,1,0:T(8,128)S(1)} %multiply_add_fusion.7), channel_id=1, source_target_pairs={{0,8},{4,12},{8,16},{12,20},{16,24},{20,28},{1,9},{5,13},{9,17},{1... | collective-permute-start | bytes 2359304 | tf_op jit(solution)/shard_map/ppermute | solution.py:269
  98.7 20.4 %collective-permute-start.3 = (f32[96,16,128]{2,1,0:T(8,128)}, f32[96,16,128]{2,1,0:T(8,128)}, u32[]{:S(2)}, u32[]{:S(2)}) collective-permute-start(f32[96,16,128]{2,1,0:T(8,128)} %multiply_add_fusion.5), channel_id=1, source_target_pairs={{0,16},{4,20},{8,24},{12,28},{1,17},{5,21},{9,25},{13,29},{2,18},{... | collective-permute-start | bytes 2359304 | tf_op jit(solution)/shard_map/ppermute | solution.py:269
  110.9 28.5 %copy-start.24 = (bf16[192,768]{1,0:T(8,128)(2,1)S(1)}, bf16[192,768]{1,0:T(8,128)(2,1)}, u32[]{:S(2)}) copy-start(bf16[192,768]{1,0:T(8,128)(2,1)} %param.25) | copy-start | bytes 884740
  139.4 5.5 copy-start.60
  144.3 278.7 %all-reduce.12.cloned.1.call-start = ((), (), s32[]{:S(2)}) async-start(), calls=%async_computation.1 | async-start | bytes 12582912 | tf_op jit(solution)/shard_map/psum | solution.py:363
  144.9 288.8 %copy-start.42 = (f32[16,128]{1,0:T(8,128)}, f32[16,128]{1,0:T(8,128)S(1)}, u32[]{:S(2)}) copy-start(f32[16,128]{1,0:T(8,128)S(1)} %compare_convert_fusion) | copy-start | bytes 24580
  287.1 142.3 %copy-start.46 = (f32[16,128]{1,0:T(8,128)}, f32[16,128]{1,0:T(8,128)S(1)}, u32[]{:S(2)}) copy-start(f32[16,128]{1,0:T(8,128)S(1)} %fusion.57) | copy-start | bytes 24580
  290.7 6.1 copy-start.62
  303.0 526.1 %all-reduce.18.cloned.1.call-start = ((), (), s32[]{:S(2)}) async-start(), calls=%async_computation.4 | async-start | bytes 25165824 | tf_op jit(solution)/shard_map/psum | solution.py:354
  423.0 6.4 copy-start.12
  429.4 4.3 copy-start.14
  438.7 75.6 %copy-start.16 = (f32[4,192]{0,1:T(8,128)S(1)}, f32[4,192]{0,1:T(8,128)}, u32[]{:S(2)}) copy-start(f32[4,192]{0,1:T(8,128)} %copy.59) | copy-start | bytes 9220
  490.5 21.3 %collective-permute-start.4 = (f32[96,16,128]{2,1,0:T(8,128)}, f32[96,16,128]{2,1,0:T(8,128)S(1)}, u32[]{:S(2)}, u32[]{:S(2)}) collective-permute-start(f32[96,16,128]{2,1,0:T(8,128)} %get-tuple-element.36), channel_id=1, source_target_pairs={{4,0},{8,4},{12,8},{16,12},{20,16},{24,20},{28,24},{5,1},{9,5},{13... | collective-permute-start | bytes 2359304 | tf_op jit(solution)/shard_map/ppermute | solution.py:269
  513.1 20.0 %collective-permute-start.5 = (f32[96,16,128]{2,1,0:T(8,128)S(1)}, f32[96,16,128]{2,1,0:T(8,128)S(1)}, u32[]{:S(2)}, u32[]{:S(2)}) collective-permute-start(f32[96,16,128]{2,1,0:T(8,128)S(1)} %multiply_add_fusion.3), channel_id=1, source_target_pairs={{8,0},{12,4},{16,8},{20,12},{24,16},{28,20},{9,1},{13,5},{17,9},{2... | collective-permute-start | bytes 2359304 | tf_op jit(solution)/shard_map/ppermute | solution.py:269
  534.4 37.2 %copy-start.17 = (f32[96,16,128]{2,1,0:T(8,128)S(1)}, f32[96,16,128]{2,1,0:T(8,128)}, u32[]{:S(2)}) copy-start(f32[96,16,128]{2,1,0:T(8,128)} %multiply_add_fusion.4.hin_ref) | copy-start | bytes 2359300
  534.4 37.2 %copy-start.18 = (f32[96,16,128]{2,1,0:T(8,128)S(1)}, f32[96,16,128]{2,1,0:T(8,128)}, u32[]{:S(2)}) copy-start(f32[96,16,128]{2,1,0:T(8,128)} %get-tuple-element.36) | copy-start | bytes 2359300
  534.4 37.2 %copy-start.27 = (f32[96,16,128]{2,1,0:T(8,128)S(1)}, f32[96,16,128]{2,1,0:T(8,128)}, u32[]{:S(2)}) copy-start(f32[96,16,128]{2,1,0:T(8,128)} %get-tuple-element.43) | copy-start | bytes 2359300
  534.5 37.2 %copy-start.30 = (f32[96,16,128]{2,1,0:T(8,128)S(1)}, f32[96,16,128]{2,1,0:T(8,128)}, u32[]{:S(2)}) copy-start(f32[96,16,128]{2,1,0:T(8,128)} %get-tuple-element.42) | copy-start | bytes 2359300
  534.5 37.1 %collective-permute-start.6 = (f32[96,16,128]{2,1,0:T(8,128)S(1)}, f32[96,16,128]{2,1,0:T(8,128)S(1)}, u32[]{:S(2)}, u32[]{:S(2)}) collective-permute-start(f32[96,16,128]{2,1,0:T(8,128)S(1)} %multiply_add_fusion.1), channel_id=1, source_target_pairs={{16,0},{20,4},{24,8},{28,12},{17,1},{21,5},{25,9},{29,13},{18,2},{... | collective-permute-start | bytes 2359304 | tf_op jit(solution)/shard_map/ppermute | solution.py:269
  545.6 44.8 %copy-start.28 = (bf16[16,192,128]{2,1,0:T(8,128)(2,1)S(1)}, bf16[16,192,128]{2,1,0:T(8,128)(2,1)}, u32[]{:S(2)}) copy-start(bf16[16,192,128]{2,1,0:T(8,128)(2,1)} %get-tuple-element.34) | copy-start | bytes 2359300
  589.0 7.1 collective-permute-start.7
  590.3 12.3 %copy-start.33 = (bf16[768,192]{0,1:T(8,128)(2,1)S(1)}, bf16[768,192]{0,1:T(8,128)(2,1)}, u32[]{:S(2)}) copy-start(bf16[768,192]{0,1:T(8,128)(2,1)} %param.19) | copy-start | bytes 884740
  596.2 7.4 copy-start.26
  596.8 6.9 copy-start.11
  596.8 6.9 copy-start.35
  607.6 8.9 copy-start.43
  607.6 304.7 %all-reduce.14.cloned.1.call-start = ((), (), s32[]{:S(2)}) async-start(), calls=%async_computation.2 | async-start | bytes 608256 | tf_op jit(solution)/shard_map/psum | solution.py:405
  608.3 8.2 copy-start.15
  616.5 8.1 copy-start.39
  616.5 8.7 copy-start.10
  616.5 8.7 copy-start.19
  616.5 10.4 copy-start.4
  616.5 10.4 copy-start.29
  616.5 10.4 copy-start.51
  616.5 10.3 copy-start.55
  625.2 3.9 copy-start.20
  625.2 3.9 copy-start.25
  625.2 3.9 copy-start.37
  625.2 3.9 copy-start.38
  625.2 3.9 copy-start.52
  625.3 5.4 copy-start.40
  635.4 198.4 %copy-start.49 = (f32[16,128]{1,0:T(8,128)S(1)}, f32[16,128]{1,0:T(8,128)}, u32[]{:S(2)}) copy-start(f32[16,128]{1,0:T(8,128)} %copy-done.48) | copy-start | bytes 24580
  829.1 4.7 copy-start.5
  829.1 6.5 copy-start.7
  839.5 4.4 copy-start.45
  839.5 316.6 %all-reduce.16.cloned.1.call-start = ((), (), s32[]{:S(2)}) async-start(), calls=%async_computation.3 | async-start | bytes 14155776 | tf_op jit(solution)/shard_map/psum | solution.py:405
  1156.0 11.7 copy-start.22
  1156.0 13.1 %copy-start.21 = (f32[768,768]{1,0:T(8,128)S(1)}, f32[768,768]{1,0:T(8,128)}, u32[]{:S(2)}) copy-start(f32[768,768]{1,0:T(8,128)} %get-tuple-element.137) | copy-start | bytes 7077892
  1157.5 13.1 %copy-start.1 = (bf16[768,768]{1,0:T(8,128)(2,1)S(1)}, bf16[768,768]{1,0:T(8,128)(2,1)}, u32[]{:S(2)}) copy-start(bf16[768,768]{1,0:T(8,128)(2,1)} %param.27) | copy-start | bytes 3538948
  (13 other events, 27.5 us)
Sparse Core Ops, SparseCore 0:
  144.4 137.3 all-reduce.9
  303.2 119.7 all-reduce.11
  607.7 221.3 all-reduce.17
  839.6 72.6 all-reduce.13
  919.2 236.8 all-reduce.15

commit v2 on v1

v2 whole, which is shorter than its diff:
```python
import functools

import jax
import jax.numpy as jnp
from jax import lax
from jax.experimental import pallas as pl
from jax.experimental.pallas import tpu as pltpu
from jax.sharding import PartitionSpec as P

LANES = 128
GROUP = 32
BF = jnp.bfloat16
F32 = jnp.float32


def iota2(axis):
    return lax.broadcasted_iota(jnp.int32, (LANES, LANES), axis)


def strided(ref, c, rows):
    return ref[pl.ds(c, rows, stride=GROUP), :]


def lag_rows(block, edge, offset, lane):
    return pltpu.roll(jnp.where(lane < LANES - offset, block, edge), offset, 1)


def unpack_tail(tail, b, taps):
    return pltpu.roll(tail, (LANES - (taps - 1) * (b + 1)) % LANES, 1)


def spread_taps(taps_ref):
    rows, taps = taps_ref.shape
    return [jnp.broadcast_to(taps_ref[:, i : i + 1], (rows, LANES)) for i in range(taps)]


def shift_sum(block, tail, b, spread, lane):
    edge = unpack_tail(tail, b, len(spread))
    total = spread[0] * block
    for offset in range(1, len(spread)):
        total = total + spread[offset] * lag_rows(block, edge, offset, lane)
    return total


def fwd_local_kernel(
    k_ref, v_ref, tail_ref, taps_ref, rate_ref, kern_ref, y_ref, mixed_ref, h_ref, mix_ref, out_ref
):
    batch = k_ref.shape[0]
    lane = lax.broadcasted_iota(jnp.int32, (GROUP, LANES), 1)
    tail = tail_ref[...]
    spread = spread_taps(taps_ref)
    for b in range(batch):
        mixed = shift_sum(k_ref[b], tail, b, spread, lane) * v_ref[b]
        mix_ref[b * GROUP : (b + 1) * GROUP, :] = mixed
        mixed_ref[b] = mixed
    row = iota2(0)
    col = iota2(1)
    away = (LANES - 1 - row).astype(F32)
    low_half = lax.broadcasted_iota(jnp.int32, (batch, LANES), 1) < LANES // 2
    for p in range(GROUP // 2):
        xs = []
        for c in (2 * p, 2 * p + 1):
            x = strided(mix_ref, c, batch).astype(BF)
            xs.append(x)
            toep = jnp.broadcast_to(kern_ref[c : c + 1, :], (LANES, LANES))
            toep = pltpu.roll(toep, 0, 1, stride=1, stride_axis=0)
            toep = jnp.where(col >= row, toep, 0.0).astype(BF)
            out_ref[pl.ds(c, batch, stride=GROUP), :] = jnp.dot(
                x, toep, preferred_element_type=F32
            )
        decay = jnp.exp(-rate_ref[p : p + 1, :] * away)
        both = jnp.concatenate(xs, axis=0)
        grown = jnp.dot(both, decay.astype(BF), preferred_element_type=F32)
        h_ref[p] = jnp.where(low_half, grown[:batch], grown[batch:])
    for b in range(batch):
        y_ref[b] = out_ref[b * GROUP : (b + 1) * GROUP, :]


def fwd_post_kernel(
    y_ref, hin_ref, coef_ref, rate_ref, mixed_ref, q_ref, skip_ref, state_ref, gated_ref, out_ref
):
    batch = y_ref.shape[0]
    ahead = (iota2(0) + 1).astype(F32)
    low_half = lax.broadcasted_iota(jnp.int32, (batch, LANES), 1) < LANES // 2
    for p in range(GROUP // 2):
        grow = jnp.exp(-rate_ref[p : p + 1, :] * ahead).astype(BF)
        h = hin_ref[p] * coef_ref[p : p + 1, :]
        both = jnp.concatenate([jnp.where(low_half, h, 0.0), jnp.where(low_half, 0.0, h)], axis=0)
        cross = lax.dot_general(
            both.astype(BF), grow, (((1,), (1,)), ((), ())), preferred_element_type=F32
        )
        out_ref[pl.ds(2 * p, batch, stride=GROUP), :] = cross[:batch]
        out_ref[pl.ds(2 * p + 1, batch, stride=GROUP), :] = cross[batch:]
    skip = jnp.broadcast_to(skip_ref[...], (GROUP, LANES))
    for b in range(batch):
        state = y_ref[b] + out_ref[b * GROUP : (b + 1) * GROUP, :] + skip * mixed_ref[b]
        state_ref[b] = state
        gated_ref[b] = (q_ref[b] * state).astype(BF)


def bwd_local_kernel(
    dg_ref, q_ref, state_ref, skip_ref, rate_ref, kern_ref, dq_ref, d_ref, dx_ref, g_ref,
    d_scr, out_ref,
):
    batch = dg_ref.shape[0]
    for b in range(batch):
        dg = dg_ref[b]
        dq_ref[b] = (dg * state_ref[b]).astype(BF)
        d = dg * q_ref[b]
        d_ref[b] = d
        d_scr[b * GROUP : (b + 1) * GROUP, :] = d
    row = iota2(0)
    col = iota2(1)
    ahead = (row + 1).astype(F32)
    low_half = lax.broadcasted_iota(jnp.int32, (batch, LANES), 1) < LANES // 2
    for p in range(GROUP // 2):
        ds = []
        for c in (2 * p, 2 * p + 1):
            d = strided(d_scr, c, batch).astype(BF)
            ds.append(d)
            toep = jnp.broadcast_to(kern_ref[c : c + 1, :], (LANES, LANES))
            toep = pltpu.roll(toep, 1, 1, stride=1, stride_axis=0)
            toep = jnp.where(col <= row, toep, 0.0).astype(BF)
            out_ref[pl.ds(c, batch, stride=GROUP), :] = jnp.dot(
                d, toep, preferred_element_type=F32
            )
        grow = jnp.exp(-rate_ref[p : p + 1, :] * ahead)
        got = jnp.dot(jnp.concatenate(ds, axis=0), grow.astype(BF), preferred_element_type=F32)
        g_ref[p] = jnp.where(low_half, got[:batch], got[batch:])
    skip = jnp.broadcast_to(skip_ref[...], (GROUP, LANES))
    for b in range(batch):
        dx_ref[b] = out_ref[b * GROUP : (b + 1) * GROUP, :] + skip * d_ref[b]


def bwd_lags_kernel(
    d_ref, mixed_ref, rate_ref, h1_ref, g1_ref, lag_ref, s0_ref, s1_ref, x_scr, d_scr, turn_scr,
    grow_scr,
):
    batch = d_ref.shape[0]
    for b in range(batch):
        x_scr[b * GROUP : (b + 1) * GROUP, :] = mixed_ref[b]
        d_scr[b * GROUP : (b + 1) * GROUP, :] = d_ref[b]
    row = iota2(0)
    col = iota2(1)
    mirror = jnp.where(row + col == LANES - 1, 1.0, 0.0).astype(BF)
    ahead = (row + 1).astype(F32)
    away = (LANES - 1 - row).astype(F32)
    low_half = lax.broadcasted_iota(jnp.int32, (batch, LANES), 1) < LANES // 2
    low_row = lax.broadcasted_iota(jnp.int32, (1, LANES), 1) < LANES // 2
    lagrow = lax.broadcasted_iota(jnp.int32, (8, LANES), 0)
    for p in range(GROUP // 2):
        xs = jnp.concatenate([strided(x_scr, 2 * p + i, batch) for i in (0, 1)], axis=0).astype(BF)
        turn_scr[p] = jnp.dot(xs, mirror, preferred_element_type=F32).T.astype(BF)
        fall = jnp.exp(-rate_ref[p : p + 1, :] * away) * away
        got = jnp.dot(xs, fall.astype(BF), preferred_element_type=F32)
        h1_ref[p] = jnp.where(low_half, got[:batch], got[batch:])
    for p in range(GROUP // 2):
        ds = jnp.concatenate([strided(d_scr, 2 * p + i, batch) for i in (0, 1)], axis=0).astype(BF)
        for i in (0, 1):
            part = slice(i * batch, (i + 1) * batch)
            pairs = jnp.dot(turn_scr[p, :, part], ds[part], preferred_element_type=F32)
            pairs = jnp.where(col + row >= LANES - 1, pairs, 0.0)
            pairs = pltpu.roll(pairs, 1, 1, stride=1, stride_axis=0)
            lag_ref[2 * p + i : 2 * p + i + 1, :] = jnp.sum(pairs, axis=0, keepdims=True)
        grow = jnp.exp(-rate_ref[p : p + 1, :] * ahead)
        grow_scr[p, :, :LANES] = grow.astype(BF)
        grow1_low = (grow * ahead).astype(BF)
        grow_scr[p, :, LANES:] = grow1_low
        got = jnp.dot(ds, grow1_low, preferred_element_type=F32)
        g1_ref[p] = jnp.where(low_half, got[:batch], got[batch:])
    for p in range(GROUP // 2):
        lags = [lag_ref[2 * p + i : 2 * p + i + 1, :] for i in (0, 1)]
        high = [lag.astype(BF).astype(F32) for lag in lags]
        rest = jnp.where(lagrow == 2, lags[0] - high[0], lags[1] - high[1])
        stack = jnp.where(lagrow == 0, high[0], jnp.where(lagrow == 1, high[1], rest))
        stack = jnp.where(lagrow < 4, stack, 0.0).astype(BF)
        got = jnp.dot(stack, grow_scr[p], preferred_element_type=F32)
        even = got[0:1] + got[2:3]
        uneven = got[1:2] + got[3:4]
        s0_ref[p : p + 1, :] = jnp.where(low_row, even[:, :LANES], uneven[:, :LANES])
        s1_ref[p : p + 1, :] = jnp.where(low_row, even[:, LANES:], uneven[:, LANES:])


def bwd_post_kernel(
    dx_ref, gin_ref, coef_ref, rate_ref, k_ref, v_ref, tail_ref, taps_ref,
    dv_ref, ds_ref, head_ref, gtap_ref, out_ref,
):
    batch = k_ref.shape[0]
    taps = taps_ref.shape[1]
    away = (LANES - 1 - iota2(0)).astype(F32)
    low_half = lax.broadcasted_iota(jnp.int32, (batch, LANES), 1) < LANES // 2
    for p in range(GROUP // 2):
        decay = jnp.exp(-rate_ref[p : p + 1, :] * away).astype(BF)
        g = gin_ref[p] * coef_ref[p : p + 1, :]
        both = jnp.concatenate([jnp.where(low_half, g, 0.0), jnp.where(low_half, 0.0, g)], axis=0)
        cross = lax.dot_general(
            both.astype(BF), decay, (((1,), (1,)), ((), ())), preferred_element_type=F32
        )
        out_ref[pl.ds(2 * p, batch, stride=GROUP), :] = cross[:batch]
        out_ref[pl.ds(2 * p + 1, batch, stride=GROUP), :] = cross[batch:]
    lane = lax.broadcasted_iota(jnp.int32, (GROUP, LANES), 1)
    tail = tail_ref[...]
    spread = spread_taps(taps_ref)
    head = jnp.zeros((GROUP, LANES), F32)
    sums = [jnp.zeros((GROUP, LANES), F32) for _ in range(taps)]
    for b in range(batch):
        block = k_ref[b]
        edge = unpack_tail(tail, b, taps)
        lagged = [block] + [lag_rows(block, edge, i, lane) for i in range(1, taps)]
        shifted = spread[0] * block
        for i in range(1, taps):
            shifted = shifted + spread[i] * lagged[i]
        d_mixed = dx_ref[b] + out_ref[b * GROUP : (b + 1) * GROUP, :]
        dv_ref[b] = (d_mixed * shifted).astype(BF)
        d_shifted = d_mixed * v_ref[b]
        ds_ref[b] = d_shifted
        for i in range(taps):
            sums[i] = sums[i] + d_shifted * lagged[i]
        start = (taps - 1) * b
        head = jnp.where(
            (lane >= start) & (lane < start + taps - 1), pltpu.roll(d_shifted, start, 1), head
        )
    head_ref[...] = head
    packed = jnp.zeros((GROUP, LANES), F32)
    for i in range(taps):
        packed = jnp.where(lane == i, jnp.sum(sums[i], axis=1, keepdims=True), packed)
    gtap_ref[...] = packed


def first_kernel(
    mine_ref, x_ref, gain_ref, wq_ref, wk_ref, wv_ref, normed_ref, q_ref, k_ref, v_ref, tail_ref,
    *, edge
):
    step = pl.program_id(0)
    channels = wq_ref.shape[0]

    @pl.when(step == 0)
    def start():
        tail_ref[...] = jnp.zeros_like(tail_ref)

    seqs = x_ref.shape[0]
    rows = x_ref[...].reshape(seqs * LANES, x_ref.shape[2]).astype(F32)
    center = rows - jnp.mean(rows, axis=-1, keepdims=True)
    spread = jnp.mean(center * center, axis=-1, keepdims=True)
    normed = (center * lax.rsqrt(spread + 1e-05) * gain_ref[...]).astype(BF)
    normed_ref[...] = normed.reshape(normed_ref.shape)
    lane = lax.broadcasted_iota(jnp.int32, (channels, LANES), 1)
    for w_ref, out_ref in ((wq_ref, q_ref), (wk_ref, k_ref), (wv_ref, v_ref)):
        out = lax.dot_general(
            w_ref[...], normed, (((1,), (1,)), ((), ())), preferred_element_type=F32
        )
        for j in range(seqs):
            block = out[:, j * LANES : (j + 1) * LANES]
            out_ref[j] = block
            if out_ref is k_ref:
                at = edge * (step * seqs + j)
                block = pltpu.roll(block, at + edge, 1)
                tail_ref[...] = jnp.where((lane >= at) & (lane < at + edge), block, tail_ref[...])


def last_kernel(
    dq_ref, dv_ref, ds_ref, spill_ref, taps_ref, normed_ref, wq_ref, wk_ref, wv_ref, *rest
):
    piece_refs = rest[:-2]
    grad_ref, gain_ref = rest[-2:]
    step = pl.program_id(0)
    seqs, channels, _ = dq_ref.shape
    taps = taps_ref.shape[1]
    edge = taps - 1

    @pl.when(step == 0)
    def start():
        grad_ref[...] = jnp.zeros_like(grad_ref)
        gain_ref[...] = jnp.zeros_like(gain_ref)

    lane = lax.broadcasted_iota(jnp.int32, (channels, LANES), 1)
    spread = spread_taps(taps_ref)
    sides = []
    for j in range(seqs):
        block = ds_ref[j]
        at = edge * (step * seqs + j)
        after = pltpu.roll(spill_ref[...], (LANES - at) % LANES, 1)
        d_keys = spread[0] * block
        for i in range(1, taps):
            moved = pltpu.roll(jnp.where(lane >= i, block, after), LANES - i, 1)
            d_keys = d_keys + spread[i] * moved
        sides.append(jnp.concatenate([dq_ref[j], d_keys.astype(BF), dv_ref[j]], axis=0))
    both = jnp.concatenate(sides, axis=1)
    normed = normed_ref[...].reshape(seqs * LANES, normed_ref.shape[2])
    grad_ref[: 2 * channels, :] += jnp.dot(both[channels:], normed, preferred_element_type=F32)
    weights = jnp.concatenate([wq_ref[...], wk_ref[...], wv_ref[...]], axis=0)
    rows = lax.dot_general(both, weights, (((0,), (0,)), ((), ())), preferred_element_type=F32)
    gain_ref[...] += jnp.sum(rows * normed.astype(F32), axis=0, keepdims=True)
    for i, piece_ref in enumerate(piece_refs):

        @pl.when(step == i)
        def store(piece_ref=piece_ref):
            piece_ref[...] = rows.reshape(piece_ref.shape)


def first_call(mine, inputs, gain, weights, edge, chunks, parts):
    num_seqs, _, width = inputs.shape
    channels = weights[0].shape[0]
    seqs = num_seqs // (chunks * parts)
    whole = pl.BlockSpec((channels, width), lambda s, m: (0, 0))
    act = pl.BlockSpec((seqs, channels, LANES), lambda s, m: (s, 0, 0))
    rows = pl.BlockSpec((seqs, LANES, width), lambda s, m: (s, 0, 0))
    a = shape(num_seqs, channels, LANES)
    return pl.pallas_call(
        functools.partial(first_kernel, edge=edge),
        grid_spec=pltpu.PrefetchScalarGridSpec(
            num_scalar_prefetch=1,
            grid=(chunks * parts,),
            in_specs=[
                pl.BlockSpec(
                    (seqs, LANES, width),
                    lambda s, m: ((m[0] ^ (s % parts)) * chunks + s // parts, 0, 0),
                ),
                pl.BlockSpec((1, width), lambda s, m: (0, 0)),
                whole,
                whole,
                whole,
            ],
            out_specs=[
                rows,
                act,
                act,
                act,
                pl.BlockSpec((channels, LANES), lambda s, m: (0, 0)),
            ],
        ),
        out_shape=[
            shape(num_seqs, LANES, width, dtype=BF),
            a,
            a,
            a,
            shape(channels, LANES),
        ],
    )(mine[None], inputs, gain[None, :], *weights)


def last_call(dq, dv, ds, spill, tap_rows, normed, weights, pieces, more):
    num_seqs, channels, _ = dq.shape
    taps = tap_rows.shape[1]
    width = normed.shape[2]
    seqs = num_seqs // pieces
    act = pl.BlockSpec((seqs, channels, LANES), lambda s: (s, 0, 0))
    out = pl.pallas_call(
        last_kernel,
        grid=(pieces,),
        in_specs=[
            act,
            act,
            act,
            pl.BlockSpec((channels, LANES), lambda s: (0, 0)),
            pl.BlockSpec((channels, taps), lambda s: (0, 0)),
            pl.BlockSpec((seqs, LANES, width), lambda s: (s, 0, 0)),
        ]
        + [pl.BlockSpec((channels, width), lambda s: (0, 0))] * 3,
        out_specs=[pl.BlockSpec((seqs, LANES, width), lambda s: (0, 0, 0))] * pieces
        + [
            pl.BlockSpec((2 * channels + more, width), lambda s: (0, 0)),
            pl.BlockSpec((1, width), lambda s: (0, 0)),
        ],
        out_shape=[shape(seqs, LANES, width)] * pieces
        + [shape(2 * channels + more, width), shape(1, width)],
    )(dq, dv, ds, spill, tap_rows, normed, *weights)
    return out[:-2], out[-2], out[-1]


def place_kernel(blocks_ref, *refs):
    step = pl.program_id(0)
    for i, piece_ref in enumerate(refs[:-1]):

        @pl.when(step == i)
        def store(piece_ref=piece_ref):
            refs[-1][...] = piece_ref[...]


def place_call(blocks, pieces):
    count = len(pieces)
    piece = pieces[0].shape
    return pl.pallas_call(
        place_kernel,
        grid_spec=pltpu.PrefetchScalarGridSpec(
            num_scalar_prefetch=1,
            grid=(count,),
            in_specs=[pl.BlockSpec(piece, lambda s, b: (0, 0, 0))] * count,
            out_specs=pl.BlockSpec(piece, lambda s, b: (b[s], 0, 0)),
        ),
        out_shape=shape(count * piece[0], *piece[1:]),
    )(blocks, *pieces)


def specs(batch, taps):
    return dict(
        act=pl.BlockSpec((batch, GROUP, LANES), lambda i: (0, i, 0)),
        row=pl.BlockSpec((GROUP, LANES), lambda i: (i, 0)),
        pair=pl.BlockSpec((GROUP // 2, LANES), lambda i: (i, 0)),
        state=pl.BlockSpec((GROUP // 2, batch, LANES), lambda i: (i, 0, 0)),
        taps=pl.BlockSpec((GROUP, taps), lambda i: (i, 0)),
        one=pl.BlockSpec((GROUP, 1), lambda i: (i, 0)),
    )


def shape(*dims, dtype=F32):
    return jax.ShapeDtypeStruct(dims, dtype)


def call(kernel, ins, outs, out_shapes, scratch, channels, args):
    return pl.pallas_call(
        kernel,
        grid=(channels // GROUP,),
        in_specs=ins,
        out_specs=outs,
        out_shape=out_shapes,
        scratch_shapes=scratch,
    )(*args)


def conv_calls(batch, channels, taps):
    s = specs(batch, taps)
    act, row, pair, state, tap, one = (s[n] for n in ("act", "row", "pair", "state", "taps", "one"))
    a = shape(batch, channels, LANES)
    alow = shape(batch, channels, LANES, dtype=BF)
    st = shape(channels // 2, batch, LANES)
    rows = shape(channels, LANES)
    pairs = shape(channels // 2, LANES)
    scr = pltpu.VMEM((batch * GROUP, LANES), F32)

    def fwd_local(k, v, tail, tap_rows, rate, kern):
        return call(fwd_local_kernel, [act, act, row, tap, pair, row], [act, act, state],
                    [a, a, st], [scr, scr], channels, (k, v, tail, tap_rows, rate, kern))

    def fwd_post(y, hin, coef, rate, mixed, q, skip):
        return call(fwd_post_kernel, [act, state, pair, pair, act, act, one],
                    [act, act], [a, alow], [scr], channels, (y, hin, coef, rate, mixed, q, skip))

    def bwd_local(dg, q, so, skip, rate, kern):
        return call(bwd_local_kernel, [act, act, act, one, pair, row],
                    [act, act, act, state], [alow, a, a, st], [scr, scr], channels,
                    (dg, q, so, skip, rate, kern))

    def bwd_lags(d, mixed, rate, part, parts):
        steps = channels // GROUP // parts
        ins = [
            pl.BlockSpec((batch, GROUP, LANES), lambda i: (0, i + part * steps, 0)),
            pl.BlockSpec((batch, GROUP, LANES), lambda i: (0, i + part * steps, 0)),
            pl.BlockSpec((GROUP // 2, LANES), lambda i: (i + part * steps, 0)),
        ]
        count = channels // parts
        sp = shape(count // 2, batch, LANES)
        two = shape(count // 2, LANES)
        return call(bwd_lags_kernel, ins, [state, state, row, pair, pair],
                    [sp, sp, shape(count, LANES), two, two],
                    [scr, scr, pltpu.VMEM((GROUP // 2, LANES, 2 * batch), BF),
                     pltpu.VMEM((GROUP // 2, LANES, 2 * LANES), BF)], count, (d, mixed, rate))

    def bwd_post(dx, gin, coef, rate, k, v, tail, tap_rows):
        return call(bwd_post_kernel, [act, state, pair, pair, act, act, row, tap],
                    [act, act, row, row], [alow, a, rows, rows], [scr], channels,
                    (dx, gin, coef, rate, k, v, tail, tap_rows))

    return fwd_local, fwd_post, bwd_local, bwd_lags, bwd_post


def passed_along(x, axis, by):
    count = lax.axis_size(axis)
    pairs = [(i, i + by) for i in range(count) if 0 <= i + by < count]
    return lax.ppermute(x, axis, pairs)


def swapped(x, axis, bit):
    return lax.ppermute(x, axis, [(i, i ^ bit) for i in range(lax.axis_size(axis))])


def summed(x, axes):
    for axis in axes:
        bit = 1
        while bit < lax.axis_size(axis):
            x = x + swapped(x, axis, bit)
            bit *= 2
    return x


def carried(own, decay, sign, fill=lambda got, step: got):
    count = lax.axis_size("seq")
    odd = lax.axis_index("seq") % 2 == 1
    rows = own.shape[0] // 2
    fall = jnp.where(odd, decay(1)[rows:], decay(1)[:rows])
    keep = jnp.where(odd, own[rows:], own[:rows])
    got = fill(swapped(jnp.where(odd, own[:rows], own[rows:]), "seq", 1), 0)
    leads = odd if sign < 0 else jnp.logical_not(odd)
    lead = jnp.where(leads, keep, got)
    both = fall * lead + jnp.where(leads, got, keep)
    into = fill(passed_along(both, "seq", 2 * sign), 1)
    reach = 1
    while reach < count // 2 - 1:
        far = jnp.where(odd, decay(2 * reach)[rows:], decay(2 * reach)[:rows])
        whole = both + fall * fall * into
        got = passed_along(whole, "seq", 2 * sign * (reach + 1))
        into = into + far * (fill(got, 2) if reach == 1 else got)
        reach = 2 * reach + 1
    then = fall * into + lead
    stay = jnp.where(leads, into, then)
    back = fill(swapped(jnp.where(leads, then, into), "seq", 1), 3)
    return jnp.concatenate([jnp.where(odd, back, stay), jnp.where(odd, stay, back)], axis=0)


class Link:
    def __init__(self):
        self.waits = ()

    def swap(self, x, *more):
        x, *_ = lax.optimization_barrier((x, *self.waits, *more))
        got = swapped(x, "tp", 2)
        self.waits = (got,)
        return got


def far_total(part):
    own, side = part if isinstance(part, (tuple, list)) else jnp.split(part, 2, axis=0)
    return own + swapped(side, "tp", 1)


def total_steps(x, digits):
    index = lax.axis_index("seq")
    for stride, radix in digits:
        digit = (index // stride) % radix
        rows = x.shape[0] // radix
        got = yield [
            (lax.dynamic_slice_in_dim(x, (digit ^ k) * rows, rows, 0), k * stride)
            for k in range(1, radix)
        ]
        x = sum(got, lax.dynamic_slice_in_dim(x, digit * rows, rows, 0))
    for stride, radix in reversed(digits):
        digit = (index // stride) % radix
        rows = x.shape[0]
        got = yield [(x, k * stride) for k in range(1, radix)]
        whole = jnp.zeros((radix * rows,) + x.shape[1:], x.dtype)
        for k, part in enumerate([x, *got]):
            whole = lax.dynamic_update_slice_in_dim(whole, part, (digit ^ k) * rows, 0)
        x = whole
    return x


class Total:
    def __init__(self, x):
        count = lax.axis_size("seq")
        digits = [(1, 2)]
        while digits[-1][0] * digits[-1][1] < count:
            stride = digits[-1][0] * digits[-1][1]
            digits.append((stride, min(4, count // stride)))
        self.rounds = 2 * len(digits)
        self.steps = total_steps(x, digits)
        self.sends = next(self.steps)

    def run(self, rounds):
        got = ()
        for _ in range(rounds * self.rounds // 4):
            got = tuple(swapped(x, "seq", by) for x, by in self.sends)
            try:
                self.sends = self.steps.send(got)
            except StopIteration as end:
                self.done = end.value
        return got


def centered(rows):
    center = rows - jnp.mean(rows, axis=-1, keepdims=True)
    spread = jnp.mean(center * center, axis=-1, keepdims=True)
    inverse = lax.rsqrt(spread + 1e-05)
    return center * inverse, inverse


def norm_back(unit, inverse, grad, gain):
    scaled = grad * gain
    mean_one = jnp.mean(scaled, axis=-1, keepdims=True)
    mean_two = jnp.mean(scaled * unit, axis=-1, keepdims=True)
    return inverse * (scaled - mean_one - unit * mean_two)


def product(form, left, right):
    return jnp.einsum(form, left, right, preferred_element_type=F32)


def local(
    inputs,
    lengths,
    first_gain,
    query_weight,
    key_weight,
    value_weight,
    shift_taps,
    state_coef,
    state_rate,
    skip_gain,
    project_weight,
    second_gain,
    up_weight,
    down_weight,
    cotangent,
):
    place = lax.axis_index("seq")
    mine = lax.axis_index("tp")
    parts = lax.axis_size("tp")
    assert parts == 4
    num_seqs, block_len, width_all = inputs.shape
    taps = shift_taps.shape[0]
    channels, states = state_coef.shape
    assert block_len == LANES and 2 * states == LANES and channels % GROUP == 0
    edge = taps - 1
    chunks = 2
    size = num_seqs // chunks
    piece = size // parts
    half = 2 * piece
    group_seqs = num_seqs // parts

    def starts():
        for u in range(chunks):
            for r in range(parts):
                yield (mine ^ r) * group_seqs + u * piece

    def groups(x):
        return jnp.concatenate(
            [lax.dynamic_slice_in_dim(x, at, piece, 0) for at in starts()], axis=0
        )

    def placed(pieces):
        blocks = [(mine ^ r) * chunks + u for u in range(chunks) for r in range(parts)]
        return place_call(jnp.stack(blocks), pieces)

    own_inputs = [
        lax.dynamic_slice_in_dim(inputs, mine * group_seqs + u * piece, piece, 0).astype(F32)
        for u in range(chunks)
    ]

    def nears(x, u):
        return x[u * size : u * size + half]

    def fars(x, u):
        return x[u * size + half : (u + 1) * size]

    def owns(x, u):
        return x[u * size : u * size + piece]

    link = Link()
    lengths = groups(lengths)
    positions = place * block_len + jnp.arange(block_len)
    valid = (positions[None, :] < lengths[:, None])[:, :, None]
    d_mlp = jnp.where(valid, groups(cotangent), 0)
    fwd_local, fwd_post, bwd_local, bwd_lags, bwd_post = conv_calls(num_seqs, channels, taps)
    rate = state_rate.reshape(channels // 2, LANES)
    coef = state_coef.reshape(channels // 2, LANES)
    tap_rows = shift_taps.T
    skip = skip_gain[:, None]
    lag = jnp.arange(LANES).astype(F32)
    kern = jnp.sum(
        state_coef[:, :, None] * jnp.exp(-state_rate[:, :, None] * lag[None, None, :]), axis=1
    )

    def block_decay(count):
        return jnp.exp(-rate * (LANES * count))[:, None, :]

    turned = (query_weight.T, key_weight.T, value_weight.T)
    normed, queries, keys, values, tail = first_call(
        mine, inputs, first_gain, turned, edge, chunks, parts
    )
    tail = passed_along(tail, "seq", 1)
    conv, mixed, own = fwd_local(keys, values, tail, tap_rows, rate, kern)
    def mask_fill(got, step):
        nonlocal d_mlp
        if step == 1:
            got, d_mlp = lax.optimization_barrier((got, d_mlp))
        return got

    before = carried(own, block_decay, 1, mask_fill)
    state_out, gated_out = fwd_post(conv, before, coef, rate, mixed, queries, skip)

    sums = []
    for u in range(chunks):
        far = link.swap(far_total(product("bct,cd->btd", fars(gated_out, u), project_weight)))
        near = far_total(product("bct,cd->btd", nears(gated_out, u), project_weight))
        sums.append((near, far))
    def feed(first, d_out):
        up_act = product("btd,df->btf", first, up_weight)
        hidden, pull = jax.vjp(jax.nn.gelu, up_act)
        hidden = hidden.astype(BF)
        d_hidden = product("btd,fd->btf", d_out, down_weight)
        d_up = pull(d_hidden)[0].astype(BF)
        return hidden, d_up, product("btf,df->btd", d_up, up_weight)

    def scaled(*two):
        return (jnp.concatenate(two, axis=0) * second_gain).astype(BF)

    residuals = []
    units = []
    seconds = []
    fed = []
    for u in range(chunks):
        near, far = sums[u]
        residual = own_inputs[u] + (near + far)
        unit = centered(residual)
        residuals.append(residual)
        units.append(unit)
        side = swapped(unit[0], "tp", 1)
        far = link.swap(unit[0])
        near_fed = feed(scaled(unit[0], side), nears(d_mlp, u))
        if u + 1 < chunks:
            link.waits += tuple(near_fed)
        else:
            far, near_fed, fed = lax.optimization_barrier((far, near_fed, fed))
        second_far = scaled(far, swapped(far, "tp", 1))
        far_fed = feed(second_far, fars(d_mlp, u))
        seconds += [scaled(unit[0], side), second_far]
        fed += [near_fed, far_fed]
    sums = []
    for u in range(chunks):
        far = link.swap(far_total(fed[2 * u + 1][2]))
        sums.append((far_total(fed[2 * u][2]), far))
    hiddens = [x[0] for x in fed]
    d_ups = [x[1] for x in fed]
    hidden = jnp.concatenate(hiddens, axis=0)
    d_up = jnp.concatenate(d_ups, axis=0)
    second = jnp.concatenate(seconds, axis=0)
    grad_down = product("btf,btd->fd", hidden, d_mlp)
    grad_up = product("btd,btf->df", second, d_up)
    link.waits += (grad_up, grad_down)
    early = lax.psum_scatter(
        jnp.concatenate([grad_up, grad_down], axis=0), "seq", scatter_dimension=0, tiled=True
    )
    grad_second = 0.0
    d_norms = []
    groups_back = []
    for u in range(chunks):
        d_second = sums[u][0] + sums[u][1]
        unit, inverse = units[u]
        d_norm = norm_back(unit, inverse, d_second, second_gain)
        grad_second = grad_second + jnp.sum(d_second * unit, axis=(0, 1))
        side = swapped(d_norm, "tp", 1)
        far = link.swap(d_norm)
        groups_back += [d_norm, side, far, swapped(far, "tp", 1)]
        d_norms.append(d_norm)
    lowered = [
        (
            product("btf,fd->btd", hiddens[2 * u], down_weight),
            product("btf,fd->btd", hiddens[2 * u + 1], down_weight),
        )
        for u in range(chunks)
    ]
    groups_back, lowered = lax.optimization_barrier((groups_back, lowered))
    d_resid_low = (jnp.concatenate(groups_back, axis=0) + d_mlp.astype(F32)).astype(BF)
    d_gated = product("btd,cd->bct", d_resid_low, project_weight)
    d_queries, d_state, d_part, back = bwd_local(
        d_gated, queries, state_out, skip, rate, kern[:, ::-1]
    )
    outs = []
    out_groups = []

    def lower(u):
        far = link.swap(far_total(lowered[u][1]))
        outs.append(far_total(lowered[u][0]) + far)
        return far

    def give_out(u):
        out = jnp.where(owns(valid, u), residuals[u] + outs[u], 0.0)
        side = swapped(out, "tp", 1)
        far = link.swap(out)
        out_groups.extend([out, side, far, swapped(far, "tp", 1)])
        return far

    grad_project = product("bct,btd->cd", gated_out, d_resid_low)
    grad_query = product("bct,btd->cd", d_queries, normed)
    lagged = bwd_lags(d_state, mixed, rate, 0, 1)

    def back_fill(got, step):
        nonlocal lagged, grad_project, grad_query, early
        if step == 0:
            got, _ = lax.optimization_barrier((got, lower(0)))
        elif step == 1:
            got, grad_project, grad_query, early = lax.optimization_barrier(
                (got, grad_project, grad_query, early)
            )
        elif step == 2:
            got, lagged, _ = lax.optimization_barrier((got, lagged, lower(1)))
        else:
            got, _ = lax.optimization_barrier((got, give_out(0)))
        return got

    after = carried(back, block_decay, -1, back_fill)
    early = lax.all_gather(early, "seq", axis=0, tiled=True)
    give_out(1)
    block_out = placed(out_groups)
    others = Total(jnp.concatenate([grad_project, grad_query], axis=0))
    first_got = others.run(1)
    d_values, d_shifted, head, grad_taps = bwd_post(
        d_part, after, coef, rate, keys, values, tail, tap_rows
    )
    spill = passed_along(head, "seq", -1)
    spill, block_out, _ = lax.optimization_barrier((spill, block_out, first_got))
    link.waits += others.run(1)
    pieces, main, grad_first = last_call(
        d_queries, d_values, d_shifted, spill, tap_rows, normed, turned, chunks * parts, 64
    )
    own_lag, back_lag, lags, near, near_lag = lagged
    grow = jnp.exp(rate)
    grad_coef = jnp.sum(before * back, axis=1) + grow * near
    grad_rate = -coef * (
        jnp.sum(
            back_lag * before + after * (own_lag + LANES * block_decay(1) * before), axis=1
        )
        + grow * (near_lag - near)
    )
    pairs = channels // 2
    edges = jnp.concatenate([grad_taps[:, :taps].T.reshape(-1), lags[:, 0]])
    edges = jnp.pad(edges, (0, -edges.shape[0] % width_all)).reshape(-1, width_all)
    gains = summed(jnp.concatenate([grad_first / first_gain, grad_second[None, :]]), ("tp",))
    tables = [grad_coef.reshape(-1, width_all), grad_rate.reshape(-1, width_all), gains, edges]
    rows = sum(x.shape[0] for x in tables)
    tables.append(jnp.zeros((64 - rows, width_all), F32))
    main = lax.dynamic_update_slice(main, jnp.concatenate(tables, axis=0), (2 * channels, 0))
    mains = Total(main)
    rows = grad_up.shape[0]
    grad_up, grad_down = early[:rows], early[rows:]
    link.waits += (gains,)
    sums = []
    for u in range(chunks):
        at = parts * u
        far = link.swap(far_total((pieces[at + 2], pieces[at + 3])))
        link.waits += mains.run(1) + others.run(1)
        sums.append((far_total((pieces[at], pieces[at + 1])), far))
    out_groups = []
    for u in range(chunks):
        d_first = sums[u][0] + sums[u][1]
        unit, inverse = centered(own_inputs[u])
        d_rows = d_norms[u] + owns(d_mlp, u).astype(F32)
        d_rows = d_rows + norm_back(unit, inverse, d_first, first_gain)
        side = swapped(d_rows, "tp", 1)
        far = link.swap(d_rows)
        link.waits += mains.run(1) + (() if u else (grad_up, grad_down))
        out_groups += [d_rows, side, far, swapped(far, "tp", 1)]
    grad_inputs = placed(out_groups)
    main = mains.done
    at = 2 * channels
    grad_key, grad_value = main[:channels].T, main[channels:at].T
    rows = pairs * LANES // width_all
    grad_coef = main[at : at + rows].reshape(channels, states)
    grad_rate = main[at + rows : at + 2 * rows].reshape(channels, states)
    at += 2 * rows
    gains = main[at : at + 2]
    edges = main[at + 2 :].reshape(-1)
    grad_taps = edges[: taps * channels].reshape(taps, channels)
    grad_skip = edges[taps * channels : (taps + 1) * channels]
    grad_project, grad_query = others.done[:channels], others.done[channels:].T
    return (
        block_out,
        grad_inputs,
        gains[0],
        grad_query,
        grad_key,
        grad_value,
        grad_taps,
        grad_coef,
        grad_rate,
        grad_skip,
        grad_project,
        gains[1],
        grad_up,
        grad_down,
    )


def solution(mesh):
    return jax.shard_map(
        local,
        mesh=mesh,
        in_specs=(
            P(None, "seq", None),
            P(),
            P(),
            P(None, "tp"),
            P(None, "tp"),
            P(None, "tp"),
            P(None, "tp"),
            P("tp", None),
            P("tp", None),
            P("tp"),
            P("tp", None),
            P(),
            P(None, "tp"),
            P("tp", None),
            P(None, "seq", None),
        ),
        out_specs=(
            P(None, "seq", None),
            P(None, "seq", None),
            P(),
            P(None, "tp"),
            P(None, "tp"),
            P(None, "tp"),
            P(None, "tp"),
            P("tp", None),
            P("tp", None),
            P("tp"),
            P("tp", None),
            P(),
            P(None, "tp"),
            P("tp", None),
        ),
        check_vma=False,
    )
```

time: 1190 us -> 602 us (0.51)
  waiting for transfers between devices: 848 us -> 238 us
  starting transfers between devices: 26.6 us -> 94.7 us
  matrix products: 77.5 us -> 37 us
  local copies, waits for them, and re-layouts: 40.2 us -> 59.8 us
    psum x5 -> x0, waiting for transfers between devices: 742 us -> none  [the longest x2 292 us: local(): lax.psum((grad_first, grad_query, grad_key, grad_value, grad_taps, grad_c...]
    ppermute x0 -> x70, waiting for transfers between devices: none -> 222 us  [swapped(): lax.ppermute(x, axis, [(i, i ^ bit) for i in range(lax.axis_size(axis))])]
    ppermute x8 -> x6, waiting for transfers between devices: 106 us -> 15.3 us  [passed_along(): return lax.ppermute(x, axis, pairs)]
    ppermute x0 -> x70, starting transfers between devices: none -> 76.4 us  [swapped(): lax.ppermute(x, axis, [(i, i ^ bit) for i in range(lax.axis_size(axis))])]
    pallas_call x4 -> x5, Pallas kernels: 102 us -> 51.2 us  [call(): pl.pallas_call(kernel, grid=(channels // GROUP,), in_specs=ins, out_specs...]
    dot_general x18 -> x25, matrix products: 77.5 us -> 37 us  [product(): return jnp.einsum(form, left, right, preferred_element_type=F32)]
    pallas_call x0 -> x4, Pallas kernels: none -> 39.9 us  [the longest x2 15.4 us: place_call(): pl.pallas_call(place_kernel, grid_spec=pltpu.PrefetchScalarGridSpec(num_s...]
    reduce_sum x8, other arithmetic: 29.8 us -> 9.53 us  [the longest x2 3.42 us: local(): grad_second = grad_second + jnp.sum(d_second * unit, axis=(0, 1))]
  transfers between devices with their start and end apart: 13 -> 78, of which waited for: 12 -> 29; matrix products, arithmetic and copies ran while one was open for 7% -> 21% of each run, Pallas kernels for 0% -> 9%
where the time goes in v2:
time: 602 us; the launch traced here: 594 us
  waiting for transfers between devices  238 us (40%)
  starting transfers between devices  94.7 us (16%)
  Pallas kernels  91.1 us (15%)
  local copies, waits for them, and re-layouts  59.8 us (10%)
  other arithmetic  57.5 us (10%)
  matrix products  37 us (6%)
  between operations  16.2 us (3%)
    ppermute x70, waiting for transfers between devices, swapped(): lax.ppermute(x, axis, [(i, i ^ bit) for i in range(lax.axis_size(axis))])  222 us
    ppermute x70, starting transfers between devices, swapped(): lax.ppermute(x, axis, [(i, i ^ bit) for i in range(lax.axis_size(axis))])  76.4 us
    pallas_call x5, Pallas kernels, call(): pl.pallas_call(kernel, grid=(channels // GROUP,), in_specs=ins, out_specs...  51.2 us
    dot_general x25, matrix products, product(): return jnp.einsum(form, left, right, preferred_element_type=F32)  37 us
    unnamed x214, local copies, waits for them, and re-layouts  25.8 us
    ppermute x6, starting transfers between devices, passed_along(): return lax.ppermute(x, axis, pairs)  17.9 us
    pallas_call x2, Pallas kernels, place_call(): pl.pallas_call(place_kernel, grid_spec=pltpu.PrefetchScalarGridSpec(num_s...  15.4 us
    ppermute x6, waiting for transfers between devices, passed_along(): return lax.ppermute(x, axis, pairs)  15.3 us
  transfers between devices with their start and end apart: 78, of which 29 were waited for; matrix products, arithmetic and copies ran while one was open for 21% of the time, Pallas kernels for 9%

profile of v2, /device:TPU:0, one launch (start us, length us, event | category | flops | bytes accessed | tf_op | source)
XLA Modules:
  0.0 594.1 jit_solution(2985451019286157102)
XLA Ops:
  8.6 9.9 %shard_map.254 = (bf16[16,128,768]{2,1,0:T(8,128)(2,1)}, f32[16,192,128]{2,1,0:T(8,128)}, f32[16,192,128]{2,1,0:T(8,128)}, f32[16,192,128]{2,1,0:T(8,128)}, f32[192,128]{1,0:T(8,128)}) custom-call(s32[1]{0:T(128)} %bitcast.mine_ref, bf16[16,128,768]{2,1,0:T(8,128)(2,1)} %x_ref.1, f32[1,768]{1,0:T(1,128)} %broadcast_in_dim.43.gain_ref, ...), custom_call_target="tpu_custom_call" | custom-call | tf_op jit(solution)/shard_map/pallas_call | solution.py:309
  18.5 4.9 collective-permute-start
  32.6 4.6 multiply_reduce_fusion.kern_ref
  39.6 12.9 %shard_map.255 = (f32[16,192,128]{2,1,0:T(8,128)}, f32[16,192,128]{2,1,0:T(8,128)}, f32[96,16,128]{2,1,0:T(8,128)}) custom-call(f32[16,192,128]{2,1,0:T(8,128)} %get-tuple-element.100.k_ref, f32[16,192,128]{2,1,0:T(8,128)} %get-tuple-element.101.v_ref, f32[192,128]{1,0:T(8,128)} %copy-done.68, f32[192,4]{1,0:T(8,128)} %bitcast.109, f32[96,128]{1,0:T(8,128)} %copy-done.23, ...), custom_call_target="tpu_custom_call" | custom-call | tf_op jit(solution)/shard_map/pallas_call | solution.py:411
  58.8 5.5 collective-permute-done.1
  64.4 3.5 collective-permute-start.2
  69.7 3.3 broadcast_select_fusion
  73.0 2.1 collective-permute-done.2
  75.2 5.4 collective-permute-start.3
  80.6 6.2 %collective-permute-done.3 = f32[48,16,128]{2,1,0:T(8,128)S(1)} collective-permute-done((f32[48,16,128]{2,1,0:T(8,128)S(1)}, f32[48,16,128]{2,1,0:T(8,128)S(1)}, u32[]{:S(2)}, u32[]{:S(2)}) %collective-permute-start.3) | collective-permute-done | bytes 393248 | tf_op jit(solution)/shard_map/ppermute | solution.py:470
  90.7 5.1 collective-permute-done.4
  97.1 7.4 %shard_map.256 = (f32[16,192,128]{2,1,0:T(8,128)}, bf16[16,192,128]{2,1,0:T(8,128)(2,1)}) custom-call(f32[16,192,128]{2,1,0:T(8,128)} %get-tuple-element.103.y_ref, f32[96,16,128]{2,1,0:T(8,128)} %pad_maximum_fusion.1.hin_ref, f32[96,128]{1,0:T(8,128)} %reshape.217.coef_ref, f32[96,128]{1,0:T(8,128)} %copy-done.23, ...), custom_call_target="tpu_custom_call" | custom-call | tf_op jit(solution)/shard_map/pallas_call | solution.py:411
  111.7 16.4 %collective-permute-done.7 = f32[2,128,768]{2,1,0:T(8,128)S(1)} collective-permute-done((f32[2,128,768]{2,1,0:T(8,128)S(1)}, f32[2,128,768]{2,1,0:T(8,128)S(1)}, u32[]{:S(2)}, u32[]{:S(2)}) %collective-permute-start.7) | collective-permute-done | bytes 786464 | tf_op jit(solution)/shard_map/ppermute | solution.py:474
  130.7 16.1 %collective-permute-done.10 = f32[2,128,768]{2,1,0:T(8,128)S(1)} collective-permute-done((f32[2,128,768]{2,1,0:T(8,128)S(1)}, f32[2,128,768]{2,1,0:T(8,128)S(1)}, u32[]{:S(2)}, u32[]{:S(2)}) %collective-permute-start.10) | collective-permute-done | bytes 786464 | tf_op jit(solution)/shard_map/ppermute | solution.py:474
  146.9 2.3 fusion.107
  151.9 17.8 %collective-permute-done.11 = f32[2,128,768]{2,1,0:T(8,128)S(1)} collective-permute-done((f32[2,128,768]{2,1,0:T(8,128)S(1)}, f32[2,128,768]{2,1,0:T(8,128)S(1)}, u32[]{:S(2)}, u32[]{:S(2)}) %collective-permute-start.11) | collective-permute-done | bytes 786464 | tf_op jit(solution)/shard_map/ppermute | solution.py:474
  169.6 2.3 collective-permute-done.15
  180.8 2.0 fusion.87
  186.8 15.6 %collective-permute-done.13 = f32[2,128,768]{2,1,0:T(8,128)S(1)} collective-permute-done((f32[2,128,768]{2,1,0:T(8,128)S(1)}, f32[2,128,768]{2,1,0:T(8,128)S(1)}, u32[]{:S(2)}, u32[]{:S(2)}) %collective-permute-start.13) | collective-permute-done | bytes 786464 | tf_op jit(solution)/shard_map/ppermute | solution.py:474
  210.1 2.8 fusion.26
  213.0 2.8 fusion.23
  216.9 11.7 %collective-permute-done.18 = f32[2,128,768]{2,1,0:T(8,128)} collective-permute-done((f32[2,128,768]{2,1,0:T(8,128)S(1)}, f32[2,128,768]{2,1,0:T(8,128)}, u32[]{:S(2)}, u32[]{:S(2)}) %collective-permute-start.18) | collective-permute-done | bytes 786464 | tf_op jit(solution)/shard_map/ppermute | solution.py:474
  230.0 2.5 pad_maximum_fusion
  234.2 13.5 %collective-permute-done.22 = f32[2,128,768]{2,1,0:T(8,128)S(1)} collective-permute-done((f32[2,128,768]{2,1,0:T(8,128)}, f32[2,128,768]{2,1,0:T(8,128)S(1)}, u32[]{:S(2)}, u32[]{:S(2)}) %collective-permute-start.22) | collective-permute-done | bytes 786464 | tf_op jit(solution)/shard_map/ppermute | solution.py:474
  249.4 1.8 multiply_reduce_fusion.3
  253.1 16.6 %collective-permute-done.23 = f32[2,128,768]{2,1,0:T(8,128)S(1)} collective-permute-done((f32[2,128,768]{2,1,0:T(8,128)S(1)}, f32[2,128,768]{2,1,0:T(8,128)S(1)}, u32[]{:S(2)}, u32[]{:S(2)}) %collective-permute-start.23) | collective-permute-done | bytes 786464 | tf_op jit(solution)/shard_map/ppermute | solution.py:474
  271.2 2.0 fusion.65
  273.7 13.3 %collective-permute-done.27 = f32[2,128,768]{2,1,0:T(8,128)S(1)} collective-permute-done((f32[2,128,768]{2,1,0:T(8,128)S(1)}, f32[2,128,768]{2,1,0:T(8,128)S(1)}, u32[]{:S(2)}, u32[]{:S(2)}) %collective-permute-start.27) | collective-permute-done | bytes 786464 | tf_op jit(solution)/shard_map/ppermute | solution.py:474
  289.6 1.9 fusion.63
  304.3 16.2 %collective-permute-done.31 = f32[2,128,768]{2,1,0:T(8,128)} collective-permute-done((f32[2,128,768]{2,1,0:T(8,128)S(1)}, f32[2,128,768]{2,1,0:T(8,128)}, u32[]{:S(2)}, u32[]{:S(2)}) %collective-permute-start.31) | collective-permute-done | bytes 786464 | tf_op jit(solution)/shard_map/ppermute | solution.py:474
  321.9 2.5 convolution_bitcast_fusion.dg_ref
  324.4 8.2 %shard_map.257 = (bf16[16,192,128]{2,1,0:T(8,128)(2,1)}, f32[16,192,128]{2,1,0:T(8,128)}, f32[16,192,128]{2,1,0:T(8,128)}, f32[96,16,128]{2,1,0:T(8,128)}) custom-call(f32[16,192,128]{2,1,0:T(8,128)} %convolution_bitcast_fusion.dg_ref, f32[16,192,128]{2,1,0:T(8,128)} %get-tuple-element.107.q_ref, f32[16,192,128]{2,1,0:T(8,128)} %get-tuple-element.135.state_ref, ...), custom_call_target="tpu_custom_call" | custom-call | tf_op jit(solution)/shard_map/pallas_call | solution.py:411
  332.6 2.1 slice_select_fusion
  336.1 2.1 split.95
  338.2 2.5 add_select_fusion.1.refs_0_
  341.3 3.8 collective-permute-done.29
  347.7 2.8 add_select_fusion.refs_4_
  350.5 10.5 %collective-permute-done.38.refs_2_ = f32[2,128,768]{2,1,0:T(8,128)} collective-permute-done((f32[2,128,768]{2,1,0:T(8,128)}, f32[2,128,768]{2,1,0:T(8,128)}, u32[]{:S(2)}, u32[]{:S(2)}) %collective-permute-start.38) | collective-permute-done | bytes 786464 | tf_op jit(solution)/shard_map/ppermute | solution.py:474
  361.6 4.5 convolution_bitcast_fusion.2
  368.2 12.3 %collective-permute-done.44.refs_6_ = f32[2,128,768]{2,1,0:T(8,128)} collective-permute-done((f32[2,128,768]{2,1,0:T(8,128)}, f32[2,128,768]{2,1,0:T(8,128)}, u32[]{:S(2)}, u32[]{:S(2)}) %collective-permute-start.44) | collective-permute-done | bytes 786464 | tf_op jit(solution)/shard_map/ppermute | solution.py:474
  380.6 2.0 multiply_add_fusion.2
  387.2 13.0 %shard_map.258 = (f32[96,16,128]{2,1,0:T(8,128)}, f32[96,16,128]{2,1,0:T(8,128)}, f32[192,128]{1,0:T(8,128)}, f32[96,128]{1,0:T(8,128)}, f32[96,128]{1,0:T(8,128)}) custom-call(f32[16,192,128]{2,1,0:T(8,128)} %get-tuple-element.144.d_ref, f32[16,192,128]{2,1,0:T(8,128)} %get-tuple-element.106.mixed_ref, f32[96,128]{1,0:T(8,128)} %copy-done.23), custom_call_target="tpu_custom_call" | custom-call | tf_op jit(solution)/shard_map/pallas_call | solution.py:411
  400.3 7.7 %shard_map.260 = f32[16,128,768]{2,1,0:T(8,128)} custom-call(s32[8]{0:T(128)} %stack.44.blocks_ref, f32[2,128,768]{2,1,0:T(8,128)} %add_select_fusion.1.refs_0_, f32[2,128,768]{2,1,0:T(8,128)} %collective-permute-done.40.refs_1_, f32[2,128,768]{2,1,0:T(8,128)} %collective-permute-done.38.refs_2_, f32[2,128,768]{2,1,0:T(8,128)} %collective-permute-done.41.refs_3_, ...), custom_call_target="tpu_custom_call" | custom-call | tf_op jit(solution)/shard_map/pallas_call | solution.py:383
  413.9 12.0 %collective-permute-start.49 = (f32[48,768]{1,0:T(8,128)}, f32[48,768]{1,0:T(8,128)}, u32[]{:S(2)}, u32[]{:S(2)}) collective-permute-start(f32[48,768]{1,0:T(8,128)} %get-tuple-element.272), channel_id=1, source_target_pairs={{0,8},{4,12},{8,0},{12,4},{16,24},{20,28},{24,16},{28,20},{1,9},{5... | collective-permute-start | bytes 442376 | tf_op jit(solution)/shard_map/ppermute | solution.py:474
  426.0 4.3 collective-permute-start.50
  433.6 9.7 %shard_map.259 = (bf16[16,192,128]{2,1,0:T(8,128)(2,1)}, f32[16,192,128]{2,1,0:T(8,128)}, f32[192,128]{1,0:T(8,128)}, f32[192,128]{1,0:T(8,128)}) custom-call(f32[16,192,128]{2,1,0:T(8,128)} %get-tuple-element.136.dx_ref, f32[96,16,128]{2,1,0:T(8,128)} %get-tuple-element.266.gin_ref, f32[96,128]{1,0:T(8,128)} %reshape.217.coef_ref, f32[96,128]{1,0:T(8,128)} %copy-done.23, ...), custom_call_target="tpu_custom_call" | custom-call | tf_op jit(solution)/shard_map/pallas_call | solution.py:411
  445.5 7.0 %collective-permute-done.39.spill_ref = f32[192,128]{1,0:T(8,128)S(1)} collective-permute-done((f32[192,128]{1,0:T(8,128)}, f32[192,128]{1,0:T(8,128)S(1)}, u32[]{:S(2)}, u32[]{:S(2)}) %collective-permute-start.39) | collective-permute-done | bytes 98336 | tf_op jit(solution)/shard_map/ppermute | solution.py:470
  453.1 14.7 %shard_map.261 = (f32[2,128,768]{2,1,0:T(8,128)}, f32[2,128,768]{2,1,0:T(8,128)}, f32[2,128,768]{2,1,0:T(8,128)}, f32[2,128,768]{2,1,0:T(8,128)}, f32[2,128,768]...) custom-call(bf16[16,192,128]{2,1,0:T(8,128)(2,1)} %get-tuple-element, ...), custom_call_target="tpu_custom_call" | custom-call | tf_op jit(solution)/shard_map/pallas_call | solution.py:348
  472.0 2.0 collective-permute-done.53
  476.9 2.4 add.456
  480.7 4.6 collective-permute-start.57
  486.2 1.9 constant_dynamic-update-slice_fusion.21
  488.1 8.0 %collective-permute-start.58 = (f32[48,768]{1,0:T(8,128)}, f32[48,768]{1,0:T(8,128)S(1)}, u32[]{:S(2)}, u32[]{:S(2)}) collective-permute-start(f32[48,768]{1,0:T(8,128)} %get-tuple-element.235), channel_id=1, source_target_pairs={{0,8},{4,12},{8,0},{12,4},{16,24},{20,28},{24,16},{28,20},{1,9},{5... | collective-permute-start | bytes 442376 | tf_op jit(solution)/shard_map/ppermute | solution.py:474
  496.1 2.4 collective-permute-start.60
  500.6 8.2 %collective-permute-done.59 = f32[48,768]{1,0:T(8,128)S(1)} collective-permute-done((f32[48,768]{1,0:T(8,128)}, f32[48,768]{1,0:T(8,128)S(1)}, u32[]{:S(2)}, u32[]{:S(2)}) %collective-permute-start.59) | collective-permute-done | bytes 147488 | tf_op jit(solution)/shard_map/ppermute | solution.py:474
  515.3 3.7 collective-permute-start.62
  519.0 9.3 %collective-permute-done.61 = f32[2,128,768]{2,1,0:T(8,128)S(1)} collective-permute-done((f32[2,128,768]{2,1,0:T(8,128)S(1)}, f32[2,128,768]{2,1,0:T(8,128)S(1)}, u32[]{:S(2)}, u32[]{:S(2)}) %collective-permute-start.61) | collective-permute-done | bytes 786464 | tf_op jit(solution)/shard_map/ppermute | solution.py:474
  537.4 4.2 collective-permute-start.70
  541.6 2.4 collective-permute-start.72
  544.0 3.7 collective-permute-done.70
  547.7 4.9 fusion.133
  552.7 4.0 collective-permute-done.71
  560.4 13.9 %collective-permute-done.73.refs_6_ = f32[2,128,768]{2,1,0:T(8,128)} collective-permute-done((f32[2,128,768]{2,1,0:T(8,128)S(1)}, f32[2,128,768]{2,1,0:T(8,128)}, u32[]{:S(2)}, u32[]{:S(2)}) %collective-permute-start.73) | collective-permute-done | bytes 786464 | tf_op jit(solution)/shard_map/ppermute | solution.py:474
  579.1 7.7 %shard_map.262 = f32[16,128,768]{2,1,0:T(8,128)} custom-call(s32[8]{0:T(128)} %stack.44.blocks_ref, f32[2,128,768]{2,1,0:T(8,128)} %get-tuple-element.181.refs_0_, f32[2,128,768]{2,1,0:T(8,128)} %collective-permute-done.55.refs_1_, f32[2,128,768]{2,1,0:T(8,128)} %collective-permute-done.66.refs_2_, f32[2,128,768]{2,1,0:T(8,128)} %collective-permute-done.67.refs_3_, ...), custom_call_target="tpu_custom_call" | custom-call | tf_op jit(solution)/shard_map/pallas_call | solution.py:383
  (480 shorter events, 144.7 us)
Async XLA Ops:
  7.2 373.3 %reduce-scatter.2.cloned.1.call-start = ((), (), s32[]{:S(2)}) async-start(), calls=%async_computation.1 | async-start | bytes 5308416 | tf_op jit(solution)/shard_map/reduce_scatter | solution.py:729
  18.5 20.5 %collective-permute-start = (f32[192,128]{1,0:T(8,128)}, f32[192,128]{1,0:T(8,128)S(1)}, u32[]{:S(2)}, u32[]{:S(2)}) collective-permute-start(f32[192,128]{1,0:T(8,128)} %get-tuple-element.102), channel_id=1, source_target_pairs={{0,4},{4,8},{8,12},{12,16},{16,20},{20,24},{24,28},{1,5},{5,9},{9,... | collective-permute-start | bytes 294920 | tf_op jit(solution)/shard_map/ppermute | solution.py:470
  53.7 10.6 %collective-permute-start.1 = (f32[48,16,128]{2,1,0:T(8,128)S(1)}, f32[48,16,128]{2,1,0:T(8,128)S(1)}, u32[]{:S(2)}, u32[]{:S(2)}) collective-permute-start(f32[48,16,128]{2,1,0:T(8,128)S(1)} %slice_select_fusion.2), channel_id=1, source_target_pairs={{0,4},{4,0},{8,12},{12,8},{16,20},{20,16},{24,28},{28,24},{1,5},{5... | collective-permute-start | bytes 1179656 | tf_op jit(solution)/shard_map/ppermute | solution.py:474
  64.4 10.7 %collective-permute-start.2 = (f32[48,16,128]{2,1,0:T(8,128)S(1)}, f32[48,16,128]{2,1,0:T(8,128)S(1)}, u32[]{:S(2)}, u32[]{:S(2)}) collective-permute-start(f32[48,16,128]{2,1,0:T(8,128)S(1)} %get-tuple-element.250), channel_id=1, source_target_pairs={{0,8},{4,12},{8,16},{12,20},{16,24},{20,28},{1,9},{5,13},{9,17},{1... | collective-permute-start | bytes 1179656 | tf_op jit(solution)/shard_map/ppermute | solution.py:470
  75.2 11.7 %collective-permute-start.3 = (f32[48,16,128]{2,1,0:T(8,128)S(1)}, f32[48,16,128]{2,1,0:T(8,128)S(1)}, u32[]{:S(2)}, u32[]{:S(2)}) collective-permute-start(f32[48,16,128]{2,1,0:T(8,128)S(1)} %multiply_add_fusion.5), channel_id=1, source_target_pairs={{0,16},{4,20},{8,24},{12,28},{1,17},{5,21},{9,25},{13,29},{2,18},{... | collective-permute-start | bytes 1179656 | tf_op jit(solution)/shard_map/ppermute | solution.py:470
  108.5 19.6 %collective-permute-start.7 = (f32[2,128,768]{2,1,0:T(8,128)S(1)}, f32[2,128,768]{2,1,0:T(8,128)S(1)}, u32[]{:S(2)}, u32[]{:S(2)}) collective-permute-start(f32[2,128,768]{2,1,0:T(8,128)S(1)} %slice_add_fusion.3), channel_id=1, source_target_pairs={{0,2},{1,3},{2,0},{3,1},{4,6},{5,7},{6,4},{7,5},{8,10},{9,11},{10,... | collective-permute-start | bytes 2359304 | tf_op jit(solution)/shard_map/ppermute | solution.py:474
  110.5 20.2 %collective-permute-start.5 = (f32[2,128,768]{2,1,0:T(8,128)S(1)}, f32[2,128,768]{2,1,0:T(8,128)S(1)}, u32[]{:S(2)}, u32[]{:S(2)}) collective-permute-start(f32[2,128,768]{2,1,0:T(8,128)S(1)} %split.97), channel_id=1, source_target_pairs={{0,1},{1,0},{2,3},{3,2},{4,5},{5,4},{6,7},{7,6},{8,9},{9,8},{10,11... | collective-permute-start | bytes 2359304 | tf_op jit(solution)/shard_map/ppermute | solution.py:474
  111.0 19.7 %collective-permute-start.8 = (f32[2,128,768]{2,1,0:T(8,128)S(1)}, f32[2,128,768]{2,1,0:T(8,128)S(1)}, u32[]{:S(2)}, u32[]{:S(2)}) collective-permute-start(f32[2,128,768]{2,1,0:T(8,128)S(1)} %split.101), channel_id=1, source_target_pairs={{0,1},{1,0},{2,3},{3,2},{4,5},{5,4},{6,7},{7,6},{8,9},{9,8},{10,11... | collective-permute-start | bytes 2359304 | tf_op jit(solution)/shard_map/ppermute | solution.py:474
  128.1 18.8 %collective-permute-start.10 = (f32[2,128,768]{2,1,0:T(8,128)S(1)}, f32[2,128,768]{2,1,0:T(8,128)S(1)}, u32[]{:S(2)}, u32[]{:S(2)}) collective-permute-start(f32[2,128,768]{2,1,0:T(8,128)S(1)} %slice_add_fusion.1), channel_id=1, source_target_pairs={{0,2},{1,3},{2,0},{3,1},{4,6},{5,7},{6,4},{7,5},{8,10},{9,11},{10,... | collective-permute-start | bytes 2359304 | tf_op jit(solution)/shard_map/ppermute | solution.py:474
  149.6 20.0 %collective-permute-start.12 = (f32[2,128,768]{2,1,0:T(8,128)S(1)}, f32[2,128,768]{2,1,0:T(8,128)S(1)}, u32[]{:S(2)}, u32[]{:S(2)}) collective-permute-start(f32[2,128,768]{2,1,0:T(8,128)S(1)} %subtract_multiply_fusion.3), channel_id=1, source_target_pairs={{0,1},{1,0},{2,3},{3,2},{4,5},{5,4},{6,7},{7,6},{8,9},{9,8},{10,11... | collective-permute-start | bytes 2359304 | tf_op jit(solution)/shard_map/ppermute | solution.py:474
  149.7 20.0 %collective-permute-start.11 = (f32[2,128,768]{2,1,0:T(8,128)S(1)}, f32[2,128,768]{2,1,0:T(8,128)S(1)}, u32[]{:S(2)}, u32[]{:S(2)}) collective-permute-start(f32[2,128,768]{2,1,0:T(8,128)S(1)} %subtract_multiply_fusion.3), channel_id=1, source_target_pairs={{0,2},{1,3},{2,0},{3,1},{4,6},{5,7},{6,4},{7,5},{8,10},{9,11},{10,... | collective-permute-start | bytes 2359304 | tf_op jit(solution)/shard_map/ppermute | solution.py:474
  151.6 18.0 %collective-permute-start.14 = (f32[2,128,768]{2,1,0:T(8,128)S(1)}, f32[2,128,768]{2,1,0:T(8,128)S(1)}, u32[]{:S(2)}, u32[]{:S(2)}) collective-permute-start(f32[2,128,768]{2,1,0:T(8,128)S(1)} %subtract_multiply_fusion.2), channel_id=1, source_target_pairs={{0,1},{1,0},{2,3},{3,2},{4,5},{5,4},{6,7},{7,6},{8,9},{9,8},{10,11... | collective-permute-start | bytes 2359304 | tf_op jit(solution)/shard_map/ppermute | solution.py:474
  182.8 19.6 %collective-permute-start.13 = (f32[2,128,768]{2,1,0:T(8,128)S(1)}, f32[2,128,768]{2,1,0:T(8,128)S(1)}, u32[]{:S(2)}, u32[]{:S(2)}) collective-permute-start(f32[2,128,768]{2,1,0:T(8,128)S(1)} %subtract_multiply_fusion.2), channel_id=1, source_target_pairs={{0,2},{1,3},{2,0},{3,1},{4,6},{5,7},{6,4},{7,5},{8,10},{9,11},{10,... | collective-permute-start | bytes 2359304 | tf_op jit(solution)/shard_map/ppermute | solution.py:474
  204.0 30.2 %collective-permute-start.25 = (f32[2,128,768]{2,1,0:T(8,128)}, f32[2,128,768]{2,1,0:T(8,128)}, u32[]{:S(2)}, u32[]{:S(2)}) collective-permute-start(f32[2,128,768]{2,1,0:T(8,128)} %split.87), channel_id=1, source_target_pairs={{0,1},{1,0},{2,3},{3,2},{4,5},{5,4},{6,7},{7,6},{8,9},{9,8},{10,11... | collective-permute-start | bytes 2359304 | tf_op jit(solution)/shard_map/ppermute | solution.py:474
  208.6 20.0 %collective-permute-start.18 = (f32[2,128,768]{2,1,0:T(8,128)S(1)}, f32[2,128,768]{2,1,0:T(8,128)}, u32[]{:S(2)}, u32[]{:S(2)}) collective-permute-start(f32[2,128,768]{2,1,0:T(8,128)S(1)} %slice_add_fusion.7), channel_id=1, source_target_pairs={{0,2},{1,3},{2,0},{3,1},{4,6},{5,7},{6,4},{7,5},{8,10},{9,11},{10,... | collective-permute-start | bytes 2359304 | tf_op jit(solution)/shard_map/ppermute | solution.py:474
  228.5 19.2 %collective-permute-start.22 = (f32[2,128,768]{2,1,0:T(8,128)}, f32[2,128,768]{2,1,0:T(8,128)S(1)}, u32[]{:S(2)}, u32[]{:S(2)}) collective-permute-start(f32[2,128,768]{2,1,0:T(8,128)} %slice_add_fusion), channel_id=1, source_target_pairs={{0,2},{1,3},{2,0},{3,1},{4,6},{5,7},{6,4},{7,5},{8,10},{9,11},{10,... | collective-permute-start | bytes 2359304 | tf_op jit(solution)/shard_map/ppermute | solution.py:474
  232.5 315.2 %all-gather.2.cloned.1.call-start = ((), (), s32[]{:S(2)}) async-start(), calls=%async_computation.2 | async-start | bytes 5308416 | tf_op jit(solution)/shard_map/all_gather | solution.py:791
  234.1 15.2 %collective-permute-start.16 = (f32[2,128,768]{2,1,0:T(8,128)S(1)}, f32[2,128,768]{2,1,0:T(8,128)S(1)}, u32[]{:S(2)}, u32[]{:S(2)}) collective-permute-start(f32[2,128,768]{2,1,0:T(8,128)S(1)} %split.81), channel_id=1, source_target_pairs={{0,1},{1,0},{2,3},{3,2},{4,5},{5,4},{6,7},{7,6},{8,9},{9,8},{10,11... | collective-permute-start | bytes 2359304 | tf_op jit(solution)/shard_map/ppermute | solution.py:474
  251.6 18.1 %collective-permute-start.23 = (f32[2,128,768]{2,1,0:T(8,128)S(1)}, f32[2,128,768]{2,1,0:T(8,128)S(1)}, u32[]{:S(2)}, u32[]{:S(2)}) collective-permute-start(f32[2,128,768]{2,1,0:T(8,128)S(1)} %subtract_multiply_fusion.1), channel_id=1, source_target_pairs={{0,2},{1,3},{2,0},{3,1},{4,6},{5,7},{6,4},{7,5},{8,10},{9,11},{10,... | collective-permute-start | bytes 2359304 | tf_op jit(solution)/shard_map/ppermute | solution.py:474
  269.7 17.3 %collective-permute-start.27 = (f32[2,128,768]{2,1,0:T(8,128)S(1)}, f32[2,128,768]{2,1,0:T(8,128)S(1)}, u32[]{:S(2)}, u32[]{:S(2)}) collective-permute-start(f32[2,128,768]{2,1,0:T(8,128)S(1)} %get-tuple-element.131), channel_id=1, source_target_pairs={{0,2},{1,3},{2,0},{3,1},{4,6},{5,7},{6,4},{7,5},{8,10},{9,11},{10,... | collective-permute-start | bytes 2359304 | tf_op jit(solution)/shard_map/ppermute | solution.py:474
  273.2 18.4 %collective-permute-start.19 = (f32[2,128,768]{2,1,0:T(8,128)S(1)}, f32[2,128,768]{2,1,0:T(8,128)S(1)}, u32[]{:S(2)}, u32[]{:S(2)}) collective-permute-start(f32[2,128,768]{2,1,0:T(8,128)S(1)} %subtract_multiply_fusion.1), channel_id=1, source_target_pairs={{0,1},{1,0},{2,3},{3,2},{4,5},{5,4},{6,7},{7,6},{8,9},{9,8},{10,11... | collective-permute-start | bytes 2359304 | tf_op jit(solution)/shard_map/ppermute | solution.py:474
  273.2 18.4 %collective-permute-start.26 = (f32[2,128,768]{2,1,0:T(8,128)S(1)}, f32[2,128,768]{2,1,0:T(8,128)S(1)}, u32[]{:S(2)}, u32[]{:S(2)}) collective-permute-start(f32[2,128,768]{2,1,0:T(8,128)S(1)} %get-tuple-element.131), channel_id=1, source_target_pairs={{0,1},{1,0},{2,3},{3,2},{4,5},{5,4},{6,7},{7,6},{8,9},{9,8},{10,11... | collective-permute-start | bytes 2359304 | tf_op jit(solution)/shard_map/ppermute | solution.py:474
  273.7 17.9 %collective-permute-start.24 = (f32[2,128,768]{2,1,0:T(8,128)S(1)}, f32[2,128,768]{2,1,0:T(8,128)S(1)}, u32[]{:S(2)}, u32[]{:S(2)}) collective-permute-start(f32[2,128,768]{2,1,0:T(8,128)S(1)} %collective-permute-done.23), channel_id=1, source_target_pairs={{0,1},{1,0},{2,3},{3,2},{4,5},{5,4},{6,7},{7,6},{8,9},{9,8},{10,11... | collective-permute-start | bytes 2359304 | tf_op jit(solution)/shard_map/ppermute | solution.py:474
  296.3 41.9 %collective-permute-start.37 = (f32[2,128,768]{2,1,0:T(8,128)}, f32[2,128,768]{2,1,0:T(8,128)}, u32[]{:S(2)}, u32[]{:S(2)}) collective-permute-start(f32[2,128,768]{2,1,0:T(8,128)} %split.93), channel_id=1, source_target_pairs={{0,1},{1,0},{2,3},{3,2},{4,5},{5,4},{6,7},{7,6},{8,9},{9,8},{10,11... | collective-permute-start | bytes 2359304 | tf_op jit(solution)/shard_map/ppermute | solution.py:474
  300.4 20.0 %collective-permute-start.31 = (f32[2,128,768]{2,1,0:T(8,128)S(1)}, f32[2,128,768]{2,1,0:T(8,128)}, u32[]{:S(2)}, u32[]{:S(2)}) collective-permute-start(f32[2,128,768]{2,1,0:T(8,128)S(1)} %slice_add_fusion.6), channel_id=1, source_target_pairs={{0,2},{1,3},{2,0},{3,1},{4,6},{5,7},{6,4},{7,5},{8,10},{9,11},{10,... | collective-permute-start | bytes 2359304 | tf_op jit(solution)/shard_map/ppermute | solution.py:474
  320.4 20.3 %collective-permute-start.35 = (f32[2,128,768]{2,1,0:T(8,128)}, f32[2,128,768]{2,1,0:T(8,128)}, u32[]{:S(2)}, u32[]{:S(2)}) collective-permute-start(f32[2,128,768]{2,1,0:T(8,128)} %slice_add_fusion.5), channel_id=1, source_target_pairs={{0,2},{1,3},{2,0},{3,1},{4,6},{5,7},{6,4},{7,5},{8,10},{9,11},{10,... | collective-permute-start | bytes 2359304 | tf_op jit(solution)/shard_map/ppermute | solution.py:474
  334.6 10.5 %collective-permute-start.29 = (f32[48,16,128]{2,1,0:T(8,128)}, f32[48,16,128]{2,1,0:T(8,128)S(1)}, u32[]{:S(2)}, u32[]{:S(2)}) collective-permute-start(f32[48,16,128]{2,1,0:T(8,128)} %slice_select_fusion), channel_id=1, source_target_pairs={{0,4},{4,0},{8,12},{12,8},{16,20},{20,16},{24,28},{28,24},{1,5},{5... | collective-permute-start | bytes 1179656 | tf_op jit(solution)/shard_map/ppermute | solution.py:474
  338.2 9.5 %collective-permute-start.42 = (f32[2,128,768]{2,1,0:T(8,128)}, f32[2,128,768]{2,1,0:T(8,128)}, u32[]{:S(2)}, u32[]{:S(2)}) collective-permute-start(f32[2,128,768]{2,1,0:T(8,128)} %split.95), channel_id=1, source_target_pairs={{0,1},{1,0},{2,3},{3,2},{4,5},{5,4},{6,7},{7,6},{8,9},{9,8},{10,11... | collective-permute-start | bytes 2359304 | tf_op jit(solution)/shard_map/ppermute | solution.py:474
  340.7 20.3 %collective-permute-start.38 = (f32[2,128,768]{2,1,0:T(8,128)}, f32[2,128,768]{2,1,0:T(8,128)}, u32[]{:S(2)}, u32[]{:S(2)}) collective-permute-start(f32[2,128,768]{2,1,0:T(8,128)} %add_select_fusion.1.refs_0_), channel_id=1, source_target_pairs={{0,2},{1,3},{2,0},{3,1},{4,6},{5,7},{6,4},{7,5},{8,10},{9,11},{10,... | collective-permute-start | bytes 2359304 | tf_op jit(solution)/shard_map/ppermute | solution.py:474
  346.4 34.1 %collective-permute-start.32 = (f32[48,16,128]{2,1,0:T(8,128)S(1)}, f32[48,16,128]{2,1,0:T(8,128)}, u32[]{:S(2)}, u32[]{:S(2)}) collective-permute-start(f32[48,16,128]{2,1,0:T(8,128)S(1)} %select_add_fusion), channel_id=1, source_target_pairs={{8,0},{12,4},{16,8},{20,12},{24,16},{28,20},{9,1},{13,5},{17,9},{2... | collective-permute-start | bytes 1179656 | tf_op jit(solution)/shard_map/ppermute | solution.py:470
  361.0 19.5 %collective-permute-start.44 = (f32[2,128,768]{2,1,0:T(8,128)}, f32[2,128,768]{2,1,0:T(8,128)}, u32[]{:S(2)}, u32[]{:S(2)}) collective-permute-start(f32[2,128,768]{2,1,0:T(8,128)} %add_select_fusion.refs_4_), channel_id=1, source_target_pairs={{0,2},{1,3},{2,0},{3,1},{4,6},{5,7},{6,4},{7,5},{8,10},{9,11},{10,... | collective-permute-start | bytes 2359304 | tf_op jit(solution)/shard_map/ppermute | solution.py:474
  366.1 20.0 %collective-permute-start.40 = (f32[2,128,768]{2,1,0:T(8,128)}, f32[2,128,768]{2,1,0:T(8,128)}, u32[]{:S(2)}, u32[]{:S(2)}) collective-permute-start(f32[2,128,768]{2,1,0:T(8,128)} %add_select_fusion.1.refs_0_), channel_id=1, source_target_pairs={{0,1},{1,0},{2,3},{3,2},{4,5},{5,4},{6,7},{7,6},{8,9},{9,8},{10,11... | collective-permute-start | bytes 2359304 | tf_op jit(solution)/shard_map/ppermute | solution.py:474
  367.7 32.6 %collective-permute-start.43 = (f32[2,128,768]{2,1,0:T(8,128)}, f32[2,128,768]{2,1,0:T(8,128)}, u32[]{:S(2)}, u32[]{:S(2)}) collective-permute-start(f32[2,128,768]{2,1,0:T(8,128)} %add_select_fusion.refs_4_), channel_id=1, source_target_pairs={{0,1},{1,0},{2,3},{3,2},{4,5},{5,4},{6,7},{7,6},{8,9},{9,8},{10,11... | collective-permute-start | bytes 2359304 | tf_op jit(solution)/shard_map/ppermute | solution.py:474
  368.2 32.1 %collective-permute-start.41 = (f32[2,128,768]{2,1,0:T(8,128)}, f32[2,128,768]{2,1,0:T(8,128)}, u32[]{:S(2)}, u32[]{:S(2)}) collective-permute-start(f32[2,128,768]{2,1,0:T(8,128)} %collective-permute-done.38.refs_2_), channel_id=1, source_target_pairs={{0,1},{1,0},{2,3},{3,2},{4,5},{5,4},{6,7},{7,6},{8,9},{9,8},{10,11... | collective-permute-start | bytes 2359304 | tf_op jit(solution)/shard_map/ppermute | solution.py:474
  380.5 19.8 %collective-permute-start.45 = (f32[2,128,768]{2,1,0:T(8,128)}, f32[2,128,768]{2,1,0:T(8,128)}, u32[]{:S(2)}, u32[]{:S(2)}) collective-permute-start(f32[2,128,768]{2,1,0:T(8,128)} %collective-permute-done.44.refs_6_), channel_id=1, source_target_pairs={{0,1},{1,0},{2,3},{3,2},{4,5},{5,4},{6,7},{7,6},{8,9},{9,8},{10,11... | collective-permute-start | bytes 2359304 | tf_op jit(solution)/shard_map/ppermute | solution.py:474
  382.6 25.4 %collective-permute-start.33 = (f32[48,16,128]{2,1,0:T(8,128)}, f32[48,16,128]{2,1,0:T(8,128)}, u32[]{:S(2)}, u32[]{:S(2)}) collective-permute-start(f32[48,16,128]{2,1,0:T(8,128)} %multiply_add_fusion.2), channel_id=1, source_target_pairs={{16,0},{20,4},{24,8},{28,12},{17,1},{21,5},{25,9},{29,13},{18,2},{... | collective-permute-start | bytes 1179656 | tf_op jit(solution)/shard_map/ppermute | solution.py:470
  386.1 25.9 %collective-permute-start.46 = (f32[192,768]{1,0:T(8,128)}, f32[192,768]{1,0:T(8,128)}, u32[]{:S(2)}, u32[]{:S(2)}) collective-permute-start(f32[192,768]{1,0:T(8,128)} %constant_dynamic-slice_fusion.7), channel_id=1, source_target_pairs={{0,4},{4,0},{8,12},{12,8},{16,20},{20,16},{24,28},{28,24},{1,5},{5... | collective-permute-start | bytes 1769480 | tf_op jit(solution)/shard_map/ppermute | solution.py:474
  409.7 20.7 %collective-permute-start.36 = (f32[48,16,128]{2,1,0:T(8,128)S(1)}, f32[48,16,128]{2,1,0:T(8,128)S(1)}, u32[]{:S(2)}, u32[]{:S(2)}) collective-permute-start(f32[48,16,128]{2,1,0:T(8,128)S(1)} %fusion.112), channel_id=1, source_target_pairs={{0,4},{4,0},{8,12},{12,8},{16,20},{20,16},{24,28},{28,24},{1,5},{5... | collective-permute-start | bytes 1179656 | tf_op jit(solution)/shard_map/ppermute | solution.py:474
  413.9 65.4 %collective-permute-start.49 = (f32[48,768]{1,0:T(8,128)}, f32[48,768]{1,0:T(8,128)}, u32[]{:S(2)}, u32[]{:S(2)}) collective-permute-start(f32[48,768]{1,0:T(8,128)} %get-tuple-element.272), channel_id=1, source_target_pairs={{0,8},{4,12},{8,0},{12,4},{16,24},{20,28},{24,16},{28,20},{1,9},{5... | collective-permute-start | bytes 442376 | tf_op jit(solution)/shard_map/ppermute | solution.py:474
  426.0 53.4 %collective-permute-start.50 = (f32[48,768]{1,0:T(8,128)}, f32[48,768]{1,0:T(8,128)}, u32[]{:S(2)}, u32[]{:S(2)}) collective-permute-start(f32[48,768]{1,0:T(8,128)} %get-tuple-element.271), channel_id=1, source_target_pairs={{0,16},{4,20},{8,24},{12,28},{16,0},{20,4},{24,8},{28,12},{1,17},{... | collective-permute-start | bytes 442376 | tf_op jit(solution)/shard_map/ppermute | solution.py:474
  430.3 49.1 %collective-permute-start.51 = (f32[48,768]{1,0:T(8,128)}, f32[48,768]{1,0:T(8,128)}, u32[]{:S(2)}, u32[]{:S(2)}) collective-permute-start(f32[48,768]{1,0:T(8,128)} %get-tuple-element.270), channel_id=1, source_target_pairs={{0,24},{4,28},{8,16},{12,20},{16,8},{20,12},{24,0},{28,4},{1,25},{... | collective-permute-start | bytes 442376 | tf_op jit(solution)/shard_map/ppermute | solution.py:474
  443.3 9.1 %collective-permute-start.39 = (f32[192,128]{1,0:T(8,128)}, f32[192,128]{1,0:T(8,128)S(1)}, u32[]{:S(2)}, u32[]{:S(2)}) collective-permute-start(f32[192,128]{1,0:T(8,128)} %get-tuple-element.156), channel_id=1, source_target_pairs={{4,0},{8,4},{12,8},{16,12},{20,16},{24,20},{28,24},{5,1},{9,5},{13... | collective-permute-start | bytes 294920 | tf_op jit(solution)/shard_map/ppermute | solution.py:470
  468.6 8.3 %collective-permute-start.48 = (f32[2,128,768]{2,1,0:T(8,128)}, f32[2,128,768]{2,1,0:T(8,128)}, u32[]{:S(2)}, u32[]{:S(2)}) collective-permute-start(f32[2,128,768]{2,1,0:T(8,128)} %get-tuple-element.168), channel_id=1, source_target_pairs={{0,1},{1,0},{2,3},{3,2},{4,5},{5,4},{6,7},{7,6},{8,9},{9,8},{10,11... | collective-permute-start | bytes 2359304 | tf_op jit(solution)/shard_map/ppermute | solution.py:474
  474.0 22.1 %collective-permute-start.56 = (f32[2,128,768]{2,1,0:T(8,128)}, f32[2,128,768]{2,1,0:T(8,128)}, u32[]{:S(2)}, u32[]{:S(2)}) collective-permute-start(f32[2,128,768]{2,1,0:T(8,128)} %get-tuple-element.172), channel_id=1, source_target_pairs={{0,1},{1,0},{2,3},{3,2},{4,5},{5,4},{6,7},{7,6},{8,9},{9,8},{10,11... | collective-permute-start | bytes 2359304 | tf_op jit(solution)/shard_map/ppermute | solution.py:474
  479.4 29.5 %collective-permute-start.54 = (f32[2,128,768]{2,1,0:T(8,128)}, f32[2,128,768]{2,1,0:T(8,128)}, u32[]{:S(2)}, u32[]{:S(2)}) collective-permute-start(f32[2,128,768]{2,1,0:T(8,128)} %add.456), channel_id=1, source_target_pairs={{0,2},{1,3},{2,0},{3,1},{4,6},{5,7},{6,4},{7,5},{8,10},{9,11},{10,... | collective-permute-start | bytes 2359304 | tf_op jit(solution)/shard_map/ppermute | solution.py:474
  480.7 28.2 %collective-permute-start.57 = (f32[224,768]{1,0:T(8,128)}, f32[224,768]{1,0:T(8,128)}, u32[]{:S(2)}, u32[]{:S(2)}) collective-permute-start(f32[224,768]{1,0:T(8,128)} %constant_dynamic-slice_fusion.3), channel_id=1, source_target_pairs={{0,4},{4,0},{8,12},{12,8},{16,20},{20,16},{24,28},{28,24},{1,5},{5... | collective-permute-start | bytes 2064392 | tf_op jit(solution)/shard_map/ppermute | solution.py:474
  488.1 12.6 %collective-permute-start.58 = (f32[48,768]{1,0:T(8,128)}, f32[48,768]{1,0:T(8,128)S(1)}, u32[]{:S(2)}, u32[]{:S(2)}) collective-permute-start(f32[48,768]{1,0:T(8,128)} %get-tuple-element.235), channel_id=1, source_target_pairs={{0,8},{4,12},{8,0},{12,4},{16,24},{20,28},{24,16},{28,20},{1,9},{5... | collective-permute-start | bytes 442376 | tf_op jit(solution)/shard_map/ppermute | solution.py:474
  496.1 12.8 %collective-permute-start.59 = (f32[48,768]{1,0:T(8,128)}, f32[48,768]{1,0:T(8,128)S(1)}, u32[]{:S(2)}, u32[]{:S(2)}) collective-permute-start(f32[48,768]{1,0:T(8,128)} %get-tuple-element.235), channel_id=1, source_target_pairs={{0,16},{4,20},{8,24},{12,28},{16,0},{20,4},{24,8},{28,12},{1,17},{... | collective-permute-start | bytes 442376 | tf_op jit(solution)/shard_map/ppermute | solution.py:474
  496.1 12.8 %collective-permute-start.60 = (f32[48,768]{1,0:T(8,128)}, f32[48,768]{1,0:T(8,128)}, u32[]{:S(2)}, u32[]{:S(2)}) collective-permute-start(f32[48,768]{1,0:T(8,128)} %get-tuple-element.235), channel_id=1, source_target_pairs={{0,24},{4,28},{8,16},{12,20},{16,8},{20,12},{24,0},{28,4},{1,25},{... | collective-permute-start | bytes 442376 | tf_op jit(solution)/shard_map/ppermute | solution.py:474
  500.6 18.4 %collective-permute-start.68 = (f32[2,128,768]{2,1,0:T(8,128)}, f32[2,128,768]{2,1,0:T(8,128)S(1)}, u32[]{:S(2)}, u32[]{:S(2)}) collective-permute-start(f32[2,128,768]{2,1,0:T(8,128)} %get-tuple-element.183), channel_id=1, source_target_pairs={{0,1},{1,0},{2,3},{3,2},{4,5},{5,4},{6,7},{7,6},{8,9},{9,8},{10,11... | collective-permute-start | bytes 2359304 | tf_op jit(solution)/shard_map/ppermute | solution.py:474
  508.9 19.4 %collective-permute-start.61 = (f32[2,128,768]{2,1,0:T(8,128)S(1)}, f32[2,128,768]{2,1,0:T(8,128)S(1)}, u32[]{:S(2)}, u32[]{:S(2)}) collective-permute-start(f32[2,128,768]{2,1,0:T(8,128)S(1)} %add.469), channel_id=1, source_target_pairs={{0,2},{1,3},{2,0},{3,1},{4,6},{5,7},{6,4},{7,5},{8,10},{9,11},{10,... | collective-permute-start | bytes 2359304 | tf_op jit(solution)/shard_map/ppermute | solution.py:474
  513.8 20.0 %collective-permute-start.65 = (f32[192,768]{1,0:T(8,128)}, f32[192,768]{1,0:T(8,128)S(1)}, u32[]{:S(2)}, u32[]{:S(2)}) collective-permute-start(f32[192,768]{1,0:T(8,128)} %constant_dynamic-update-slice_fusion.18), channel_id=1, source_target_pairs={{0,4},{4,0},{8,12},{12,8},{16,20},{20,16},{24,28},{28,24},{1,5},{5... | collective-permute-start | bytes 1769480 | tf_op jit(solution)/shard_map/ppermute | solution.py:474
  514.0 15.6 %collective-permute-start.47 = (f32[2,128,768]{2,1,0:T(8,128)S(1)}, f32[2,128,768]{2,1,0:T(8,128)S(1)}, u32[]{:S(2)}, u32[]{:S(2)}) collective-permute-start(f32[2,128,768]{2,1,0:T(8,128)S(1)} %copy-done.88), channel_id=1, source_target_pairs={{0,1},{1,0},{2,3},{3,2},{4,5},{5,4},{6,7},{7,6},{8,9},{9,8},{10,11... | collective-permute-start | bytes 2359304 | tf_op jit(solution)/shard_map/ppermute | solution.py:474
  515.3 18.4 %collective-permute-start.62 = (f32[56,768]{1,0:T(8,128)S(1)}, f32[56,768]{1,0:T(8,128)S(1)}, u32[]{:S(2)}, u32[]{:S(2)}) collective-permute-start(f32[56,768]{1,0:T(8,128)S(1)} %get-tuple-element.269), channel_id=1, source_target_pairs={{0,8},{4,12},{8,0},{12,4},{16,24},{20,28},{24,16},{28,20},{1,9},{5... | collective-permute-start | bytes 516104 | tf_op jit(solution)/shard_map/ppermute | solution.py:474
  519.0 14.7 %collective-permute-start.63 = (f32[56,768]{1,0:T(8,128)S(1)}, f32[56,768]{1,0:T(8,128)S(1)}, u32[]{:S(2)}, u32[]{:S(2)}) collective-permute-start(f32[56,768]{1,0:T(8,128)S(1)} %get-tuple-element.268), channel_id=1, source_target_pairs={{0,16},{4,20},{8,24},{12,28},{16,0},{20,4},{24,8},{28,12},{1,17},{... | collective-permute-start | bytes 516104 | tf_op jit(solution)/shard_map/ppermute | solution.py:474
  535.6 21.1 %collective-permute-start.66 = (f32[2,128,768]{2,1,0:T(8,128)}, f32[2,128,768]{2,1,0:T(8,128)}, u32[]{:S(2)}, u32[]{:S(2)}) collective-permute-start(f32[2,128,768]{2,1,0:T(8,128)} %get-tuple-element.181.refs_0_), channel_id=1, source_target_pairs={{0,2},{1,3},{2,0},{3,1},{4,6},{5,7},{6,4},{7,5},{8,10},{9,11},{10,... | collective-permute-start | bytes 2359304 | tf_op jit(solution)/shard_map/ppermute | solution.py:474
  537.4 10.3 %collective-permute-start.70 = (f32[56,768]{1,0:T(8,128)S(1)}, f32[56,768]{1,0:T(8,128)S(1)}, u32[]{:S(2)}, u32[]{:S(2)}) collective-permute-start(f32[56,768]{1,0:T(8,128)S(1)} %get-tuple-element.233), channel_id=1, source_target_pairs={{0,8},{4,12},{8,0},{12,4},{16,24},{20,28},{24,16},{28,20},{1,9},{5... | collective-permute-start | bytes 516104 | tf_op jit(solution)/shard_map/ppermute | solution.py:474
  541.6 15.1 %collective-permute-start.71 = (f32[56,768]{1,0:T(8,128)S(1)}, f32[56,768]{1,0:T(8,128)S(1)}, u32[]{:S(2)}, u32[]{:S(2)}) collective-permute-start(f32[56,768]{1,0:T(8,128)S(1)} %get-tuple-element.233), channel_id=1, source_target_pairs={{0,16},{4,20},{8,24},{12,28},{16,0},{20,4},{24,8},{28,12},{1,17},{... | collective-permute-start | bytes 516104 | tf_op jit(solution)/shard_map/ppermute | solution.py:474
  541.6 15.1 %collective-permute-start.72 = (f32[56,768]{1,0:T(8,128)S(1)}, f32[56,768]{1,0:T(8,128)S(1)}, u32[]{:S(2)}, u32[]{:S(2)}) collective-permute-start(f32[56,768]{1,0:T(8,128)S(1)} %get-tuple-element.233), channel_id=1, source_target_pairs={{0,24},{4,28},{8,16},{12,20},{16,8},{20,12},{24,0},{28,4},{1,25},{... | collective-permute-start | bytes 516104 | tf_op jit(solution)/shard_map/ppermute | solution.py:474
  556.7 17.6 %collective-permute-start.73 = (f32[2,128,768]{2,1,0:T(8,128)S(1)}, f32[2,128,768]{2,1,0:T(8,128)}, u32[]{:S(2)}, u32[]{:S(2)}) collective-permute-start(f32[2,128,768]{2,1,0:T(8,128)S(1)} %copy-done.27), channel_id=1, source_target_pairs={{0,2},{1,3},{2,0},{3,1},{4,6},{5,7},{6,4},{7,5},{8,10},{9,11},{10,... | collective-permute-start | bytes 2359304 | tf_op jit(solution)/shard_map/ppermute | solution.py:474
  557.1 17.3 %collective-permute-start.75 = (f32[224,768]{1,0:T(8,128)S(1)}, f32[224,768]{1,0:T(8,128)S(1)}, u32[]{:S(2)}, u32[]{:S(2)}) collective-permute-start(f32[224,768]{1,0:T(8,128)S(1)} %constant_dynamic-update-slice_fusion.14), channel_id=1, source_target_pairs={{0,4},{4,0},{8,12},{12,8},{16,20},{20,16},{24,28},{28,24},{1,5},{5... | collective-permute-start | bytes 2064392 | tf_op jit(solution)/shard_map/ppermute | solution.py:474
  559.9 19.2 %collective-permute-start.55 = (f32[2,128,768]{2,1,0:T(8,128)}, f32[2,128,768]{2,1,0:T(8,128)}, u32[]{:S(2)}, u32[]{:S(2)}) collective-permute-start(f32[2,128,768]{2,1,0:T(8,128)} %get-tuple-element.181.refs_0_), channel_id=1, source_target_pairs={{0,1},{1,0},{2,3},{3,2},{4,5},{5,4},{6,7},{7,6},{8,9},{9,8},{10,11... | collective-permute-start | bytes 2359304 | tf_op jit(solution)/shard_map/ppermute | solution.py:474
  559.9 19.2 %collective-permute-start.69 = (f32[2,128,768]{2,1,0:T(8,128)S(1)}, f32[2,128,768]{2,1,0:T(8,128)}, u32[]{:S(2)}, u32[]{:S(2)}) collective-permute-start(f32[2,128,768]{2,1,0:T(8,128)S(1)} %copy-done.27), channel_id=1, source_target_pairs={{0,1},{1,0},{2,3},{3,2},{4,5},{5,4},{6,7},{7,6},{8,9},{9,8},{10,11... | collective-permute-start | bytes 2359304 | tf_op jit(solution)/shard_map/ppermute | solution.py:474
  560.4 18.7 %collective-permute-start.67 = (f32[2,128,768]{2,1,0:T(8,128)}, f32[2,128,768]{2,1,0:T(8,128)}, u32[]{:S(2)}, u32[]{:S(2)}) collective-permute-start(f32[2,128,768]{2,1,0:T(8,128)} %collective-permute-done.66.refs_2_), channel_id=1, source_target_pairs={{0,1},{1,0},{2,3},{3,2},{4,5},{5,4},{6,7},{7,6},{8,9},{9,8},{10,11... | collective-permute-start | bytes 2359304 | tf_op jit(solution)/shard_map/ppermute | solution.py:474
  (111 other events, 1434.5 us)
Sparse Core Ops, SparseCore 0:
  232.7 106.9 reduce-scatter.1
  380.7 103.2 all-gather.1

commit v3 on v2

--- a/solution.py
+++ b/solution.py
@@ -228,8 +228,8 @@
 
 
 def first_kernel(
-    mine_ref, x_ref, gain_ref, wq_ref, wk_ref, wv_ref, normed_ref, q_ref, k_ref, v_ref, tail_ref,
-    *, edge
+    at_ref, x_ref, cot_ref, gain_ref, wq_ref, wk_ref, wv_ref, normed_ref, cut_ref, q_ref, k_ref,
+    v_ref, tail_ref, *, edge, chunks, parts
 ):
     step = pl.program_id(0)
     channels = wq_ref.shape[0]
@@ -244,6 +244,11 @@
     spread = jnp.mean(center * center, axis=-1, keepdims=True)
     normed = (center * lax.rsqrt(spread + 1e-05) * gain_ref[...]).astype(BF)
     normed_ref[...] = normed.reshape(normed_ref.shape)
+    place = at_ref[1] * LANES + lax.broadcasted_iota(jnp.int32, cot_ref.shape[1:], 0)
+    first = 2 + seqs * ((at_ref[0] ^ (step % parts)) * chunks + step // parts)
+    for j in range(seqs):
+        kept = jnp.where(place < at_ref[first + j], cot_ref[j].astype(F32), 0.0)
+        cut_ref[j] = kept.astype(BF)
     lane = lax.broadcasted_iota(jnp.int32, (channels, LANES), 1)
     for w_ref, out_ref in ((wq_ref, q_ref), (wk_ref, k_ref), (wv_ref, v_ref)):
         out = lax.dot_general(
@@ -298,7 +303,7 @@
             piece_ref[...] = rows.reshape(piece_ref.shape)
 
 
-def first_call(mine, inputs, gain, weights, edge, chunks, parts):
+def first_call(at, inputs, cotangent, gain, weights, edge, chunks, parts):
     num_seqs, _, width = inputs.shape
     channels = weights[0].shape[0]
     seqs = num_seqs // (chunks * parts)
@@ -306,22 +311,25 @@
     act = pl.BlockSpec((seqs, channels, LANES), lambda s, m: (s, 0, 0))
     rows = pl.BlockSpec((seqs, LANES, width), lambda s, m: (s, 0, 0))
     a = shape(num_seqs, channels, LANES)
+    own = pl.BlockSpec(
+        (seqs, LANES, width),
+        lambda s, m: ((m[0] ^ (s % parts)) * chunks + s // parts, 0, 0),
+    )
     return pl.pallas_call(
-        functools.partial(first_kernel, edge=edge),
+        functools.partial(first_kernel, edge=edge, chunks=chunks, parts=parts),
         grid_spec=pltpu.PrefetchScalarGridSpec(
             num_scalar_prefetch=1,
             grid=(chunks * parts,),
             in_specs=[
-                pl.BlockSpec(
-                    (seqs, LANES, width),
-                    lambda s, m: ((m[0] ^ (s % parts)) * chunks + s // parts, 0, 0),
-                ),
+                own,
+                own,
                 pl.BlockSpec((1, width), lambda s, m: (0, 0)),
                 whole,
                 whole,
                 whole,
             ],
             out_specs=[
+                rows,
                 rows,
                 act,
                 act,
@@ -331,12 +339,13 @@
         ),
         out_shape=[
             shape(num_seqs, LANES, width, dtype=BF),
+            shape(num_seqs, LANES, width, dtype=BF),
             a,
             a,
             a,
             shape(channels, LANES),
         ],
-    )(mine[None], inputs, gain[None, :], *weights)
+    )(at, inputs, cotangent, gain[None, :], *weights)
 
 
 def last_call(dq, dv, ds, spill, tap_rows, normed, weights, pieces, more):
@@ -368,28 +377,31 @@
     return out[:-2], out[-2], out[-1]
 
 
-def place_kernel(blocks_ref, *refs):
+def place_kernel(blocks_ref, *refs, count):
     step = pl.program_id(0)
-    for i, piece_ref in enumerate(refs[:-1]):
+    for i, piece_ref in enumerate(refs[:count]):
 
         @pl.when(step == i)
         def store(piece_ref=piece_ref):
             refs[-1][...] = piece_ref[...]
 
 
-def place_call(blocks, pieces):
+def place_call(blocks, pieces, rows, whole=None):
     count = len(pieces)
     piece = pieces[0].shape
+    old = () if whole is None else (whole,)
     return pl.pallas_call(
-        place_kernel,
+        functools.partial(place_kernel, count=count),
         grid_spec=pltpu.PrefetchScalarGridSpec(
             num_scalar_prefetch=1,
             grid=(count,),
-            in_specs=[pl.BlockSpec(piece, lambda s, b: (0, 0, 0))] * count,
+            in_specs=[pl.BlockSpec(piece, lambda s, b: (0, 0, 0))] * count
+            + [pl.BlockSpec(memory_space=pl.ANY)] * len(old),
             out_specs=pl.BlockSpec(piece, lambda s, b: (b[s], 0, 0)),
         ),
-        out_shape=shape(count * piece[0], *piece[1:]),
-    )(blocks, *pieces)
+        out_shape=shape(rows, *piece[1:]),
+        input_output_aliases={count + 1: 0} if old else {},
+    )(blocks, *pieces, *old)
 
 
 def specs(batch, taps):
@@ -510,11 +522,14 @@
 class Link:
     def __init__(self):
         self.waits = ()
-
-    def swap(self, x, *more):
-        x, *_ = lax.optimization_barrier((x, *self.waits, *more))
+        self.last = ()
+
+    def swap(self, x, *more, free=False):
+        x, *_ = lax.optimization_barrier((x, *self.waits, *(() if free else self.last), *more))
         got = swapped(x, "tp", 2)
-        self.waits = (got,)
+        self.waits = ()
+        self.last = (got,)
+        self.sent = x
         return got
 
 
@@ -555,8 +570,9 @@
         self.steps = total_steps(x, digits)
         self.sends = next(self.steps)
 
-    def run(self, rounds):
+    def run(self, rounds, after=()):
         got = ()
+        self.sends = [(lax.optimization_barrier((x, after))[0], by) for x, by in self.sends]
         for _ in range(rounds * self.rounds // 4):
             got = tuple(swapped(x, "seq", by) for x, by in self.sends)
             try:
@@ -626,9 +642,9 @@
             [lax.dynamic_slice_in_dim(x, at, piece, 0) for at in starts()], axis=0
         )
 
-    def placed(pieces):
-        blocks = [(mine ^ r) * chunks + u for u in range(chunks) for r in range(parts)]
-        return place_call(jnp.stack(blocks), pieces)
+    def placed(pieces, u, whole=None):
+        blocks = jnp.stack([(mine ^ r) * chunks + u for r in range(parts)])
+        return place_call(blocks, pieces, num_seqs, whole)
 
     own_inputs = [
         lax.dynamic_slice_in_dim(inputs, mine * group_seqs + u * piece, piece, 0).astype(F32)
@@ -645,10 +661,9 @@
         return x[u * size : u * size + piece]
 
     link = Link()
-    lengths = groups(lengths)
+    ends = groups(lengths)
     positions = place * block_len + jnp.arange(block_len)
-    valid = (positions[None, :] < lengths[:, None])[:, :, None]
-    d_mlp = jnp.where(valid, groups(cotangent), 0)
+    valid = (positions[None, :] < ends[:, None])[:, :, None]
     fwd_local, fwd_post, bwd_local, bwd_lags, bwd_post = conv_calls(num_seqs, channels, taps)
     rate = state_rate.reshape(channels // 2, LANES)
     coef = state_coef.reshape(channels // 2, LANES)
@@ -663,18 +678,13 @@
         return jnp.exp(-rate * (LANES * count))[:, None, :]
 
     turned = (query_weight.T, key_weight.T, value_weight.T)
-    normed, queries, keys, values, tail = first_call(
-        mine, inputs, first_gain, turned, edge, chunks, parts
+    at = jnp.concatenate([jnp.stack([mine, place]), lengths])
+    normed, d_mlp, queries, keys, values, tail = first_call(
+        at, inputs, cotangent, first_gain, turned, edge, chunks, parts
     )
     tail = passed_along(tail, "seq", 1)
     conv, mixed, own = fwd_local(keys, values, tail, tap_rows, rate, kern)
-    def mask_fill(got, step):
-        nonlocal d_mlp
-        if step == 1:
-            got, d_mlp = lax.optimization_barrier((got, d_mlp))
-        return got
-
-    before = carried(own, block_decay, 1, mask_fill)
+    before = carried(own, block_decay, 1)
     state_out, gated_out = fwd_post(conv, before, coef, rate, mixed, queries, skip)
 
     sums = []
@@ -704,34 +714,32 @@
         residuals.append(residual)
         units.append(unit)
         side = swapped(unit[0], "tp", 1)
-        far = link.swap(unit[0])
+        far = link.swap(unit[0], free=u > 0)
         near_fed = feed(scaled(unit[0], side), nears(d_mlp, u))
-        if u + 1 < chunks:
-            link.waits += tuple(near_fed)
-        else:
-            far, near_fed, fed = lax.optimization_barrier((far, near_fed, fed))
+        far, near_fed, fed = lax.optimization_barrier((far, near_fed, fed))
         second_far = scaled(far, swapped(far, "tp", 1))
         far_fed = feed(second_far, fars(d_mlp, u))
         seconds += [scaled(unit[0], side), second_far]
         fed += [near_fed, far_fed]
+    hiddens = [x[0] for x in fed]
+    d_ups = [x[1] for x in fed]
     sums = []
     for u in range(chunks):
-        far = link.swap(far_total(fed[2 * u + 1][2]))
+        far = link.swap(far_total(fed[2 * u + 1][2]), *((early,) if u else ()))
+        if u == 0:
+            late_mlp, late_up, _ = lax.optimization_barrier((d_mlp, d_ups, link.sent))
+            grad_down = product("btf,btd->fd", jnp.concatenate(hiddens, axis=0), late_mlp)
+            grad_up = product(
+                "btd,btf->df", jnp.concatenate(seconds, axis=0), jnp.concatenate(late_up, axis=0)
+            )
+            early = jnp.concatenate([grad_up, grad_down], axis=0)
         sums.append((far_total(fed[2 * u][2]), far))
-    hiddens = [x[0] for x in fed]
-    d_ups = [x[1] for x in fed]
-    hidden = jnp.concatenate(hiddens, axis=0)
-    d_up = jnp.concatenate(d_ups, axis=0)
-    second = jnp.concatenate(seconds, axis=0)
-    grad_down = product("btf,btd->fd", hidden, d_mlp)
-    grad_up = product("btd,btf->df", second, d_up)
-    link.waits += (grad_up, grad_down)
-    early = lax.psum_scatter(
-        jnp.concatenate([grad_up, grad_down], axis=0), "seq", scatter_dimension=0, tiled=True
-    )
+    early = lax.psum_scatter(early, "seq", scatter_dimension=0, tiled=True)
+    lowered = [product("btf,fd->btd", hidden, down_weight) for hidden in hiddens]
     grad_second = 0.0
     d_norms = []
-    groups_back = []
+    lows = []
+    gated = []
     for u in range(chunks):
         d_second = sums[u][0] + sums[u][1]
         unit, inverse = units[u]
@@ -739,66 +747,62 @@
         grad_second = grad_second + jnp.sum(d_second * unit, axis=(0, 1))
         side = swapped(d_norm, "tp", 1)
         far = link.swap(d_norm)
-        groups_back += [d_norm, side, far, swapped(far, "tp", 1)]
+        if u + 1 == chunks:
+            far, lowered, lows, gated = lax.optimization_barrier((far, lowered, lows, gated))
+        rows = jnp.concatenate([d_norm, side, far, swapped(far, "tp", 1)], axis=0)
+        low = (rows + d_mlp[u * size : (u + 1) * size].astype(F32)).astype(BF)
+        lows.append(low)
+        gated.append(product("btd,cd->bct", low, project_weight))
         d_norms.append(d_norm)
-    lowered = [
-        (
-            product("btf,fd->btd", hiddens[2 * u], down_weight),
-            product("btf,fd->btd", hiddens[2 * u + 1], down_weight),
-        )
-        for u in range(chunks)
-    ]
-    groups_back, lowered = lax.optimization_barrier((groups_back, lowered))
-    d_resid_low = (jnp.concatenate(groups_back, axis=0) + d_mlp.astype(F32)).astype(BF)
-    d_gated = product("btd,cd->bct", d_resid_low, project_weight)
+    d_resid_low = jnp.concatenate(lows, axis=0)
+    d_gated = jnp.concatenate(gated, axis=0)
     d_queries, d_state, d_part, back = bwd_local(
         d_gated, queries, state_out, skip, rate, kern[:, ::-1]
     )
     outs = []
-    out_groups = []
-
-    def lower(u):
-        far = link.swap(far_total(lowered[u][1]))
-        outs.append(far_total(lowered[u][0]) + far)
+
+    def lower(u, after):
+        far = link.swap(far_total(lowered[2 * u + 1]), after)
+        outs.append(far_total(lowered[2 * u]) + far)
         return far
 
-    def give_out(u):
+    block_out = None
+
+    def give_out(u, after):
+        nonlocal block_out
         out = jnp.where(owns(valid, u), residuals[u] + outs[u], 0.0)
         side = swapped(out, "tp", 1)
-        far = link.swap(out)
-        out_groups.extend([out, side, far, swapped(far, "tp", 1)])
+        far = link.swap(out, after)
+        block_out = placed([out, side, far, swapped(far, "tp", 1)], u, block_out)
         return far
 
     grad_project = product("bct,btd->cd", gated_out, d_resid_low)
     grad_query = product("bct,btd->cd", d_queries, normed)
     lagged = bwd_lags(d_state, mixed, rate, 0, 1)
+    flying = lower(0, back)
 
     def back_fill(got, step):
-        nonlocal lagged, grad_project, grad_query, early
-        if step == 0:
-            got, _ = lax.optimization_barrier((got, lower(0)))
-        elif step == 1:
-            got, grad_project, grad_query, early = lax.optimization_barrier(
-                (got, grad_project, grad_query, early)
-            )
+        nonlocal lagged, grad_project, grad_query, early, flying
+        if step == 1:
+            got, grad_project, _ = lax.optimization_barrier((got, grad_project, flying))
+            flying = lower(1, got)
         elif step == 2:
-            got, lagged, _ = lax.optimization_barrier((got, lagged, lower(1)))
-        else:
-            got, _ = lax.optimization_barrier((got, give_out(0)))
+            got, lagged, early, _ = lax.optimization_barrier((got, lagged, early, flying))
+            flying = give_out(0, got)
+        elif step == 3:
+            got, grad_query, _ = lax.optimization_barrier((got, grad_query, flying))
         return got
 
     after = carried(back, block_decay, -1, back_fill)
     early = lax.all_gather(early, "seq", axis=0, tiled=True)
-    give_out(1)
-    block_out = placed(out_groups)
+    flying = give_out(1, after)
     others = Total(jnp.concatenate([grad_project, grad_query], axis=0))
-    first_got = others.run(1)
     d_values, d_shifted, head, grad_taps = bwd_post(
         d_part, after, coef, rate, keys, values, tail, tap_rows
     )
     spill = passed_along(head, "seq", -1)
-    spill, block_out, _ = lax.optimization_barrier((spill, block_out, first_got))
-    link.waits += others.run(1)
+    spill, _ = lax.optimization_barrier((spill, flying))
+    others.run(1, spill)
     pieces, main, grad_first = last_call(
         d_queries, d_values, d_shifted, spill, tap_rows, normed, turned, chunks * parts, 64
     )
@@ -827,9 +831,9 @@
     for u in range(chunks):
         at = parts * u
         far = link.swap(far_total((pieces[at + 2], pieces[at + 3])))
-        link.waits += mains.run(1) + others.run(1)
+        link.waits += others.run(1, link.sent) + mains.run(1, link.sent) + ((block_out,) if u else ())
         sums.append((far_total((pieces[at], pieces[at + 1])), far))
-    out_groups = []
+    grad_inputs = None
     for u in range(chunks):
         d_first = sums[u][0] + sums[u][1]
         unit, inverse = centered(own_inputs[u])
@@ -837,9 +841,12 @@
         d_rows = d_rows + norm_back(unit, inverse, d_first, first_gain)
         side = swapped(d_rows, "tp", 1)
         far = link.swap(d_rows)
-        link.waits += mains.run(1) + (() if u else (grad_up, grad_down))
-        out_groups += [d_rows, side, far, swapped(far, "tp", 1)]
-    grad_inputs = placed(out_groups)
+        link.waits += mains.run(1, link.sent)
+        if u == 0:
+            link.waits += (*others.run(1, link.sent), grad_up, grad_down)
+        if u:
+            far, grad_inputs = lax.optimization_barrier((far, grad_inputs))
+        grad_inputs = placed([d_rows, side, far, swapped(far, "tp", 1)], u, grad_inputs)
     main = mains.done
     at = 2 * channels
     grad_key, grad_value = main[:channels].T, main[channels:at].T

time: 602 us -> 568 us (0.944)
  starting transfers between devices: 94.7 us -> 72.4 us
  local copies, waits for them, and re-layouts: 59.8 us -> 45.8 us
    ppermute x70, starting transfers between devices: 76.4 us -> 53.8 us  [swapped(): lax.ppermute(x, axis, [(i, i ^ bit) for i in range(lax.axis_size(axis))])]
    ppermute x70, waiting for transfers between devices: 222 us -> 201 us  [swapped(): lax.ppermute(x, axis, [(i, i ^ bit) for i in range(lax.axis_size(axis))])]
    ppermute x6, waiting for transfers between devices: 15.3 us -> 36.9 us  [passed_along(): return lax.ppermute(x, axis, pairs)]
    unnamed x214 -> x166, local copies, waits for them, and re-layouts: 25.8 us -> 11.8 us
    pallas_call x3 -> x5, Pallas kernels: 25.2 us -> 31.3 us  [the longest x4 19 us: place_call(): pl.pallas_call(functools.partial(place_kernel, count=count), grid_spec=pl...]
    dot_general x25 -> x26, matrix products: 37 us -> 38 us  [product(): return jnp.einsum(form, left, right, preferred_element_type=F32)]
  transfers between devices with their start and end apart: 78 -> 78, of which waited for: 29 -> 32; matrix products, arithmetic and copies ran while one was open for 21% -> 19% of each run, Pallas kernels for 9% -> 11%
where the time goes in v3:
time: 568 us; the launch traced here: 562 us
  waiting for transfers between devices  238 us (42%)
  Pallas kernels  97 us (17%)
  starting transfers between devices  72.4 us (13%)
  other arithmetic  55 us (10%)
  local copies, waits for them, and re-layouts  45.8 us (8%)
  matrix products  38 us (7%)
  between operations  15.7 us (3%)
    ppermute x70, waiting for transfers between devices, swapped(): lax.ppermute(x, axis, [(i, i ^ bit) for i in range(lax.axis_size(axis))])  201 us
    ppermute x70, starting transfers between devices, swapped(): lax.ppermute(x, axis, [(i, i ^ bit) for i in range(lax.axis_size(axis))])  53.8 us
    pallas_call x5, Pallas kernels, call(): pl.pallas_call(kernel, grid=(channels // GROUP,), in_specs=ins, out_specs...  51 us
    dot_general x26, matrix products, product(): return jnp.einsum(form, left, right, preferred_element_type=F32)  38 us
    ppermute x6, waiting for transfers between devices, passed_along(): return lax.ppermute(x, axis, pairs)  36.9 us
    pallas_call x4, Pallas kernels, place_call(): pl.pallas_call(functools.partial(place_kernel, count=count), grid_spec=pl...  19 us
    ppermute x6, starting transfers between devices, passed_along(): return lax.ppermute(x, axis, pairs)  18.1 us
    pallas_call x1, Pallas kernels, last_call(): pl.pallas_call(last_kernel, grid=(pieces,), in_specs=[act, act, act, pl.B...  14.7 us
  transfers between devices with their start and end apart: 78, of which 32 were waited for; matrix products, arithmetic and copies ran while one was open for 19% of the time, Pallas kernels for 11%

profile of v3, /device:TPU:0, one launch (start us, length us, event | category | flops | bytes accessed | tf_op | source)
XLA Modules:
  0.0 561.7 jit_solution(5277056608027600909)
XLA Ops:
  9.8 12.4 %shard_map.254 = (bf16[16,128,768]{2,1,0:T(8,128)(2,1)}, bf16[16,128,768]{2,1,0:T(8,128)(2,1)}, f32[16,192,128]{2,1,0:T(8,128)}, f32[16,192,128]{2,1,0:T(8,128)}...) custom-call(s32[18]{0:T(128)} %pad_add_fusion.1.at_ref, bf16[16,128,768]{2,1,0:T(8,128)(2,1)} %x_ref.1, ...), custom_call_target="tpu_custom_call" | custom-call | tf_op jit(solution)/shard_map/pallas_call | solution.py:318
  22.2 4.9 collective-permute-start
  27.4 4.6 multiply_reduce_fusion.kern_ref
  34.1 12.9 %shard_map.255 = (f32[16,192,128]{2,1,0:T(8,128)}, f32[16,192,128]{2,1,0:T(8,128)}, f32[96,16,128]{2,1,0:T(8,128)}) custom-call(f32[16,192,128]{2,1,0:T(8,128)} %get-tuple-element.114.k_ref, f32[16,192,128]{2,1,0:T(8,128)} %get-tuple-element.115.v_ref, f32[192,128]{1,0:T(8,128)} %copy-done.54, f32[192,4]{1,0:T(8,128)} %bitcast.116, ...), custom_call_target="tpu_custom_call" | custom-call | tf_op jit(solution)/shard_map/pallas_call | solution.py:423
  50.5 8.5 %collective-permute-done.1 = f32[48,16,128]{2,1,0:T(8,128)S(1)} collective-permute-done((f32[48,16,128]{2,1,0:T(8,128)S(1)}, f32[48,16,128]{2,1,0:T(8,128)S(1)}, u32[]{:S(2)}, u32[]{:S(2)}) %collective-permute-start.1) | collective-permute-done | bytes 393248 | tf_op jit(solution)/shard_map/ppermute | solution.py:486
  59.1 3.5 collective-permute-start.2
  62.6 7.2 %collective-permute-done.2 = f32[48,16,128]{2,1,0:T(8,128)S(1)} collective-permute-done((f32[48,16,128]{2,1,0:T(8,128)S(1)}, f32[48,16,128]{2,1,0:T(8,128)S(1)}, u32[]{:S(2)}, u32[]{:S(2)}) %collective-permute-start.2) | collective-permute-done | bytes 393248 | tf_op jit(solution)/shard_map/ppermute | solution.py:482
  69.9 5.4 collective-permute-start.3
  75.3 6.3 %collective-permute-done.3 = f32[48,16,128]{2,1,0:T(8,128)S(1)} collective-permute-done((f32[48,16,128]{2,1,0:T(8,128)S(1)}, f32[48,16,128]{2,1,0:T(8,128)S(1)}, u32[]{:S(2)}, u32[]{:S(2)}) %collective-permute-start.3) | collective-permute-done | bytes 393248 | tf_op jit(solution)/shard_map/ppermute | solution.py:482
  84.9 5.0 collective-permute-done.4
  92.1 7.2 %shard_map.256 = (f32[16,192,128]{2,1,0:T(8,128)}, bf16[16,192,128]{2,1,0:T(8,128)(2,1)}) custom-call(f32[16,192,128]{2,1,0:T(8,128)} %get-tuple-element.117.y_ref, f32[96,16,128]{2,1,0:T(8,128)} %pad_maximum_fusion.2.hin_ref, f32[96,128]{1,0:T(8,128)} %reshape.190.coef_ref, f32[96,128]{1,0:T(8,128)} %reshape.189.rate_ref, ...), custom_call_target="tpu_custom_call" | custom-call | tf_op jit(solution)/shard_map/pallas_call | solution.py:423
  109.3 13.7 %collective-permute-done.8 = f32[2,128,768]{2,1,0:T(8,128)} collective-permute-done((f32[2,128,768]{2,1,0:T(8,128)S(1)}, f32[2,128,768]{2,1,0:T(8,128)}, u32[]{:S(2)}, u32[]{:S(2)}) %collective-permute-start.8) | collective-permute-done | bytes 786464 | tf_op jit(solution)/shard_map/ppermute | solution.py:486
  127.2 14.9 %collective-permute-done.9 = f32[2,128,768]{2,1,0:T(8,128)} collective-permute-done((f32[2,128,768]{2,1,0:T(8,128)}, f32[2,128,768]{2,1,0:T(8,128)}, u32[]{:S(2)}, u32[]{:S(2)}) %collective-permute-start.9) | collective-permute-done | bytes 786464 | tf_op jit(solution)/shard_map/ppermute | solution.py:486
  142.1 3.7 fusion.116
  152.7 2.0 fusion.92
  154.7 11.5 %collective-permute-done.13 = f32[2,128,768]{2,1,0:T(8,128)S(1)} collective-permute-done((f32[2,128,768]{2,1,0:T(8,128)S(1)}, f32[2,128,768]{2,1,0:T(8,128)S(1)}, u32[]{:S(2)}, u32[]{:S(2)}) %collective-permute-start.13) | collective-permute-done | bytes 786464 | tf_op jit(solution)/shard_map/ppermute | solution.py:486
  171.4 2.0 fusion.96
  177.0 9.2 %collective-permute-done.10 = f32[2,128,768]{2,1,0:T(8,128)S(1)} collective-permute-done((f32[2,128,768]{2,1,0:T(8,128)S(1)}, f32[2,128,768]{2,1,0:T(8,128)S(1)}, u32[]{:S(2)}, u32[]{:S(2)}) %collective-permute-start.10) | collective-permute-done | bytes 786464 | tf_op jit(solution)/shard_map/ppermute | solution.py:486
  192.3 2.8 fusion.32
  195.2 2.8 fusion.29
  198.1 2.5 pad_maximum_fusion
  201.1 2.1 fusion.84
  205.7 17.6 %collective-permute-done.20 = f32[2,128,768]{2,1,0:T(8,128)S(1)} collective-permute-done((f32[2,128,768]{2,1,0:T(8,128)S(1)}, f32[2,128,768]{2,1,0:T(8,128)S(1)}, u32[]{:S(2)}, u32[]{:S(2)}) %collective-permute-start.20) | collective-permute-done | bytes 786464 | tf_op jit(solution)/shard_map/ppermute | solution.py:486
  224.5 2.0 fusion.78
  226.9 15.5 %collective-permute-done.21 = f32[2,128,768]{2,1,0:T(8,128)S(1)} collective-permute-done((f32[2,128,768]{2,1,0:T(8,128)S(1)}, f32[2,128,768]{2,1,0:T(8,128)S(1)}, u32[]{:S(2)}, u32[]{:S(2)}) %collective-permute-start.21) | collective-permute-done | bytes 786464 | tf_op jit(solution)/shard_map/ppermute | solution.py:486
  244.2 2.0 fusion.76
  246.2 2.0 fusion.74
  248.2 13.3 %collective-permute-done.23 = f32[2,128,768]{2,1,0:T(8,128)S(1)} collective-permute-done((f32[2,128,768]{2,1,0:T(8,128)S(1)}, f32[2,128,768]{2,1,0:T(8,128)S(1)}, u32[]{:S(2)}, u32[]{:S(2)}) %collective-permute-start.23) | collective-permute-done | bytes 786464 | tf_op jit(solution)/shard_map/ppermute | solution.py:486
  268.2 14.8 %collective-permute-done.24 = f32[2,128,768]{2,1,0:T(8,128)} collective-permute-done((f32[2,128,768]{2,1,0:T(8,128)}, f32[2,128,768]{2,1,0:T(8,128)}, u32[]{:S(2)}, u32[]{:S(2)}) %collective-permute-start.24) | collective-permute-done | bytes 786464 | tf_op jit(solution)/shard_map/ppermute | solution.py:486
  283.9 2.2 split.91
  287.6 2.7 fusion.24
  292.3 8.2 %shard_map.257 = (bf16[16,192,128]{2,1,0:T(8,128)(2,1)}, f32[16,192,128]{2,1,0:T(8,128)}, f32[16,192,128]{2,1,0:T(8,128)}, f32[96,16,128]{2,1,0:T(8,128)}) custom-call(f32[16,192,128]{2,1,0:T(8,128)} %pad_maximum_fusion.1.dg_ref, f32[16,192,128]{2,1,0:T(8,128)} %get-tuple-element.120.q_ref, f32[16,192,128]{2,1,0:T(8,128)} %get-tuple-element.153.state_ref, ...), custom_call_target="tpu_custom_call" | custom-call | tf_op jit(solution)/shard_map/pallas_call | solution.py:423
  304.1 2.2 split.95
  309.3 4.8 collective-permute-done.33
  315.8 2.1 slice_add_fusion.6
  319.6 8.4 %collective-permute-done.32 = f32[2,128,768]{2,1,0:T(8,128)S(1)} collective-permute-done((f32[2,128,768]{2,1,0:T(8,128)S(1)}, f32[2,128,768]{2,1,0:T(8,128)S(1)}, u32[]{:S(2)}, u32[]{:S(2)}) %collective-permute-start.32) | collective-permute-done | bytes 786464 | tf_op jit(solution)/shard_map/ppermute | solution.py:486
  327.9 10.2 %collective-permute-done.34 = f32[48,16,128]{2,1,0:T(8,128)S(1)} collective-permute-done((f32[48,16,128]{2,1,0:T(8,128)S(1)}, f32[48,16,128]{2,1,0:T(8,128)S(1)}, u32[]{:S(2)}, u32[]{:S(2)}) %collective-permute-start.34) | collective-permute-done | bytes 393248 | tf_op jit(solution)/shard_map/ppermute | solution.py:482
  343.0 13.1 %shard_map.258 = (f32[96,16,128]{2,1,0:T(8,128)}, f32[96,16,128]{2,1,0:T(8,128)}, f32[192,128]{1,0:T(8,128)}, f32[96,128]{1,0:T(8,128)}, f32[96,128]{1,0:T(8,128)}) custom-call(f32[16,192,128]{2,1,0:T(8,128)} %get-tuple-element.160.d_ref, f32[16,192,128]{2,1,0:T(8,128)} %get-tuple-element.119.mixed_ref, f32[96,128]{1,0:T(8,128)} %reshape.189.rate_ref), custom_call_target="tpu_custom_call" | custom-call | tf_op jit(solution)/shard_map/pallas_call | solution.py:423
  356.0 5.9 %collective-permute-done.38 = f32[48,16,128]{2,1,0:T(8,128)} collective-permute-done((f32[48,16,128]{2,1,0:T(8,128)}, f32[48,16,128]{2,1,0:T(8,128)}, u32[]{:S(2)}, u32[]{:S(2)}) %collective-permute-start.38) | collective-permute-done | bytes 393248 | tf_op jit(solution)/shard_map/ppermute | solution.py:482
  368.3 2.6 add_select_fusion.1.refs_0_
  370.9 10.9 %collective-permute-done.40 = f32[48,16,128]{2,1,0:T(8,128)S(1)} collective-permute-done((f32[48,16,128]{2,1,0:T(8,128)S(1)}, f32[48,16,128]{2,1,0:T(8,128)S(1)}, u32[]{:S(2)}, u32[]{:S(2)}) %collective-permute-start.40) | collective-permute-done | bytes 393248 | tf_op jit(solution)/shard_map/ppermute | solution.py:486
  388.5 9.8 %shard_map.261 = (bf16[16,192,128]{2,1,0:T(8,128)(2,1)}, f32[16,192,128]{2,1,0:T(8,128)}, f32[192,128]{1,0:T(8,128)}, f32[192,128]{1,0:T(8,128)}) custom-call(f32[16,192,128]{2,1,0:T(8,128)} %get-tuple-element.172.dx_ref, f32[96,16,128]{2,1,0:T(8,128)} %get-tuple-element.294.gin_ref, f32[96,128]{1,0:T(8,128)} %reshape.190.coef_ref, ...), custom_call_target="tpu_custom_call" | custom-call | tf_op jit(solution)/shard_map/pallas_call | solution.py:423
  400.5 7.2 %collective-permute-done.45.spill_ref = f32[192,128]{1,0:T(8,128)S(1)} collective-permute-done((f32[192,128]{1,0:T(8,128)}, f32[192,128]{1,0:T(8,128)S(1)}, u32[]{:S(2)}, u32[]{:S(2)}) %collective-permute-start.45) | collective-permute-done | bytes 98336 | tf_op jit(solution)/shard_map/ppermute | solution.py:482
  408.4 14.7 %shard_map.262 = (f32[2,128,768]{2,1,0:T(8,128)}, f32[2,128,768]{2,1,0:T(8,128)}, f32[2,128,768]{2,1,0:T(8,128)}, f32[2,128,768]{2,1,0:T(8,128)}, f32[2,128,768]...) custom-call(bf16[16,192,128]{2,1,0:T(8,128)(2,1)} %get-tuple-element, ...), custom_call_target="tpu_custom_call" | custom-call | tf_op jit(solution)/shard_map/pallas_call | solution.py:357
  424.4 3.4 collective-permute-start.48
  429.4 2.3 collective-permute-done.51
  431.9 9.7 %collective-permute-done.48 = f32[192,768]{1,0:T(8,128)} collective-permute-done((f32[192,768]{1,0:T(8,128)}, f32[192,768]{1,0:T(8,128)}, u32[]{:S(2)}, u32[]{:S(2)}) %collective-permute-start.48) | collective-permute-done | bytes 589856 | tf_op jit(solution)/shard_map/ppermute | solution.py:486
  442.9 2.0 constant_dynamic-slice_fusion.3
  453.1 2.7 collective-permute-start.54
  455.8 4.8 shard_map.259.refs_4_
  461.8 4.7 shard_map.260
  471.4 1.9 collective-permute-start.63
  473.4 2.4 collective-permute-start.65
  475.8 2.2 fusion.112
  479.6 2.1 collective-permute-start.60
  481.7 7.6 %collective-permute-done.57 = f32[2,128,768]{2,1,0:T(8,128)S(1)} collective-permute-done((f32[2,128,768]{2,1,0:T(8,128)S(1)}, f32[2,128,768]{2,1,0:T(8,128)S(1)}, u32[]{:S(2)}, u32[]{:S(2)}) %collective-permute-start.57) | collective-permute-done | bytes 786464 | tf_op jit(solution)/shard_map/ppermute | solution.py:486
  492.3 3.0 fusion.115
  495.3 7.8 %collective-permute-done.60 = f32[56,768]{1,0:T(8,128)S(1)} collective-permute-done((f32[56,768]{1,0:T(8,128)S(1)}, f32[56,768]{1,0:T(8,128)S(1)}, u32[]{:S(2)}, u32[]{:S(2)}) %collective-permute-start.60) | collective-permute-done | bytes 172064 | tf_op jit(solution)/shard_map/ppermute | solution.py:486
  506.9 3.5 collective-permute-start.68
  510.5 4.9 fusion.144
  515.3 7.5 %collective-permute-done.70.refs_2_ = f32[2,128,768]{2,1,0:T(8,128)} collective-permute-done((f32[2,128,768]{2,1,0:T(8,128)}, f32[2,128,768]{2,1,0:T(8,128)}, u32[]{:S(2)}, u32[]{:S(2)}) %collective-permute-start.70) | collective-permute-done | bytes 786464 | tf_op jit(solution)/shard_map/ppermute | solution.py:486
  528.2 4.7 shard_map.263.refs_4_
  532.9 10.2 %collective-permute-done.71.refs_2_ = f32[2,128,768]{2,1,0:T(8,128)} collective-permute-done((f32[2,128,768]{2,1,0:T(8,128)S(1)}, f32[2,128,768]{2,1,0:T(8,128)}, u32[]{:S(2)}, u32[]{:S(2)}) %collective-permute-start.71) | collective-permute-done | bytes 786464 | tf_op jit(solution)/shard_map/ppermute | solution.py:486
  549.8 4.8 shard_map.264
  (438 shorter events, 136.7 us)
Async XLA Ops:
  7.2 354.7 %reduce-scatter.2.cloned.1.call-start = ((), (), s32[]{:S(2)}) async-start(), calls=%async_computation.1 | async-start | bytes 5308416 | tf_op jit(solution)/shard_map/reduce_scatter | solution.py:737
  22.2 11.3 %collective-permute-start = (f32[192,128]{1,0:T(8,128)}, f32[192,128]{1,0:T(8,128)S(1)}, u32[]{:S(2)}, u32[]{:S(2)}) collective-permute-start(f32[192,128]{1,0:T(8,128)} %get-tuple-element.116), channel_id=1, source_target_pairs={{0,4},{4,8},{8,12},{12,16},{16,20},{20,24},{24,28},{1,5},{5,9},{9,... | collective-permute-start | bytes 294920 | tf_op jit(solution)/shard_map/ppermute | solution.py:482
  48.3 10.7 %collective-permute-start.1 = (f32[48,16,128]{2,1,0:T(8,128)S(1)}, f32[48,16,128]{2,1,0:T(8,128)S(1)}, u32[]{:S(2)}, u32[]{:S(2)}) collective-permute-start(f32[48,16,128]{2,1,0:T(8,128)S(1)} %slice_select_fusion.2), channel_id=1, source_target_pairs={{0,4},{4,0},{8,12},{12,8},{16,20},{20,16},{24,28},{28,24},{1,5},{5... | collective-permute-start | bytes 1179656 | tf_op jit(solution)/shard_map/ppermute | solution.py:486
  59.1 10.7 %collective-permute-start.2 = (f32[48,16,128]{2,1,0:T(8,128)S(1)}, f32[48,16,128]{2,1,0:T(8,128)S(1)}, u32[]{:S(2)}, u32[]{:S(2)}) collective-permute-start(f32[48,16,128]{2,1,0:T(8,128)S(1)} %get-tuple-element.278), channel_id=1, source_target_pairs={{0,8},{4,12},{8,16},{12,20},{16,24},{20,28},{1,9},{5,13},{9,17},{1... | collective-permute-start | bytes 1179656 | tf_op jit(solution)/shard_map/ppermute | solution.py:482
  69.9 11.8 %collective-permute-start.3 = (f32[48,16,128]{2,1,0:T(8,128)S(1)}, f32[48,16,128]{2,1,0:T(8,128)S(1)}, u32[]{:S(2)}, u32[]{:S(2)}) collective-permute-start(f32[48,16,128]{2,1,0:T(8,128)S(1)} %multiply_add_fusion.5), channel_id=1, source_target_pairs={{0,16},{4,20},{8,24},{12,28},{1,17},{5,21},{9,25},{13,29},{2,18},{... | collective-permute-start | bytes 1179656 | tf_op jit(solution)/shard_map/ppermute | solution.py:482
  81.8 8.1 %collective-permute-start.4 = (f32[48,16,128]{2,1,0:T(8,128)S(1)}, f32[48,16,128]{2,1,0:T(8,128)}, u32[]{:S(2)}, u32[]{:S(2)}) collective-permute-start(f32[48,16,128]{2,1,0:T(8,128)S(1)} %fusion.123), channel_id=1, source_target_pairs={{0,4},{4,0},{8,12},{12,8},{16,20},{20,16},{24,28},{28,24},{1,5},{5... | collective-permute-start | bytes 1179656 | tf_op jit(solution)/shard_map/ppermute | solution.py:486
  101.4 7.0 %collective-permute-start.6 = (f32[2,128,768]{2,1,0:T(8,128)S(1)}, f32[2,128,768]{2,1,0:T(8,128)S(1)}, u32[]{:S(2)}, u32[]{:S(2)}) collective-permute-start(f32[2,128,768]{2,1,0:T(8,128)S(1)} %split.99), channel_id=1, source_target_pairs={{0,1},{1,0},{2,3},{3,2},{4,5},{5,4},{6,7},{7,6},{8,9},{9,8},{10,11... | collective-permute-start | bytes 2359304 | tf_op jit(solution)/shard_map/ppermute | solution.py:486
  103.2 19.8 %collective-permute-start.8 = (f32[2,128,768]{2,1,0:T(8,128)S(1)}, f32[2,128,768]{2,1,0:T(8,128)}, u32[]{:S(2)}, u32[]{:S(2)}) collective-permute-start(f32[2,128,768]{2,1,0:T(8,128)S(1)} %slice_add_fusion.2), channel_id=1, source_target_pairs={{0,2},{1,3},{2,0},{3,1},{4,6},{5,7},{6,4},{7,5},{8,10},{9,11},{10,... | collective-permute-start | bytes 2359304 | tf_op jit(solution)/shard_map/ppermute | solution.py:486
  106.0 19.3 %collective-permute-start.5 = (f32[2,128,768]{2,1,0:T(8,128)}, f32[2,128,768]{2,1,0:T(8,128)S(1)}, u32[]{:S(2)}, u32[]{:S(2)}) collective-permute-start(f32[2,128,768]{2,1,0:T(8,128)} %split.97), channel_id=1, source_target_pairs={{0,1},{1,0},{2,3},{3,2},{4,5},{5,4},{6,7},{7,6},{8,9},{9,8},{10,11... | collective-permute-start | bytes 2359304 | tf_op jit(solution)/shard_map/ppermute | solution.py:486
  107.8 17.5 %collective-permute-start.12 = (f32[2,128,768]{2,1,0:T(8,128)}, f32[2,128,768]{2,1,0:T(8,128)S(1)}, u32[]{:S(2)}, u32[]{:S(2)}) collective-permute-start(f32[2,128,768]{2,1,0:T(8,128)} %split.103), channel_id=1, source_target_pairs={{0,1},{1,0},{2,3},{3,2},{4,5},{5,4},{6,7},{7,6},{8,9},{9,8},{10,11... | collective-permute-start | bytes 2359304 | tf_op jit(solution)/shard_map/ppermute | solution.py:486
  123.0 19.1 %collective-permute-start.9 = (f32[2,128,768]{2,1,0:T(8,128)}, f32[2,128,768]{2,1,0:T(8,128)}, u32[]{:S(2)}, u32[]{:S(2)}) collective-permute-start(f32[2,128,768]{2,1,0:T(8,128)} %slice_add_fusion.3), channel_id=1, source_target_pairs={{0,2},{1,3},{2,0},{3,1},{4,6},{5,7},{6,4},{7,5},{8,10},{9,11},{10,... | collective-permute-start | bytes 2359304 | tf_op jit(solution)/shard_map/ppermute | solution.py:486
  146.3 20.0 %collective-permute-start.13 = (f32[2,128,768]{2,1,0:T(8,128)S(1)}, f32[2,128,768]{2,1,0:T(8,128)S(1)}, u32[]{:S(2)}, u32[]{:S(2)}) collective-permute-start(f32[2,128,768]{2,1,0:T(8,128)S(1)} %subtract_multiply_fusion.2), channel_id=1, source_target_pairs={{0,2},{1,3},{2,0},{3,1},{4,6},{5,7},{6,4},{7,5},{8,10},{9,11},{10,... | collective-permute-start | bytes 2359304 | tf_op jit(solution)/shard_map/ppermute | solution.py:486
  147.9 19.5 %collective-permute-start.11 = (f32[2,128,768]{2,1,0:T(8,128)S(1)}, f32[2,128,768]{2,1,0:T(8,128)S(1)}, u32[]{:S(2)}, u32[]{:S(2)}) collective-permute-start(f32[2,128,768]{2,1,0:T(8,128)S(1)} %subtract_multiply_fusion.3), channel_id=1, source_target_pairs={{0,1},{1,0},{2,3},{3,2},{4,5},{5,4},{6,7},{7,6},{8,9},{9,8},{10,11... | collective-permute-start | bytes 2359304 | tf_op jit(solution)/shard_map/ppermute | solution.py:486
  166.2 20.0 %collective-permute-start.10 = (f32[2,128,768]{2,1,0:T(8,128)S(1)}, f32[2,128,768]{2,1,0:T(8,128)S(1)}, u32[]{:S(2)}, u32[]{:S(2)}) collective-permute-start(f32[2,128,768]{2,1,0:T(8,128)S(1)} %subtract_multiply_fusion.3), channel_id=1, source_target_pairs={{0,2},{1,3},{2,0},{3,1},{4,6},{5,7},{6,4},{7,5},{8,10},{9,11},{10,... | collective-permute-start | bytes 2359304 | tf_op jit(solution)/shard_map/ppermute | solution.py:486
  200.6 309.9 %all-gather.2.cloned.1.call-start = ((), (), s32[]{:S(2)}) async-start(), calls=%async_computation.2 | async-start | bytes 5308416 | tf_op jit(solution)/shard_map/all_gather | solution.py:797
  203.5 19.8 %collective-permute-start.20 = (f32[2,128,768]{2,1,0:T(8,128)S(1)}, f32[2,128,768]{2,1,0:T(8,128)S(1)}, u32[]{:S(2)}, u32[]{:S(2)}) collective-permute-start(f32[2,128,768]{2,1,0:T(8,128)S(1)} %copy-done.49), channel_id=1, source_target_pairs={{0,2},{1,3},{2,0},{3,1},{4,6},{5,7},{6,4},{7,5},{8,10},{9,11},{10,... | collective-permute-start | bytes 2359304 | tf_op jit(solution)/shard_map/ppermute | solution.py:486
  204.7 21.7 %collective-permute-start.22 = (f32[2,128,768]{2,1,0:T(8,128)S(1)}, f32[2,128,768]{2,1,0:T(8,128)S(1)}, u32[]{:S(2)}, u32[]{:S(2)}) collective-permute-start(f32[2,128,768]{2,1,0:T(8,128)S(1)} %split.87), channel_id=1, source_target_pairs={{0,1},{1,0},{2,3},{3,2},{4,5},{5,4},{6,7},{7,6},{8,9},{9,8},{10,11... | collective-permute-start | bytes 2359304 | tf_op jit(solution)/shard_map/ppermute | solution.py:486
  204.9 22.0 %collective-permute-start.16 = (f32[2,128,768]{2,1,0:T(8,128)S(1)}, f32[2,128,768]{2,1,0:T(8,128)S(1)}, u32[]{:S(2)}, u32[]{:S(2)}) collective-permute-start(f32[2,128,768]{2,1,0:T(8,128)S(1)} %split.81), channel_id=1, source_target_pairs={{0,1},{1,0},{2,3},{3,2},{4,5},{5,4},{6,7},{7,6},{8,9},{9,8},{10,11... | collective-permute-start | bytes 2359304 | tf_op jit(solution)/shard_map/ppermute | solution.py:486
  223.3 19.1 %collective-permute-start.21 = (f32[2,128,768]{2,1,0:T(8,128)S(1)}, f32[2,128,768]{2,1,0:T(8,128)S(1)}, u32[]{:S(2)}, u32[]{:S(2)}) collective-permute-start(f32[2,128,768]{2,1,0:T(8,128)S(1)} %slice_add_fusion), channel_id=1, source_target_pairs={{0,2},{1,3},{2,0},{3,1},{4,6},{5,7},{6,4},{7,5},{8,10},{9,11},{10,... | collective-permute-start | bytes 2359304 | tf_op jit(solution)/shard_map/ppermute | solution.py:486
  243.1 18.4 %collective-permute-start.23 = (f32[2,128,768]{2,1,0:T(8,128)S(1)}, f32[2,128,768]{2,1,0:T(8,128)S(1)}, u32[]{:S(2)}, u32[]{:S(2)}) collective-permute-start(f32[2,128,768]{2,1,0:T(8,128)S(1)} %get-tuple-element.146), channel_id=1, source_target_pairs={{0,2},{1,3},{2,0},{3,1},{4,6},{5,7},{6,4},{7,5},{8,10},{9,11},{10,... | collective-permute-start | bytes 2359304 | tf_op jit(solution)/shard_map/ppermute | solution.py:486
  248.2 17.7 %collective-permute-start.25 = (f32[2,128,768]{2,1,0:T(8,128)S(1)}, f32[2,128,768]{2,1,0:T(8,128)S(1)}, u32[]{:S(2)}, u32[]{:S(2)}) collective-permute-start(f32[2,128,768]{2,1,0:T(8,128)S(1)} %get-tuple-element.146), channel_id=1, source_target_pairs={{0,1},{1,0},{2,3},{3,2},{4,5},{5,4},{6,7},{7,6},{8,9},{9,8},{10,11... | collective-permute-start | bytes 2359304 | tf_op jit(solution)/shard_map/ppermute | solution.py:486
  262.7 20.3 %collective-permute-start.24 = (f32[2,128,768]{2,1,0:T(8,128)}, f32[2,128,768]{2,1,0:T(8,128)}, u32[]{:S(2)}, u32[]{:S(2)}) collective-permute-start(f32[2,128,768]{2,1,0:T(8,128)} %subtract_multiply_fusion.1), channel_id=1, source_target_pairs={{0,2},{1,3},{2,0},{3,1},{4,6},{5,7},{6,4},{7,5},{8,10},{9,11},{10,... | collective-permute-start | bytes 2359304 | tf_op jit(solution)/shard_map/ppermute | solution.py:486
  265.6 22.0 %collective-permute-start.30 = (f32[2,128,768]{2,1,0:T(8,128)}, f32[2,128,768]{2,1,0:T(8,128)}, u32[]{:S(2)}, u32[]{:S(2)}) collective-permute-start(f32[2,128,768]{2,1,0:T(8,128)} %subtract_multiply_fusion.1), channel_id=1, source_target_pairs={{0,1},{1,0},{2,3},{3,2},{4,5},{5,4},{6,7},{7,6},{8,9},{9,8},{10,11... | collective-permute-start | bytes 2359304 | tf_op jit(solution)/shard_map/ppermute | solution.py:486
  286.1 29.7 %collective-permute-start.28 = (f32[2,128,768]{2,1,0:T(8,128)}, f32[2,128,768]{2,1,0:T(8,128)}, u32[]{:S(2)}, u32[]{:S(2)}) collective-permute-start(f32[2,128,768]{2,1,0:T(8,128)} %split.91), channel_id=1, source_target_pairs={{0,1},{1,0},{2,3},{3,2},{4,5},{5,4},{6,7},{7,6},{8,9},{9,8},{10,11... | collective-permute-start | bytes 2359304 | tf_op jit(solution)/shard_map/ppermute | solution.py:486
  287.6 19.0 %collective-permute-start.29 = (f32[2,128,768]{2,1,0:T(8,128)}, f32[2,128,768]{2,1,0:T(8,128)}, u32[]{:S(2)}, u32[]{:S(2)}) collective-permute-start(f32[2,128,768]{2,1,0:T(8,128)} %split.93), channel_id=1, source_target_pairs={{0,1},{1,0},{2,3},{3,2},{4,5},{5,4},{6,7},{7,6},{8,9},{9,8},{10,11... | collective-permute-start | bytes 2359304 | tf_op jit(solution)/shard_map/ppermute | solution.py:486
  302.4 11.7 %collective-permute-start.33 = (f32[48,16,128]{2,1,0:T(8,128)}, f32[48,16,128]{2,1,0:T(8,128)S(1)}, u32[]{:S(2)}, u32[]{:S(2)}) collective-permute-start(f32[48,16,128]{2,1,0:T(8,128)} %slice_select_fusion), channel_id=1, source_target_pairs={{0,4},{4,0},{8,12},{12,8},{16,20},{20,16},{24,28},{28,24},{1,5},{5... | collective-permute-start | bytes 1179656 | tf_op jit(solution)/shard_map/ppermute | solution.py:486
  306.3 55.6 %collective-permute-start.37 = (f32[2,128,768]{2,1,0:T(8,128)}, f32[2,128,768]{2,1,0:T(8,128)}, u32[]{:S(2)}, u32[]{:S(2)}) collective-permute-start(f32[2,128,768]{2,1,0:T(8,128)} %split.95), channel_id=1, source_target_pairs={{0,1},{1,0},{2,3},{3,2},{4,5},{5,4},{6,7},{7,6},{8,9},{9,8},{10,11... | collective-permute-start | bytes 2359304 | tf_op jit(solution)/shard_map/ppermute | solution.py:486
  308.1 19.8 %collective-permute-start.32 = (f32[2,128,768]{2,1,0:T(8,128)S(1)}, f32[2,128,768]{2,1,0:T(8,128)S(1)}, u32[]{:S(2)}, u32[]{:S(2)}) collective-permute-start(f32[2,128,768]{2,1,0:T(8,128)S(1)} %slice_add_fusion.5), channel_id=1, source_target_pairs={{0,2},{1,3},{2,0},{3,1},{4,6},{5,7},{6,4},{7,5},{8,10},{9,11},{10,... | collective-permute-start | bytes 2359304 | tf_op jit(solution)/shard_map/ppermute | solution.py:486
  314.2 23.9 %collective-permute-start.34 = (f32[48,16,128]{2,1,0:T(8,128)S(1)}, f32[48,16,128]{2,1,0:T(8,128)S(1)}, u32[]{:S(2)}, u32[]{:S(2)}) collective-permute-start(f32[48,16,128]{2,1,0:T(8,128)S(1)} %select_add_fusion), channel_id=1, source_target_pairs={{8,0},{12,4},{16,8},{20,12},{24,16},{28,20},{9,1},{13,5},{17,9},{2... | collective-permute-start | bytes 1179656 | tf_op jit(solution)/shard_map/ppermute | solution.py:482
  338.2 23.7 %collective-permute-start.35 = (f32[2,128,768]{2,1,0:T(8,128)}, f32[2,128,768]{2,1,0:T(8,128)}, u32[]{:S(2)}, u32[]{:S(2)}) collective-permute-start(f32[2,128,768]{2,1,0:T(8,128)} %slice_add_fusion.6), channel_id=1, source_target_pairs={{0,2},{1,3},{2,0},{3,1},{4,6},{5,7},{6,4},{7,5},{8,10},{9,11},{10,... | collective-permute-start | bytes 2359304 | tf_op jit(solution)/shard_map/ppermute | solution.py:486
  340.5 21.4 %collective-permute-start.38 = (f32[48,16,128]{2,1,0:T(8,128)}, f32[48,16,128]{2,1,0:T(8,128)}, u32[]{:S(2)}, u32[]{:S(2)}) collective-permute-start(f32[48,16,128]{2,1,0:T(8,128)} %multiply_add_fusion.2), channel_id=1, source_target_pairs={{16,0},{20,4},{24,8},{28,12},{17,1},{21,5},{25,9},{29,13},{18,2},{... | collective-permute-start | bytes 1179656 | tf_op jit(solution)/shard_map/ppermute | solution.py:482
  343.0 25.3 %collective-permute-start.27 = (f32[2,128,768]{2,1,0:T(8,128)}, f32[2,128,768]{2,1,0:T(8,128)}, u32[]{:S(2)}, u32[]{:S(2)}) collective-permute-start(f32[2,128,768]{2,1,0:T(8,128)} %split.89), channel_id=1, source_target_pairs={{0,1},{1,0},{2,3},{3,2},{4,5},{5,4},{6,7},{7,6},{8,9},{9,8},{10,11... | collective-permute-start | bytes 2359304 | tf_op jit(solution)/shard_map/ppermute | solution.py:486
  363.9 18.1 %collective-permute-start.39 = (f32[2,128,768]{2,1,0:T(8,128)S(1)}, f32[2,128,768]{2,1,0:T(8,128)}, u32[]{:S(2)}, u32[]{:S(2)}) collective-permute-start(f32[2,128,768]{2,1,0:T(8,128)S(1)} %add_select_fusion.refs_0_), channel_id=1, source_target_pairs={{0,2},{1,3},{2,0},{3,1},{4,6},{5,7},{6,4},{7,5},{8,10},{9,11},{10,... | collective-permute-start | bytes 2359304 | tf_op jit(solution)/shard_map/ppermute | solution.py:486
  366.2 15.6 %collective-permute-start.40 = (f32[48,16,128]{2,1,0:T(8,128)S(1)}, f32[48,16,128]{2,1,0:T(8,128)S(1)}, u32[]{:S(2)}, u32[]{:S(2)}) collective-permute-start(f32[48,16,128]{2,1,0:T(8,128)S(1)} %fusion.121), channel_id=1, source_target_pairs={{0,4},{4,0},{8,12},{12,8},{16,20},{20,16},{24,28},{28,24},{1,5},{5... | collective-permute-start | bytes 1179656 | tf_op jit(solution)/shard_map/ppermute | solution.py:486
  384.6 23.1 %collective-permute-start.41 = (f32[2,128,768]{2,1,0:T(8,128)}, f32[2,128,768]{2,1,0:T(8,128)}, u32[]{:S(2)}, u32[]{:S(2)}) collective-permute-start(f32[2,128,768]{2,1,0:T(8,128)} %add_select_fusion.1.refs_0_), channel_id=1, source_target_pairs={{0,2},{1,3},{2,0},{3,1},{4,6},{5,7},{6,4},{7,5},{8,10},{9,11},{10,... | collective-permute-start | bytes 2359304 | tf_op jit(solution)/shard_map/ppermute | solution.py:486
  385.7 61.3 %collective-permute-start.43 = (f32[2,128,768]{2,1,0:T(8,128)S(1)}, f32[2,128,768]{2,1,0:T(8,128)}, u32[]{:S(2)}, u32[]{:S(2)}) collective-permute-start(f32[2,128,768]{2,1,0:T(8,128)S(1)} %copy-done.26), channel_id=1, source_target_pairs={{0,1},{1,0},{2,3},{3,2},{4,5},{5,4},{6,7},{7,6},{8,9},{9,8},{10,11... | collective-permute-start | bytes 2359304 | tf_op jit(solution)/shard_map/ppermute | solution.py:486
  386.8 60.2 %collective-permute-start.36 = (f32[2,128,768]{2,1,0:T(8,128)}, f32[2,128,768]{2,1,0:T(8,128)}, u32[]{:S(2)}, u32[]{:S(2)}) collective-permute-start(f32[2,128,768]{2,1,0:T(8,128)} %add_select_fusion.1.refs_0_), channel_id=1, source_target_pairs={{0,1},{1,0},{2,3},{3,2},{4,5},{5,4},{6,7},{7,6},{8,9},{9,8},{10,11... | collective-permute-start | bytes 2359304 | tf_op jit(solution)/shard_map/ppermute | solution.py:486
  398.2 9.5 %collective-permute-start.45 = (f32[192,128]{1,0:T(8,128)}, f32[192,128]{1,0:T(8,128)S(1)}, u32[]{:S(2)}, u32[]{:S(2)}) collective-permute-start(f32[192,128]{1,0:T(8,128)} %get-tuple-element.175), channel_id=1, source_target_pairs={{4,0},{8,4},{12,8},{16,12},{20,16},{24,20},{28,24},{5,1},{9,5},{13... | collective-permute-start | bytes 294920 | tf_op jit(solution)/shard_map/ppermute | solution.py:482
  423.1 18.6 %collective-permute-start.49 = (f32[2,128,768]{2,1,0:T(8,128)}, f32[2,128,768]{2,1,0:T(8,128)S(1)}, u32[]{:S(2)}, u32[]{:S(2)}) collective-permute-start(f32[2,128,768]{2,1,0:T(8,128)} %get-tuple-element.185), channel_id=1, source_target_pairs={{0,1},{1,0},{2,3},{3,2},{4,5},{5,4},{6,7},{7,6},{8,9},{9,8},{10,11... | collective-permute-start | bytes 2359304 | tf_op jit(solution)/shard_map/ppermute | solution.py:486
  424.4 17.3 %collective-permute-start.48 = (f32[192,768]{1,0:T(8,128)}, f32[192,768]{1,0:T(8,128)}, u32[]{:S(2)}, u32[]{:S(2)}) collective-permute-start(f32[192,768]{1,0:T(8,128)} %constant_dynamic-slice_fusion.7), channel_id=1, source_target_pairs={{0,4},{4,0},{8,12},{12,8},{16,20},{20,16},{24,28},{28,24},{1,5},{5... | collective-permute-start | bytes 1769480 | tf_op jit(solution)/shard_map/ppermute | solution.py:486
  431.7 18.4 %collective-permute-start.44 = (f32[2,128,768]{2,1,0:T(8,128)}, f32[2,128,768]{2,1,0:T(8,128)}, u32[]{:S(2)}, u32[]{:S(2)}) collective-permute-start(f32[2,128,768]{2,1,0:T(8,128)} %collective-permute-done.39.refs_2_), channel_id=1, source_target_pairs={{0,1},{1,0},{2,3},{3,2},{4,5},{5,4},{6,7},{7,6},{8,9},{9,8},{10,11... | collective-permute-start | bytes 2359304 | tf_op jit(solution)/shard_map/ppermute | solution.py:486
  441.7 9.7 %collective-permute-start.47 = (f32[2,128,768]{2,1,0:T(8,128)}, f32[2,128,768]{2,1,0:T(8,128)}, u32[]{:S(2)}, u32[]{:S(2)}) collective-permute-start(f32[2,128,768]{2,1,0:T(8,128)} %get-tuple-element.180), channel_id=1, source_target_pairs={{0,1},{1,0},{2,3},{3,2},{4,5},{5,4},{6,7},{7,6},{8,9},{9,8},{10,11... | collective-permute-start | bytes 2359304 | tf_op jit(solution)/shard_map/ppermute | solution.py:486
  441.7 8.4 %collective-permute-start.42 = (f32[2,128,768]{2,1,0:T(8,128)}, f32[2,128,768]{2,1,0:T(8,128)}, u32[]{:S(2)}, u32[]{:S(2)}) collective-permute-start(f32[2,128,768]{2,1,0:T(8,128)} %collective-permute-done.41.refs_2_), channel_id=1, source_target_pairs={{0,1},{1,0},{2,3},{3,2},{4,5},{5,4},{6,7},{7,6},{8,9},{9,8},{10,11... | collective-permute-start | bytes 2359304 | tf_op jit(solution)/shard_map/ppermute | solution.py:486
  447.1 19.5 %collective-permute-start.55 = (f32[224,768]{1,0:T(8,128)}, f32[224,768]{1,0:T(8,128)}, u32[]{:S(2)}, u32[]{:S(2)}) collective-permute-start(f32[224,768]{1,0:T(8,128)} %constant_dynamic-slice_fusion.3), channel_id=1, source_target_pairs={{0,4},{4,0},{8,12},{12,8},{16,20},{20,16},{24,28},{28,24},{1,5},{5... | collective-permute-start | bytes 2064392 | tf_op jit(solution)/shard_map/ppermute | solution.py:486
  450.1 23.3 %collective-permute-start.62 = (f32[2,128,768]{2,1,0:T(8,128)}, f32[2,128,768]{2,1,0:T(8,128)}, u32[]{:S(2)}, u32[]{:S(2)}) collective-permute-start(f32[2,128,768]{2,1,0:T(8,128)} %get-tuple-element.204), channel_id=1, source_target_pairs={{0,1},{1,0},{2,3},{3,2},{4,5},{5,4},{6,7},{7,6},{8,9},{9,8},{10,11... | collective-permute-start | bytes 2359304 | tf_op jit(solution)/shard_map/ppermute | solution.py:486
  450.1 20.1 %collective-permute-start.56 = (f32[2,128,768]{2,1,0:T(8,128)S(1)}, f32[2,128,768]{2,1,0:T(8,128)}, u32[]{:S(2)}, u32[]{:S(2)}) collective-permute-start(f32[2,128,768]{2,1,0:T(8,128)S(1)} %add.453), channel_id=1, source_target_pairs={{0,2},{1,3},{2,0},{3,1},{4,6},{5,7},{6,4},{7,5},{8,10},{9,11},{10,... | collective-permute-start | bytes 2359304 | tf_op jit(solution)/shard_map/ppermute | solution.py:486
  451.4 15.1 %collective-permute-start.53 = (f32[48,768]{1,0:T(8,128)}, f32[48,768]{1,0:T(8,128)S(1)}, u32[]{:S(2)}, u32[]{:S(2)}) collective-permute-start(f32[48,768]{1,0:T(8,128)} %get-tuple-element.189), channel_id=1, source_target_pairs={{0,16},{4,20},{8,24},{12,28},{16,0},{20,4},{24,8},{28,12},{1,17},{... | collective-permute-start | bytes 442376 | tf_op jit(solution)/shard_map/ppermute | solution.py:486
  453.1 13.4 %collective-permute-start.54 = (f32[48,768]{1,0:T(8,128)S(1)}, f32[48,768]{1,0:T(8,128)S(1)}, u32[]{:S(2)}, u32[]{:S(2)}) collective-permute-start(f32[48,768]{1,0:T(8,128)S(1)} %get-tuple-element.190), channel_id=1, source_target_pairs={{0,24},{4,28},{8,16},{12,20},{16,8},{20,12},{24,0},{28,4},{1,25},{... | collective-permute-start | bytes 442376 | tf_op jit(solution)/shard_map/ppermute | solution.py:486
  466.5 13.2 %collective-permute-start.46 = (f32[2,128,768]{2,1,0:T(8,128)}, f32[2,128,768]{2,1,0:T(8,128)S(1)}, u32[]{:S(2)}, u32[]{:S(2)}) collective-permute-start(f32[2,128,768]{2,1,0:T(8,128)} %get-tuple-element.178), channel_id=1, source_target_pairs={{0,1},{1,0},{2,3},{3,2},{4,5},{5,4},{6,7},{7,6},{8,9},{9,8},{10,11... | collective-permute-start | bytes 2359304 | tf_op jit(solution)/shard_map/ppermute | solution.py:486
  470.2 19.1 %collective-permute-start.57 = (f32[2,128,768]{2,1,0:T(8,128)S(1)}, f32[2,128,768]{2,1,0:T(8,128)S(1)}, u32[]{:S(2)}, u32[]{:S(2)}) collective-permute-start(f32[2,128,768]{2,1,0:T(8,128)S(1)} %add.447), channel_id=1, source_target_pairs={{0,2},{1,3},{2,0},{3,1},{4,6},{5,7},{6,4},{7,5},{8,10},{9,11},{10,... | collective-permute-start | bytes 2359304 | tf_op jit(solution)/shard_map/ppermute | solution.py:486
  473.4 21.9 %collective-permute-start.64 = (f32[48,768]{1,0:T(8,128)S(1)}, f32[48,768]{1,0:T(8,128)S(1)}, u32[]{:S(2)}, u32[]{:S(2)}) collective-permute-start(f32[48,768]{1,0:T(8,128)S(1)} %get-tuple-element.205), channel_id=1, source_target_pairs={{0,16},{4,20},{8,24},{12,28},{16,0},{20,4},{24,8},{28,12},{1,17},{... | collective-permute-start | bytes 442376 | tf_op jit(solution)/shard_map/ppermute | solution.py:486
  473.4 21.9 %collective-permute-start.65 = (f32[48,768]{1,0:T(8,128)S(1)}, f32[48,768]{1,0:T(8,128)S(1)}, u32[]{:S(2)}, u32[]{:S(2)}) collective-permute-start(f32[48,768]{1,0:T(8,128)S(1)} %get-tuple-element.205), channel_id=1, source_target_pairs={{0,24},{4,28},{8,16},{12,20},{16,8},{20,12},{24,0},{28,4},{1,25},{... | collective-permute-start | bytes 442376 | tf_op jit(solution)/shard_map/ppermute | solution.py:486
  478.0 17.3 %collective-permute-start.61 = (f32[56,768]{1,0:T(8,128)S(1)}, f32[56,768]{1,0:T(8,128)S(1)}, u32[]{:S(2)}, u32[]{:S(2)}) collective-permute-start(f32[56,768]{1,0:T(8,128)S(1)} %get-tuple-element.202), channel_id=1, source_target_pairs={{0,24},{4,28},{8,16},{12,20},{16,8},{20,12},{24,0},{28,4},{1,25},{... | collective-permute-start | bytes 516104 | tf_op jit(solution)/shard_map/ppermute | solution.py:486
  479.6 23.4 %collective-permute-start.60 = (f32[56,768]{1,0:T(8,128)S(1)}, f32[56,768]{1,0:T(8,128)S(1)}, u32[]{:S(2)}, u32[]{:S(2)}) collective-permute-start(f32[56,768]{1,0:T(8,128)S(1)} %get-tuple-element.201), channel_id=1, source_target_pairs={{0,16},{4,20},{8,24},{12,28},{16,0},{20,4},{24,8},{28,12},{1,17},{... | collective-permute-start | bytes 516104 | tf_op jit(solution)/shard_map/ppermute | solution.py:486
  489.3 13.8 %collective-permute-start.59 = (f32[56,768]{1,0:T(8,128)S(1)}, f32[56,768]{1,0:T(8,128)S(1)}, u32[]{:S(2)}, u32[]{:S(2)}) collective-permute-start(f32[56,768]{1,0:T(8,128)S(1)} %get-tuple-element.200), channel_id=1, source_target_pairs={{0,8},{4,12},{8,0},{12,4},{16,24},{20,28},{24,16},{28,20},{1,9},{5... | collective-permute-start | bytes 516104 | tf_op jit(solution)/shard_map/ppermute | solution.py:486
  503.1 19.8 %collective-permute-start.70 = (f32[2,128,768]{2,1,0:T(8,128)}, f32[2,128,768]{2,1,0:T(8,128)}, u32[]{:S(2)}, u32[]{:S(2)}) collective-permute-start(f32[2,128,768]{2,1,0:T(8,128)} %get-tuple-element.206.refs_0_), channel_id=1, source_target_pairs={{0,2},{1,3},{2,0},{3,1},{4,6},{5,7},{6,4},{7,5},{8,10},{9,11},{10,... | collective-permute-start | bytes 2359304 | tf_op jit(solution)/shard_map/ppermute | solution.py:486
  504.0 18.8 %collective-permute-start.69 = (f32[192,768]{1,0:T(8,128)S(1)}, f32[192,768]{1,0:T(8,128)S(1)}, u32[]{:S(2)}, u32[]{:S(2)}) collective-permute-start(f32[192,768]{1,0:T(8,128)S(1)} %constant_dynamic-update-slice_fusion.8), channel_id=1, source_target_pairs={{0,4},{4,0},{8,12},{12,8},{16,20},{20,16},{24,28},{28,24},{1,5},{5... | collective-permute-start | bytes 1769480 | tf_op jit(solution)/shard_map/ppermute | solution.py:486
  506.1 9.3 %collective-permute-start.66 = (f32[56,768]{1,0:T(8,128)S(1)}, f32[56,768]{1,0:T(8,128)S(1)}, u32[]{:S(2)}, u32[]{:S(2)}) collective-permute-start(f32[56,768]{1,0:T(8,128)S(1)} %get-tuple-element.207), channel_id=1, source_target_pairs={{0,8},{4,12},{8,0},{12,4},{16,24},{20,28},{24,16},{28,20},{1,9},{5... | collective-permute-start | bytes 516104 | tf_op jit(solution)/shard_map/ppermute | solution.py:486
  506.1 16.8 %collective-permute-start.67 = (f32[56,768]{1,0:T(8,128)S(1)}, f32[56,768]{1,0:T(8,128)S(1)}, u32[]{:S(2)}, u32[]{:S(2)}) collective-permute-start(f32[56,768]{1,0:T(8,128)S(1)} %get-tuple-element.207), channel_id=1, source_target_pairs={{0,16},{4,20},{8,24},{12,28},{16,0},{20,4},{24,8},{28,12},{1,17},{... | collective-permute-start | bytes 516104 | tf_op jit(solution)/shard_map/ppermute | solution.py:486
  506.9 16.0 %collective-permute-start.68 = (f32[56,768]{1,0:T(8,128)S(1)}, f32[56,768]{1,0:T(8,128)S(1)}, u32[]{:S(2)}, u32[]{:S(2)}) collective-permute-start(f32[56,768]{1,0:T(8,128)S(1)} %get-tuple-element.207), channel_id=1, source_target_pairs={{0,24},{4,28},{8,16},{12,20},{16,8},{20,12},{24,0},{28,4},{1,25},{... | collective-permute-start | bytes 516104 | tf_op jit(solution)/shard_map/ppermute | solution.py:486
  515.3 12.8 %collective-permute-start.72 = (f32[2,128,768]{2,1,0:T(8,128)}, f32[2,128,768]{2,1,0:T(8,128)}, u32[]{:S(2)}, u32[]{:S(2)}) collective-permute-start(f32[2,128,768]{2,1,0:T(8,128)} %get-tuple-element.206.refs_0_), channel_id=1, source_target_pairs={{0,1},{1,0},{2,3},{3,2},{4,5},{5,4},{6,7},{7,6},{8,9},{9,8},{10,11... | collective-permute-start | bytes 2359304 | tf_op jit(solution)/shard_map/ppermute | solution.py:486
  522.9 20.1 %collective-permute-start.71 = (f32[2,128,768]{2,1,0:T(8,128)S(1)}, f32[2,128,768]{2,1,0:T(8,128)}, u32[]{:S(2)}, u32[]{:S(2)}) collective-permute-start(f32[2,128,768]{2,1,0:T(8,128)S(1)} %get-tuple-element.210.refs_0_), channel_id=1, source_target_pairs={{0,2},{1,3},{2,0},{3,1},{4,6},{5,7},{6,4},{7,5},{8,10},{9,11},{10,... | collective-permute-start | bytes 2359304 | tf_op jit(solution)/shard_map/ppermute | solution.py:486
  525.5 18.6 %collective-permute-start.75 = (f32[224,768]{1,0:T(8,128)}, f32[224,768]{1,0:T(8,128)}, u32[]{:S(2)}, u32[]{:S(2)}) collective-permute-start(f32[224,768]{1,0:T(8,128)} %constant_dynamic-update-slice_fusion.4), channel_id=1, source_target_pairs={{0,4},{4,0},{8,12},{12,8},{16,20},{20,16},{24,28},{28,24},{1,5},{5... | collective-permute-start | bytes 2064392 | tf_op jit(solution)/shard_map/ppermute | solution.py:486
  526.7 23.1 %collective-permute-start.58 = (f32[2,128,768]{2,1,0:T(8,128)S(1)}, f32[2,128,768]{2,1,0:T(8,128)}, u32[]{:S(2)}, u32[]{:S(2)}) collective-permute-start(f32[2,128,768]{2,1,0:T(8,128)S(1)} %get-tuple-element.210.refs_0_), channel_id=1, source_target_pairs={{0,1},{1,0},{2,3},{3,2},{4,5},{5,4},{6,7},{7,6},{8,9},{9,8},{10,11... | collective-permute-start | bytes 2359304 | tf_op jit(solution)/shard_map/ppermute | solution.py:486
  (94 other events, 923.1 us)
Sparse Core Ops, SparseCore 0:
  200.7 107.4 reduce-scatter.1
  362.1 80.2 all-gather.1

commit v4 on v3

--- a/solution.py
+++ b/solution.py
@@ -8,7 +8,7 @@
 from jax.sharding import PartitionSpec as P
 
 LANES = 128
-GROUP = 32
+GROUP = 64
 BF = jnp.bfloat16
 F32 = jnp.float32
 
@@ -725,7 +725,7 @@
     d_ups = [x[1] for x in fed]
     sums = []
     for u in range(chunks):
-        far = link.swap(far_total(fed[2 * u + 1][2]), *((early,) if u else ()))
+        far = link.swap(far_total(fed[2 * u + 1][2]))
         if u == 0:
             late_mlp, late_up, _ = lax.optimization_barrier((d_mlp, d_ups, link.sent))
             grad_down = product("btf,btd->fd", jnp.concatenate(hiddens, axis=0), late_mlp)
@@ -733,6 +733,8 @@
                 "btd,btf->df", jnp.concatenate(seconds, axis=0), jnp.concatenate(late_up, axis=0)
             )
             early = jnp.concatenate([grad_up, grad_down], axis=0)
+            far, early = lax.optimization_barrier((far, early))
+            link.last = (far,)
         sums.append((far_total(fed[2 * u][2]), far))
     early = lax.psum_scatter(early, "seq", scatter_dimension=0, tiled=True)
     lowered = [product("btf,fd->btd", hidden, down_weight) for hidden in hiddens]
@@ -797,12 +799,12 @@
     early = lax.all_gather(early, "seq", axis=0, tiled=True)
     flying = give_out(1, after)
     others = Total(jnp.concatenate([grad_project, grad_query], axis=0))
+    first_got = others.run(1, after)
     d_values, d_shifted, head, grad_taps = bwd_post(
         d_part, after, coef, rate, keys, values, tail, tap_rows
     )
     spill = passed_along(head, "seq", -1)
-    spill, _ = lax.optimization_barrier((spill, flying))
-    others.run(1, spill)
+    spill, _ = lax.optimization_barrier((spill, (flying, first_got)))
     pieces, main, grad_first = last_call(
         d_queries, d_values, d_shifted, spill, tap_rows, normed, turned, chunks * parts, 64
     )
@@ -818,7 +820,7 @@
     pairs = channels // 2
     edges = jnp.concatenate([grad_taps[:, :taps].T.reshape(-1), lags[:, 0]])
     edges = jnp.pad(edges, (0, -edges.shape[0] % width_all)).reshape(-1, width_all)
-    gains = summed(jnp.concatenate([grad_first / first_gain, grad_second[None, :]]), ("tp",))
+    gains = jnp.concatenate([grad_first / first_gain, grad_second[None, :]])
     tables = [grad_coef.reshape(-1, width_all), grad_rate.reshape(-1, width_all), gains, edges]
     rows = sum(x.shape[0] for x in tables)
     tables.append(jnp.zeros((64 - rows, width_all), F32))
@@ -826,7 +828,6 @@
     mains = Total(main)
     rows = grad_up.shape[0]
     grad_up, grad_down = early[:rows], early[rows:]
-    link.waits += (gains,)
     sums = []
     for u in range(chunks):
         at = parts * u
@@ -854,7 +855,7 @@
     grad_coef = main[at : at + rows].reshape(channels, states)
     grad_rate = main[at + rows : at + 2 * rows].reshape(channels, states)
     at += 2 * rows
-    gains = main[at : at + 2]
+    gains = summed(main[at : at + 2], ("tp",))
     edges = main[at + 2 :].reshape(-1)
     grad_taps = edges[: taps * channels].reshape(taps, channels)
     grad_skip = edges[taps * channels : (taps + 1) * channels]

time: 568 us -> 558 us (0.982)
  waiting for transfers between devices: 238 us -> 223 us
  Pallas kernels: 97 us -> 90.5 us
  starting transfers between devices: 72.4 us -> 78.7 us
    ppermute x70, waiting for transfers between devices: 201 us -> 188 us  [swapped(): lax.ppermute(x, axis, [(i, i ^ bit) for i in range(lax.axis_size(axis))])]
    pallas_call x5, Pallas kernels: 51 us -> 44.3 us  [call(): pl.pallas_call(kernel, grid=(channels // GROUP,), in_specs=ins, out_specs...]
    ppermute x70, starting transfers between devices: 53.8 us -> 59.8 us  [swapped(): lax.ppermute(x, axis, [(i, i ^ bit) for i in range(lax.axis_size(axis))])]
    unnamed x166 -> x168, local copies, waits for them, and re-layouts: 11.8 us -> 12.6 us
  transfers between devices with their start and end apart: 78 -> 78, of which waited for: 32 -> 34; matrix products, arithmetic and copies ran while one was open for 19% -> 22% of each run, Pallas kernels for 11% -> 10%
where the time goes in v4:
time: 558 us; the launch traced here: 552 us
  waiting for transfers between devices  223 us (40%)
  Pallas kernels  90.5 us (16%)
  starting transfers between devices  78.7 us (14%)
  other arithmetic  57.3 us (10%)
  local copies, waits for them, and re-layouts  48.2 us (9%)
  matrix products  39.2 us (7%)
  between operations  15.7 us (3%)
    ppermute x70, waiting for transfers between devices, swapped(): lax.ppermute(x, axis, [(i, i ^ bit) for i in range(lax.axis_size(axis))])  188 us
    ppermute x70, starting transfers between devices, swapped(): lax.ppermute(x, axis, [(i, i ^ bit) for i in range(lax.axis_size(axis))])  59.8 us
    pallas_call x5, Pallas kernels, call(): pl.pallas_call(kernel, grid=(channels // GROUP,), in_specs=ins, out_specs...  44.3 us
    dot_general x26, matrix products, product(): return jnp.einsum(form, left, right, preferred_element_type=F32)  39.2 us
    ppermute x6, waiting for transfers between devices, passed_along(): return lax.ppermute(x, axis, pairs)  35.2 us
    pallas_call x4, Pallas kernels, place_call(): pl.pallas_call(functools.partial(place_kernel, count=count), grid_spec=pl...  19.1 us
    ppermute x6, starting transfers between devices, passed_along(): return lax.ppermute(x, axis, pairs)  18.6 us
    pallas_call x1, Pallas kernels, last_call(): pl.pallas_call(last_kernel, grid=(pieces,), in_specs=[act, act, act, pl.B...  14.7 us
  transfers between devices with their start and end apart: 78, of which 34 were waited for; matrix products, arithmetic and copies ran while one was open for 22% of the time, Pallas kernels for 10%

profile of v4, /device:TPU:0, one launch (start us, length us, event | category | flops | bytes accessed | tf_op | source)
XLA Modules:
  0.0 552.5 jit_solution(7408964532845824349)
XLA Ops:
  9.8 12.4 %shard_map.254 = (bf16[16,128,768]{2,1,0:T(8,128)(2,1)}, bf16[16,128,768]{2,1,0:T(8,128)(2,1)}, f32[16,192,128]{2,1,0:T(8,128)}, f32[16,192,128]{2,1,0:T(8,128)}...) custom-call(s32[18]{0:T(128)} %pad_add_fusion.1.at_ref, bf16[16,128,768]{2,1,0:T(8,128)(2,1)} %x_ref.1, ...), custom_call_target="tpu_custom_call" | custom-call | tf_op jit(solution)/shard_map/pallas_call | solution.py:318
  22.2 4.9 collective-permute-start
  27.3 4.6 multiply_reduce_fusion.kern_ref
  34.1 10.7 %shard_map.255 = (f32[16,192,128]{2,1,0:T(8,128)}, f32[16,192,128]{2,1,0:T(8,128)}, f32[96,16,128]{2,1,0:T(8,128)}) custom-call(f32[16,192,128]{2,1,0:T(8,128)} %get-tuple-element.116.k_ref, f32[16,192,128]{2,1,0:T(8,128)} %get-tuple-element.117.v_ref, f32[192,128]{1,0:T(8,128)} %copy-done.52, f32[192,4]{1,0:T(8,128)} %bitcast.116, ...), custom_call_target="tpu_custom_call" | custom-call | tf_op jit(solution)/shard_map/pallas_call | solution.py:423
  48.3 8.5 %collective-permute-done.1 = f32[48,16,128]{2,1,0:T(8,128)S(1)} collective-permute-done((f32[48,16,128]{2,1,0:T(8,128)S(1)}, f32[48,16,128]{2,1,0:T(8,128)S(1)}, u32[]{:S(2)}, u32[]{:S(2)}) %collective-permute-start.1) | collective-permute-done | bytes 393248 | tf_op jit(solution)/shard_map/ppermute | solution.py:486
  56.8 3.5 collective-permute-start.2
  60.4 7.2 %collective-permute-done.2 = f32[48,16,128]{2,1,0:T(8,128)S(1)} collective-permute-done((f32[48,16,128]{2,1,0:T(8,128)S(1)}, f32[48,16,128]{2,1,0:T(8,128)S(1)}, u32[]{:S(2)}, u32[]{:S(2)}) %collective-permute-start.2) | collective-permute-done | bytes 393248 | tf_op jit(solution)/shard_map/ppermute | solution.py:482
  67.6 5.4 collective-permute-start.3
  73.1 6.3 %collective-permute-done.3 = f32[48,16,128]{2,1,0:T(8,128)S(1)} collective-permute-done((f32[48,16,128]{2,1,0:T(8,128)S(1)}, f32[48,16,128]{2,1,0:T(8,128)S(1)}, u32[]{:S(2)}, u32[]{:S(2)}) %collective-permute-start.3) | collective-permute-done | bytes 393248 | tf_op jit(solution)/shard_map/ppermute | solution.py:482
  82.6 5.0 collective-permute-done.4
  89.9 6.5 %shard_map.256 = (f32[16,192,128]{2,1,0:T(8,128)}, bf16[16,192,128]{2,1,0:T(8,128)(2,1)}) custom-call(f32[16,192,128]{2,1,0:T(8,128)} %get-tuple-element.119.y_ref, f32[96,16,128]{2,1,0:T(8,128)} %pad_maximum_fusion.2.hin_ref, f32[96,128]{1,0:T(8,128)} %reshape.190.coef_ref, f32[96,128]{1,0:T(8,128)} %reshape.189.rate_ref, ...), custom_call_target="tpu_custom_call" | custom-call | tf_op jit(solution)/shard_map/pallas_call | solution.py:423
  106.6 13.6 %collective-permute-done.8 = f32[2,128,768]{2,1,0:T(8,128)} collective-permute-done((f32[2,128,768]{2,1,0:T(8,128)S(1)}, f32[2,128,768]{2,1,0:T(8,128)}, u32[]{:S(2)}, u32[]{:S(2)}) %collective-permute-start.8) | collective-permute-done | bytes 786464 | tf_op jit(solution)/shard_map/ppermute | solution.py:486
  124.4 14.9 %collective-permute-done.9 = f32[2,128,768]{2,1,0:T(8,128)} collective-permute-done((f32[2,128,768]{2,1,0:T(8,128)}, f32[2,128,768]{2,1,0:T(8,128)}, u32[]{:S(2)}, u32[]{:S(2)}) %collective-permute-start.9) | collective-permute-done | bytes 786464 | tf_op jit(solution)/shard_map/ppermute | solution.py:486
  139.3 3.7 fusion.116
  151.9 11.5 %collective-permute-done.13 = f32[2,128,768]{2,1,0:T(8,128)S(1)} collective-permute-done((f32[2,128,768]{2,1,0:T(8,128)S(1)}, f32[2,128,768]{2,1,0:T(8,128)S(1)}, u32[]{:S(2)}, u32[]{:S(2)}) %collective-permute-start.13) | collective-permute-done | bytes 786464 | tf_op jit(solution)/shard_map/ppermute | solution.py:486
  174.1 9.3 %collective-permute-done.10 = f32[2,128,768]{2,1,0:T(8,128)S(1)} collective-permute-done((f32[2,128,768]{2,1,0:T(8,128)S(1)}, f32[2,128,768]{2,1,0:T(8,128)S(1)}, u32[]{:S(2)}, u32[]{:S(2)}) %collective-permute-start.10) | collective-permute-done | bytes 786464 | tf_op jit(solution)/shard_map/ppermute | solution.py:486
  190.7 2.8 fusion.32
  193.6 2.8 fusion.29
  196.4 2.5 pad_maximum_fusion
  198.9 10.5 %collective-permute-done.20 = f32[2,128,768]{2,1,0:T(8,128)} collective-permute-done((f32[2,128,768]{2,1,0:T(8,128)}, f32[2,128,768]{2,1,0:T(8,128)}, u32[]{:S(2)}, u32[]{:S(2)}) %collective-permute-start.20) | collective-permute-done | bytes 786464 | tf_op jit(solution)/shard_map/ppermute | solution.py:486
  219.1 14.8 %collective-permute-done.21 = f32[2,128,768]{2,1,0:T(8,128)S(1)} collective-permute-done((f32[2,128,768]{2,1,0:T(8,128)S(1)}, f32[2,128,768]{2,1,0:T(8,128)S(1)}, u32[]{:S(2)}, u32[]{:S(2)}) %collective-permute-start.21) | collective-permute-done | bytes 786464 | tf_op jit(solution)/shard_map/ppermute | solution.py:486
  239.8 13.7 %collective-permute-done.23 = f32[2,128,768]{2,1,0:T(8,128)S(1)} collective-permute-done((f32[2,128,768]{2,1,0:T(8,128)S(1)}, f32[2,128,768]{2,1,0:T(8,128)S(1)}, u32[]{:S(2)}, u32[]{:S(2)}) %collective-permute-start.23) | collective-permute-done | bytes 786464 | tf_op jit(solution)/shard_map/ppermute | solution.py:486
  260.5 14.6 %collective-permute-done.24 = f32[2,128,768]{2,1,0:T(8,128)} collective-permute-done((f32[2,128,768]{2,1,0:T(8,128)}, f32[2,128,768]{2,1,0:T(8,128)}, u32[]{:S(2)}, u32[]{:S(2)}) %collective-permute-start.24) | collective-permute-done | bytes 786464 | tf_op jit(solution)/shard_map/ppermute | solution.py:486
  276.6 2.2 split.91
  279.4 2.1 split.93
  281.5 2.4 fusion.24
  285.9 7.4 %shard_map.257 = (bf16[16,192,128]{2,1,0:T(8,128)(2,1)}, f32[16,192,128]{2,1,0:T(8,128)}, f32[16,192,128]{2,1,0:T(8,128)}, f32[96,16,128]{2,1,0:T(8,128)}) custom-call(f32[16,192,128]{2,1,0:T(8,128)} %pad_maximum_fusion.1.dg_ref, f32[16,192,128]{2,1,0:T(8,128)} %get-tuple-element.122.q_ref, f32[16,192,128]{2,1,0:T(8,128)} %get-tuple-element.156.state_ref, ...), custom_call_target="tpu_custom_call" | custom-call | tf_op jit(solution)/shard_map/pallas_call | solution.py:423
  296.3 2.1 split.95
  301.1 10.3 %collective-permute-done.33 = f32[48,16,128]{2,1,0:T(8,128)S(1)} collective-permute-done((f32[48,16,128]{2,1,0:T(8,128)S(1)}, f32[48,16,128]{2,1,0:T(8,128)S(1)}, u32[]{:S(2)}, u32[]{:S(2)}) %collective-permute-start.33) | collective-permute-done | bytes 393248 | tf_op jit(solution)/shard_map/ppermute | solution.py:486
  316.9 2.9 collective-permute-done.32
  319.9 10.5 %collective-permute-done.34 = f32[48,16,128]{2,1,0:T(8,128)S(1)} collective-permute-done((f32[48,16,128]{2,1,0:T(8,128)S(1)}, f32[48,16,128]{2,1,0:T(8,128)S(1)}, u32[]{:S(2)}, u32[]{:S(2)}) %collective-permute-start.34) | collective-permute-done | bytes 393248 | tf_op jit(solution)/shard_map/ppermute | solution.py:482
  336.1 11.3 %shard_map.258 = (f32[96,16,128]{2,1,0:T(8,128)}, f32[96,16,128]{2,1,0:T(8,128)}, f32[192,128]{1,0:T(8,128)}, f32[96,128]{1,0:T(8,128)}, f32[96,128]{1,0:T(8,128)}) custom-call(f32[16,192,128]{2,1,0:T(8,128)} %get-tuple-element.163.d_ref, f32[16,192,128]{2,1,0:T(8,128)} %get-tuple-element.121.mixed_ref, f32[96,128]{1,0:T(8,128)} %reshape.189.rate_ref), custom_call_target="tpu_custom_call" | custom-call | tf_op jit(solution)/shard_map/pallas_call | solution.py:423
  347.4 2.8 add_select_fusion.refs_0_
  350.2 3.7 collective-permute-done.38
  355.0 3.0 convolution_bitcast_fusion.2
  360.1 2.7 add_select_fusion.1.refs_0_
  362.8 12.5 %collective-permute-done.40 = f32[48,16,128]{2,1,0:T(8,128)S(1)} collective-permute-done((f32[48,16,128]{2,1,0:T(8,128)S(1)}, f32[48,16,128]{2,1,0:T(8,128)S(1)}, u32[]{:S(2)}, u32[]{:S(2)}) %collective-permute-start.40) | collective-permute-done | bytes 393248 | tf_op jit(solution)/shard_map/ppermute | solution.py:486
  381.3 8.3 %shard_map.261 = (bf16[16,192,128]{2,1,0:T(8,128)(2,1)}, f32[16,192,128]{2,1,0:T(8,128)}, f32[192,128]{1,0:T(8,128)}, f32[192,128]{1,0:T(8,128)}) custom-call(f32[16,192,128]{2,1,0:T(8,128)} %get-tuple-element.176.dx_ref, f32[96,16,128]{2,1,0:T(8,128)} %get-tuple-element.297.gin_ref, f32[96,128]{1,0:T(8,128)} %reshape.190.coef_ref, ...), custom_call_target="tpu_custom_call" | custom-call | tf_op jit(solution)/shard_map/pallas_call | solution.py:423
  391.5 7.5 %collective-permute-done.45.spill_ref = f32[192,128]{1,0:T(8,128)S(1)} collective-permute-done((f32[192,128]{1,0:T(8,128)}, f32[192,128]{1,0:T(8,128)S(1)}, u32[]{:S(2)}, u32[]{:S(2)}) %collective-permute-start.45) | collective-permute-done | bytes 98336 | tf_op jit(solution)/shard_map/ppermute | solution.py:482
  399.9 14.7 %shard_map.262 = (f32[2,128,768]{2,1,0:T(8,128)}, f32[2,128,768]{2,1,0:T(8,128)}, f32[2,128,768]{2,1,0:T(8,128)}, f32[2,128,768]{2,1,0:T(8,128)}, f32[2,128,768]...) custom-call(bf16[16,192,128]{2,1,0:T(8,128)(2,1)} %get-tuple-element, ...), custom_call_target="tpu_custom_call" | custom-call | tf_op jit(solution)/shard_map/pallas_call | solution.py:357
  421.2 2.4 add.453
  423.7 5.3 collective-permute-start.50
  429.0 2.2 collective-permute-start.53
  434.1 3.0 collective-permute-done.50
  437.1 2.2 collective-permute-start.52
  439.3 4.8 shard_map.259.refs_4_
  446.2 4.8 shard_map.260
  453.7 3.1 collective-permute-start.55
  458.2 3.0 collective-permute-start.63
  461.2 2.2 fusion.112
  465.6 8.3 %collective-permute-done.55 = f32[2,128,768]{2,1,0:T(8,128)S(1)} collective-permute-done((f32[2,128,768]{2,1,0:T(8,128)S(1)}, f32[2,128,768]{2,1,0:T(8,128)S(1)}, u32[]{:S(2)}, u32[]{:S(2)}) %collective-permute-start.55) | collective-permute-done | bytes 786464 | tf_op jit(solution)/shard_map/ppermute | solution.py:486
  475.0 2.9 fusion.115
  478.0 8.8 %collective-permute-done.58 = f32[56,768]{1,0:T(8,128)S(1)} collective-permute-done((f32[56,768]{1,0:T(8,128)S(1)}, f32[56,768]{1,0:T(8,128)S(1)}, u32[]{:S(2)}, u32[]{:S(2)}) %collective-permute-start.58) | collective-permute-done | bytes 172064 | tf_op jit(solution)/shard_map/ppermute | solution.py:486
  488.9 2.2 collective-permute-start.65
  491.1 2.4 collective-permute-start.66
  493.4 2.7 collective-permute-done.64
  496.1 3.3 collective-permute-start.67
  500.1 3.8 collective-permute-done.65
  505.3 4.9 fusion.143
  511.2 2.2 collective-permute-start.73
  517.7 4.7 shard_map.263.refs_4_
  522.4 7.5 %collective-permute-done.73 = f32[224,768]{1,0:T(8,128)} collective-permute-done((f32[224,768]{1,0:T(8,128)}, f32[224,768]{1,0:T(8,128)}, u32[]{:S(2)}, u32[]{:S(2)}) %collective-permute-start.73) | collective-permute-done | bytes 688160 | tf_op jit(solution)/shard_map/ppermute | solution.py:486
  531.1 2.2 collective-permute-done.69.refs_2_
  540.7 4.8 shard_map.264
  (441 shorter events, 146.7 us)
Async XLA Ops:
  7.2 346.7 %reduce-scatter.2.cloned.1.call-start = ((), (), s32[]{:S(2)}) async-start(), calls=%async_computation.1 | async-start | bytes 5308416 | tf_op jit(solution)/shard_map/reduce_scatter | solution.py:739
  22.2 11.3 %collective-permute-start = (f32[192,128]{1,0:T(8,128)}, f32[192,128]{1,0:T(8,128)S(1)}, u32[]{:S(2)}, u32[]{:S(2)}) collective-permute-start(f32[192,128]{1,0:T(8,128)} %get-tuple-element.118), channel_id=1, source_target_pairs={{0,4},{4,8},{8,12},{12,16},{16,20},{20,24},{24,28},{1,5},{5,9},{9,... | collective-permute-start | bytes 294920 | tf_op jit(solution)/shard_map/ppermute | solution.py:482
  46.0 10.7 %collective-permute-start.1 = (f32[48,16,128]{2,1,0:T(8,128)S(1)}, f32[48,16,128]{2,1,0:T(8,128)S(1)}, u32[]{:S(2)}, u32[]{:S(2)}) collective-permute-start(f32[48,16,128]{2,1,0:T(8,128)S(1)} %slice_select_fusion.2), channel_id=1, source_target_pairs={{0,4},{4,0},{8,12},{12,8},{16,20},{20,16},{24,28},{28,24},{1,5},{5... | collective-permute-start | bytes 1179656 | tf_op jit(solution)/shard_map/ppermute | solution.py:486
  56.8 10.7 %collective-permute-start.2 = (f32[48,16,128]{2,1,0:T(8,128)S(1)}, f32[48,16,128]{2,1,0:T(8,128)S(1)}, u32[]{:S(2)}, u32[]{:S(2)}) collective-permute-start(f32[48,16,128]{2,1,0:T(8,128)S(1)} %get-tuple-element.281), channel_id=1, source_target_pairs={{0,8},{4,12},{8,16},{12,20},{16,24},{20,28},{1,9},{5,13},{9,17},{1... | collective-permute-start | bytes 1179656 | tf_op jit(solution)/shard_map/ppermute | solution.py:482
  67.6 11.8 %collective-permute-start.3 = (f32[48,16,128]{2,1,0:T(8,128)S(1)}, f32[48,16,128]{2,1,0:T(8,128)S(1)}, u32[]{:S(2)}, u32[]{:S(2)}) collective-permute-start(f32[48,16,128]{2,1,0:T(8,128)S(1)} %multiply_add_fusion.5), channel_id=1, source_target_pairs={{0,16},{4,20},{8,24},{12,28},{1,17},{5,21},{9,25},{13,29},{2,18},{... | collective-permute-start | bytes 1179656 | tf_op jit(solution)/shard_map/ppermute | solution.py:482
  79.5 8.1 %collective-permute-start.4 = (f32[48,16,128]{2,1,0:T(8,128)S(1)}, f32[48,16,128]{2,1,0:T(8,128)}, u32[]{:S(2)}, u32[]{:S(2)}) collective-permute-start(f32[48,16,128]{2,1,0:T(8,128)S(1)} %fusion.123), channel_id=1, source_target_pairs={{0,4},{4,0},{8,12},{12,8},{16,20},{20,16},{24,28},{28,24},{1,5},{5... | collective-permute-start | bytes 1179656 | tf_op jit(solution)/shard_map/ppermute | solution.py:486
  98.5 7.1 %collective-permute-start.6 = (f32[2,128,768]{2,1,0:T(8,128)S(1)}, f32[2,128,768]{2,1,0:T(8,128)S(1)}, u32[]{:S(2)}, u32[]{:S(2)}) collective-permute-start(f32[2,128,768]{2,1,0:T(8,128)S(1)} %split.99), channel_id=1, source_target_pairs={{0,1},{1,0},{2,3},{3,2},{4,5},{5,4},{6,7},{7,6},{8,9},{9,8},{10,11... | collective-permute-start | bytes 2359304 | tf_op jit(solution)/shard_map/ppermute | solution.py:486
  100.4 19.8 %collective-permute-start.8 = (f32[2,128,768]{2,1,0:T(8,128)S(1)}, f32[2,128,768]{2,1,0:T(8,128)}, u32[]{:S(2)}, u32[]{:S(2)}) collective-permute-start(f32[2,128,768]{2,1,0:T(8,128)S(1)} %slice_add_fusion.2), channel_id=1, source_target_pairs={{0,2},{1,3},{2,0},{3,1},{4,6},{5,7},{6,4},{7,5},{8,10},{9,11},{10,... | collective-permute-start | bytes 2359304 | tf_op jit(solution)/shard_map/ppermute | solution.py:486
  103.2 19.3 %collective-permute-start.5 = (f32[2,128,768]{2,1,0:T(8,128)}, f32[2,128,768]{2,1,0:T(8,128)S(1)}, u32[]{:S(2)}, u32[]{:S(2)}) collective-permute-start(f32[2,128,768]{2,1,0:T(8,128)} %split.97), channel_id=1, source_target_pairs={{0,1},{1,0},{2,3},{3,2},{4,5},{5,4},{6,7},{7,6},{8,9},{9,8},{10,11... | collective-permute-start | bytes 2359304 | tf_op jit(solution)/shard_map/ppermute | solution.py:486
  105.1 17.5 %collective-permute-start.12 = (f32[2,128,768]{2,1,0:T(8,128)}, f32[2,128,768]{2,1,0:T(8,128)S(1)}, u32[]{:S(2)}, u32[]{:S(2)}) collective-permute-start(f32[2,128,768]{2,1,0:T(8,128)} %split.103), channel_id=1, source_target_pairs={{0,1},{1,0},{2,3},{3,2},{4,5},{5,4},{6,7},{7,6},{8,9},{9,8},{10,11... | collective-permute-start | bytes 2359304 | tf_op jit(solution)/shard_map/ppermute | solution.py:486
  120.2 19.1 %collective-permute-start.9 = (f32[2,128,768]{2,1,0:T(8,128)}, f32[2,128,768]{2,1,0:T(8,128)}, u32[]{:S(2)}, u32[]{:S(2)}) collective-permute-start(f32[2,128,768]{2,1,0:T(8,128)} %slice_add_fusion.3), channel_id=1, source_target_pairs={{0,2},{1,3},{2,0},{3,1},{4,6},{5,7},{6,4},{7,5},{8,10},{9,11},{10,... | collective-permute-start | bytes 2359304 | tf_op jit(solution)/shard_map/ppermute | solution.py:486
  143.5 20.0 %collective-permute-start.13 = (f32[2,128,768]{2,1,0:T(8,128)S(1)}, f32[2,128,768]{2,1,0:T(8,128)S(1)}, u32[]{:S(2)}, u32[]{:S(2)}) collective-permute-start(f32[2,128,768]{2,1,0:T(8,128)S(1)} %subtract_multiply_fusion.2), channel_id=1, source_target_pairs={{0,2},{1,3},{2,0},{3,1},{4,6},{5,7},{6,4},{7,5},{8,10},{9,11},{10,... | collective-permute-start | bytes 2359304 | tf_op jit(solution)/shard_map/ppermute | solution.py:486
  145.1 19.5 %collective-permute-start.11 = (f32[2,128,768]{2,1,0:T(8,128)S(1)}, f32[2,128,768]{2,1,0:T(8,128)S(1)}, u32[]{:S(2)}, u32[]{:S(2)}) collective-permute-start(f32[2,128,768]{2,1,0:T(8,128)S(1)} %subtract_multiply_fusion.3), channel_id=1, source_target_pairs={{0,1},{1,0},{2,3},{3,2},{4,5},{5,4},{6,7},{7,6},{8,9},{9,8},{10,11... | collective-permute-start | bytes 2359304 | tf_op jit(solution)/shard_map/ppermute | solution.py:486
  163.4 20.0 %collective-permute-start.10 = (f32[2,128,768]{2,1,0:T(8,128)S(1)}, f32[2,128,768]{2,1,0:T(8,128)S(1)}, u32[]{:S(2)}, u32[]{:S(2)}) collective-permute-start(f32[2,128,768]{2,1,0:T(8,128)S(1)} %subtract_multiply_fusion.3), channel_id=1, source_target_pairs={{0,2},{1,3},{2,0},{3,1},{4,6},{5,7},{6,4},{7,5},{8,10},{9,11},{10,... | collective-permute-start | bytes 2359304 | tf_op jit(solution)/shard_map/ppermute | solution.py:486
  189.5 19.9 %collective-permute-start.20 = (f32[2,128,768]{2,1,0:T(8,128)}, f32[2,128,768]{2,1,0:T(8,128)}, u32[]{:S(2)}, u32[]{:S(2)}) collective-permute-start(f32[2,128,768]{2,1,0:T(8,128)} %slice_add_fusion.7), channel_id=1, source_target_pairs={{0,2},{1,3},{2,0},{3,1},{4,6},{5,7},{6,4},{7,5},{8,10},{9,11},{10,... | collective-permute-start | bytes 2359304 | tf_op jit(solution)/shard_map/ppermute | solution.py:486
  209.4 295.9 %all-gather.2.cloned.1.call-start = ((), (), s32[]{:S(2)}) async-start(), calls=%async_computation.2 | async-start | bytes 5308416 | tf_op jit(solution)/shard_map/all_gather | solution.py:799
  214.2 19.6 %collective-permute-start.21 = (f32[2,128,768]{2,1,0:T(8,128)S(1)}, f32[2,128,768]{2,1,0:T(8,128)S(1)}, u32[]{:S(2)}, u32[]{:S(2)}) collective-permute-start(f32[2,128,768]{2,1,0:T(8,128)S(1)} %slice_add_fusion), channel_id=1, source_target_pairs={{0,2},{1,3},{2,0},{3,1},{4,6},{5,7},{6,4},{7,5},{8,10},{9,11},{10,... | collective-permute-start | bytes 2359304 | tf_op jit(solution)/shard_map/ppermute | solution.py:486
  234.6 18.9 %collective-permute-start.23 = (f32[2,128,768]{2,1,0:T(8,128)S(1)}, f32[2,128,768]{2,1,0:T(8,128)S(1)}, u32[]{:S(2)}, u32[]{:S(2)}) collective-permute-start(f32[2,128,768]{2,1,0:T(8,128)S(1)} %get-tuple-element.149), channel_id=1, source_target_pairs={{0,2},{1,3},{2,0},{3,1},{4,6},{5,7},{6,4},{7,5},{8,10},{9,11},{10,... | collective-permute-start | bytes 2359304 | tf_op jit(solution)/shard_map/ppermute | solution.py:486
  239.8 18.3 %collective-permute-start.25 = (f32[2,128,768]{2,1,0:T(8,128)S(1)}, f32[2,128,768]{2,1,0:T(8,128)S(1)}, u32[]{:S(2)}, u32[]{:S(2)}) collective-permute-start(f32[2,128,768]{2,1,0:T(8,128)S(1)} %get-tuple-element.149), channel_id=1, source_target_pairs={{0,1},{1,0},{2,3},{3,2},{4,5},{5,4},{6,7},{7,6},{8,9},{9,8},{10,11... | collective-permute-start | bytes 2359304 | tf_op jit(solution)/shard_map/ppermute | solution.py:486
  254.8 20.3 %collective-permute-start.24 = (f32[2,128,768]{2,1,0:T(8,128)}, f32[2,128,768]{2,1,0:T(8,128)}, u32[]{:S(2)}, u32[]{:S(2)}) collective-permute-start(f32[2,128,768]{2,1,0:T(8,128)} %subtract_multiply_fusion.1), channel_id=1, source_target_pairs={{0,2},{1,3},{2,0},{3,1},{4,6},{5,7},{6,4},{7,5},{8,10},{9,11},{10,... | collective-permute-start | bytes 2359304 | tf_op jit(solution)/shard_map/ppermute | solution.py:486
  257.9 23.6 %collective-permute-start.30 = (f32[2,128,768]{2,1,0:T(8,128)}, f32[2,128,768]{2,1,0:T(8,128)}, u32[]{:S(2)}, u32[]{:S(2)}) collective-permute-start(f32[2,128,768]{2,1,0:T(8,128)} %subtract_multiply_fusion.1), channel_id=1, source_target_pairs={{0,1},{1,0},{2,3},{3,2},{4,5},{5,4},{6,7},{7,6},{8,9},{9,8},{10,11... | collective-permute-start | bytes 2359304 | tf_op jit(solution)/shard_map/ppermute | solution.py:486
  278.9 34.3 %collective-permute-start.28 = (f32[2,128,768]{2,1,0:T(8,128)}, f32[2,128,768]{2,1,0:T(8,128)}, u32[]{:S(2)}, u32[]{:S(2)}) collective-permute-start(f32[2,128,768]{2,1,0:T(8,128)} %split.91), channel_id=1, source_target_pairs={{0,1},{1,0},{2,3},{3,2},{4,5},{5,4},{6,7},{7,6},{8,9},{9,8},{10,11... | collective-permute-start | bytes 2359304 | tf_op jit(solution)/shard_map/ppermute | solution.py:486
  281.5 17.1 %collective-permute-start.29 = (f32[2,128,768]{2,1,0:T(8,128)}, f32[2,128,768]{2,1,0:T(8,128)}, u32[]{:S(2)}, u32[]{:S(2)}) collective-permute-start(f32[2,128,768]{2,1,0:T(8,128)} %split.93), channel_id=1, source_target_pairs={{0,1},{1,0},{2,3},{3,2},{4,5},{5,4},{6,7},{7,6},{8,9},{9,8},{10,11... | collective-permute-start | bytes 2359304 | tf_op jit(solution)/shard_map/ppermute | solution.py:486
  294.6 16.9 %collective-permute-start.33 = (f32[48,16,128]{2,1,0:T(8,128)S(1)}, f32[48,16,128]{2,1,0:T(8,128)S(1)}, u32[]{:S(2)}, u32[]{:S(2)}) collective-permute-start(f32[48,16,128]{2,1,0:T(8,128)S(1)} %slice_select_fusion), channel_id=1, source_target_pairs={{0,4},{4,0},{8,12},{12,8},{16,20},{20,16},{24,28},{28,24},{1,5},{5... | collective-permute-start | bytes 1179656 | tf_op jit(solution)/shard_map/ppermute | solution.py:486
  298.4 49.0 %collective-permute-start.37 = (f32[2,128,768]{2,1,0:T(8,128)}, f32[2,128,768]{2,1,0:T(8,128)}, u32[]{:S(2)}, u32[]{:S(2)}) collective-permute-start(f32[2,128,768]{2,1,0:T(8,128)} %split.95), channel_id=1, source_target_pairs={{0,1},{1,0},{2,3},{3,2},{4,5},{5,4},{6,7},{7,6},{8,9},{9,8},{10,11... | collective-permute-start | bytes 2359304 | tf_op jit(solution)/shard_map/ppermute | solution.py:486
  300.0 19.9 %collective-permute-start.32 = (f32[2,128,768]{2,1,0:T(8,128)S(1)}, f32[2,128,768]{2,1,0:T(8,128)S(1)}, u32[]{:S(2)}, u32[]{:S(2)}) collective-permute-start(f32[2,128,768]{2,1,0:T(8,128)S(1)} %slice_add_fusion.5), channel_id=1, source_target_pairs={{0,2},{1,3},{2,0},{3,1},{4,6},{5,7},{6,4},{7,5},{8,10},{9,11},{10,... | collective-permute-start | bytes 2359304 | tf_op jit(solution)/shard_map/ppermute | solution.py:486
  311.6 18.7 %collective-permute-start.34 = (f32[48,16,128]{2,1,0:T(8,128)S(1)}, f32[48,16,128]{2,1,0:T(8,128)S(1)}, u32[]{:S(2)}, u32[]{:S(2)}) collective-permute-start(f32[48,16,128]{2,1,0:T(8,128)S(1)} %select_add_fusion), channel_id=1, source_target_pairs={{8,0},{12,4},{16,8},{20,12},{24,16},{28,20},{9,1},{13,5},{17,9},{2... | collective-permute-start | bytes 1179656 | tf_op jit(solution)/shard_map/ppermute | solution.py:482
  330.3 23.6 %collective-permute-start.35 = (f32[2,128,768]{2,1,0:T(8,128)}, f32[2,128,768]{2,1,0:T(8,128)}, u32[]{:S(2)}, u32[]{:S(2)}) collective-permute-start(f32[2,128,768]{2,1,0:T(8,128)} %slice_add_fusion.6), channel_id=1, source_target_pairs={{0,2},{1,3},{2,0},{3,1},{4,6},{5,7},{6,4},{7,5},{8,10},{9,11},{10,... | collective-permute-start | bytes 2359304 | tf_op jit(solution)/shard_map/ppermute | solution.py:486
  332.5 21.5 %collective-permute-start.38 = (f32[48,16,128]{2,1,0:T(8,128)}, f32[48,16,128]{2,1,0:T(8,128)}, u32[]{:S(2)}, u32[]{:S(2)}) collective-permute-start(f32[48,16,128]{2,1,0:T(8,128)} %multiply_add_fusion.2), channel_id=1, source_target_pairs={{16,0},{20,4},{24,8},{28,12},{17,1},{21,5},{25,9},{29,13},{18,2},{... | collective-permute-start | bytes 1179656 | tf_op jit(solution)/shard_map/ppermute | solution.py:482
  336.1 23.9 %collective-permute-start.27 = (f32[2,128,768]{2,1,0:T(8,128)}, f32[2,128,768]{2,1,0:T(8,128)}, u32[]{:S(2)}, u32[]{:S(2)}) collective-permute-start(f32[2,128,768]{2,1,0:T(8,128)} %split.89), channel_id=1, source_target_pairs={{0,1},{1,0},{2,3},{3,2},{4,5},{5,4},{6,7},{7,6},{8,9},{9,8},{10,11... | collective-permute-start | bytes 2359304 | tf_op jit(solution)/shard_map/ppermute | solution.py:486
  353.9 21.4 %collective-permute-start.39 = (f32[2,128,768]{2,1,0:T(8,128)}, f32[2,128,768]{2,1,0:T(8,128)}, u32[]{:S(2)}, u32[]{:S(2)}) collective-permute-start(f32[2,128,768]{2,1,0:T(8,128)} %add_select_fusion.refs_0_), channel_id=1, source_target_pairs={{0,2},{1,3},{2,0},{3,1},{4,6},{5,7},{6,4},{7,5},{8,10},{9,11},{10,... | collective-permute-start | bytes 2359304 | tf_op jit(solution)/shard_map/ppermute | solution.py:486
  359.3 16.0 %collective-permute-start.40 = (f32[48,16,128]{2,1,0:T(8,128)S(1)}, f32[48,16,128]{2,1,0:T(8,128)S(1)}, u32[]{:S(2)}, u32[]{:S(2)}) collective-permute-start(f32[48,16,128]{2,1,0:T(8,128)S(1)} %fusion.121), channel_id=1, source_target_pairs={{0,4},{4,0},{8,12},{12,8},{16,20},{20,16},{24,28},{28,24},{1,5},{5... | collective-permute-start | bytes 1179656 | tf_op jit(solution)/shard_map/ppermute | solution.py:486
  377.9 21.1 %collective-permute-start.41 = (f32[2,128,768]{2,1,0:T(8,128)}, f32[2,128,768]{2,1,0:T(8,128)S(1)}, u32[]{:S(2)}, u32[]{:S(2)}) collective-permute-start(f32[2,128,768]{2,1,0:T(8,128)} %add_select_fusion.1.refs_0_), channel_id=1, source_target_pairs={{0,2},{1,3},{2,0},{3,1},{4,6},{5,7},{6,4},{7,5},{8,10},{9,11},{10,... | collective-permute-start | bytes 2359304 | tf_op jit(solution)/shard_map/ppermute | solution.py:486
  379.7 19.2 %collective-permute-start.46 = (f32[192,768]{1,0:T(8,128)S(1)}, f32[192,768]{1,0:T(8,128)S(1)}, u32[]{:S(2)}, u32[]{:S(2)}) collective-permute-start(f32[192,768]{1,0:T(8,128)S(1)} %constant_dynamic-slice_fusion.7), channel_id=1, source_target_pairs={{0,4},{4,0},{8,12},{12,8},{16,20},{20,16},{24,28},{28,24},{1,5},{5... | collective-permute-start | bytes 1769480 | tf_op jit(solution)/shard_map/ppermute | solution.py:486
  380.7 42.9 %collective-permute-start.43 = (f32[2,128,768]{2,1,0:T(8,128)S(1)}, f32[2,128,768]{2,1,0:T(8,128)}, u32[]{:S(2)}, u32[]{:S(2)}) collective-permute-start(f32[2,128,768]{2,1,0:T(8,128)S(1)} %copy-done.25), channel_id=1, source_target_pairs={{0,1},{1,0},{2,3},{3,2},{4,5},{5,4},{6,7},{7,6},{8,9},{9,8},{10,11... | collective-permute-start | bytes 2359304 | tf_op jit(solution)/shard_map/ppermute | solution.py:486
  380.7 48.2 %collective-permute-start.36 = (f32[2,128,768]{2,1,0:T(8,128)}, f32[2,128,768]{2,1,0:T(8,128)}, u32[]{:S(2)}, u32[]{:S(2)}) collective-permute-start(f32[2,128,768]{2,1,0:T(8,128)} %add_select_fusion.1.refs_0_), channel_id=1, source_target_pairs={{0,1},{1,0},{2,3},{3,2},{4,5},{5,4},{6,7},{7,6},{8,9},{9,8},{10,11... | collective-permute-start | bytes 2359304 | tf_op jit(solution)/shard_map/ppermute | solution.py:486
  389.6 9.4 %collective-permute-start.45 = (f32[192,128]{1,0:T(8,128)}, f32[192,128]{1,0:T(8,128)S(1)}, u32[]{:S(2)}, u32[]{:S(2)}) collective-permute-start(f32[192,128]{1,0:T(8,128)} %get-tuple-element.179), channel_id=1, source_target_pairs={{4,0},{8,4},{12,8},{16,12},{20,16},{24,20},{28,24},{5,1},{9,5},{13... | collective-permute-start | bytes 294920 | tf_op jit(solution)/shard_map/ppermute | solution.py:482
  415.1 17.3 %collective-permute-start.44 = (f32[2,128,768]{2,1,0:T(8,128)}, f32[2,128,768]{2,1,0:T(8,128)}, u32[]{:S(2)}, u32[]{:S(2)}) collective-permute-start(f32[2,128,768]{2,1,0:T(8,128)} %collective-permute-done.39.refs_2_), channel_id=1, source_target_pairs={{0,1},{1,0},{2,3},{3,2},{4,5},{5,4},{6,7},{7,6},{8,9},{9,8},{10,11... | collective-permute-start | bytes 2359304 | tf_op jit(solution)/shard_map/ppermute | solution.py:486
  415.7 18.4 %collective-permute-start.48 = (f32[2,128,768]{2,1,0:T(8,128)}, f32[2,128,768]{2,1,0:T(8,128)}, u32[]{:S(2)}, u32[]{:S(2)}) collective-permute-start(f32[2,128,768]{2,1,0:T(8,128)} %get-tuple-element.187), channel_id=1, source_target_pairs={{0,1},{1,0},{2,3},{3,2},{4,5},{5,4},{6,7},{7,6},{8,9},{9,8},{10,11... | collective-permute-start | bytes 2359304 | tf_op jit(solution)/shard_map/ppermute | solution.py:486
  417.4 15.1 %collective-permute-start.42 = (f32[2,128,768]{2,1,0:T(8,128)}, f32[2,128,768]{2,1,0:T(8,128)S(1)}, u32[]{:S(2)}, u32[]{:S(2)}) collective-permute-start(f32[2,128,768]{2,1,0:T(8,128)} %copy-done.38), channel_id=1, source_target_pairs={{0,1},{1,0},{2,3},{3,2},{4,5},{5,4},{6,7},{7,6},{8,9},{9,8},{10,11... | collective-permute-start | bytes 2359304 | tf_op jit(solution)/shard_map/ppermute | solution.py:486
  423.7 13.4 %collective-permute-start.50 = (f32[48,768]{1,0:T(8,128)S(1)}, f32[48,768]{1,0:T(8,128)S(1)}, u32[]{:S(2)}, u32[]{:S(2)}) collective-permute-start(f32[48,768]{1,0:T(8,128)S(1)} %get-tuple-element.191), channel_id=1, source_target_pairs={{0,8},{4,12},{8,0},{12,4},{16,24},{20,28},{24,16},{28,20},{1,9},{5... | collective-permute-start | bytes 442376 | tf_op jit(solution)/shard_map/ppermute | solution.py:486
  429.0 22.2 %collective-permute-start.53 = (f32[224,768]{1,0:T(8,128)}, f32[224,768]{1,0:T(8,128)}, u32[]{:S(2)}, u32[]{:S(2)}) collective-permute-start(f32[224,768]{1,0:T(8,128)} %constant_dynamic-slice_fusion.3), channel_id=1, source_target_pairs={{0,4},{4,0},{8,12},{12,8},{16,20},{20,16},{24,28},{28,24},{1,5},{5... | collective-permute-start | bytes 2064392 | tf_op jit(solution)/shard_map/ppermute | solution.py:486
  432.4 25.8 %collective-permute-start.60 = (f32[2,128,768]{2,1,0:T(8,128)}, f32[2,128,768]{2,1,0:T(8,128)}, u32[]{:S(2)}, u32[]{:S(2)}) collective-permute-start(f32[2,128,768]{2,1,0:T(8,128)} %get-tuple-element.208), channel_id=1, source_target_pairs={{0,1},{1,0},{2,3},{3,2},{4,5},{5,4},{6,7},{7,6},{8,9},{9,8},{10,11... | collective-permute-start | bytes 2359304 | tf_op jit(solution)/shard_map/ppermute | solution.py:486
  432.5 21.2 %collective-permute-start.54 = (f32[2,128,768]{2,1,0:T(8,128)}, f32[2,128,768]{2,1,0:T(8,128)}, u32[]{:S(2)}, u32[]{:S(2)}) collective-permute-start(f32[2,128,768]{2,1,0:T(8,128)} %add.453), channel_id=1, source_target_pairs={{0,2},{1,3},{2,0},{3,1},{4,6},{5,7},{6,4},{7,5},{8,10},{9,11},{10,... | collective-permute-start | bytes 2359304 | tf_op jit(solution)/shard_map/ppermute | solution.py:486
  434.1 16.9 %collective-permute-start.51 = (f32[48,768]{1,0:T(8,128)S(1)}, f32[48,768]{1,0:T(8,128)S(1)}, u32[]{:S(2)}, u32[]{:S(2)}) collective-permute-start(f32[48,768]{1,0:T(8,128)S(1)} %get-tuple-element.192), channel_id=1, source_target_pairs={{0,16},{4,20},{8,24},{12,28},{16,0},{20,4},{24,8},{28,12},{1,17},{... | collective-permute-start | bytes 442376 | tf_op jit(solution)/shard_map/ppermute | solution.py:486
  437.1 14.0 %collective-permute-start.52 = (f32[48,768]{1,0:T(8,128)S(1)}, f32[48,768]{1,0:T(8,128)S(1)}, u32[]{:S(2)}, u32[]{:S(2)}) collective-permute-start(f32[48,768]{1,0:T(8,128)S(1)} %get-tuple-element.193), channel_id=1, source_target_pairs={{0,24},{4,28},{8,16},{12,20},{16,8},{20,12},{24,0},{28,4},{1,25},{... | collective-permute-start | bytes 442376 | tf_op jit(solution)/shard_map/ppermute | solution.py:486
  451.0 14.5 %collective-permute-start.47 = (f32[2,128,768]{2,1,0:T(8,128)}, f32[2,128,768]{2,1,0:T(8,128)S(1)}, u32[]{:S(2)}, u32[]{:S(2)}) collective-permute-start(f32[2,128,768]{2,1,0:T(8,128)} %get-tuple-element.185), channel_id=1, source_target_pairs={{0,1},{1,0},{2,3},{3,2},{4,5},{5,4},{6,7},{7,6},{8,9},{9,8},{10,11... | collective-permute-start | bytes 2359304 | tf_op jit(solution)/shard_map/ppermute | solution.py:486
  453.7 20.2 %collective-permute-start.55 = (f32[2,128,768]{2,1,0:T(8,128)S(1)}, f32[2,128,768]{2,1,0:T(8,128)S(1)}, u32[]{:S(2)}, u32[]{:S(2)}) collective-permute-start(f32[2,128,768]{2,1,0:T(8,128)S(1)} %copy-done.45), channel_id=1, source_target_pairs={{0,2},{1,3},{2,0},{3,1},{4,6},{5,7},{6,4},{7,5},{8,10},{9,11},{10,... | collective-permute-start | bytes 2359304 | tf_op jit(solution)/shard_map/ppermute | solution.py:486
  456.8 21.2 %collective-permute-start.62 = (f32[48,768]{1,0:T(8,128)S(1)}, f32[48,768]{1,0:T(8,128)S(1)}, u32[]{:S(2)}, u32[]{:S(2)}) collective-permute-start(f32[48,768]{1,0:T(8,128)S(1)} %get-tuple-element.209), channel_id=1, source_target_pairs={{0,16},{4,20},{8,24},{12,28},{16,0},{20,4},{24,8},{28,12},{1,17},{... | collective-permute-start | bytes 442376 | tf_op jit(solution)/shard_map/ppermute | solution.py:486
  458.2 19.8 %collective-permute-start.63 = (f32[48,768]{1,0:T(8,128)S(1)}, f32[48,768]{1,0:T(8,128)S(1)}, u32[]{:S(2)}, u32[]{:S(2)}) collective-permute-start(f32[48,768]{1,0:T(8,128)S(1)} %get-tuple-element.209), channel_id=1, source_target_pairs={{0,24},{4,28},{8,16},{12,20},{16,8},{20,12},{24,0},{28,4},{1,25},{... | collective-permute-start | bytes 442376 | tf_op jit(solution)/shard_map/ppermute | solution.py:486
  463.7 14.3 %collective-permute-start.59 = (f32[56,768]{1,0:T(8,128)S(1)}, f32[56,768]{1,0:T(8,128)S(1)}, u32[]{:S(2)}, u32[]{:S(2)}) collective-permute-start(f32[56,768]{1,0:T(8,128)S(1)} %get-tuple-element.206), channel_id=1, source_target_pairs={{0,24},{4,28},{8,16},{12,20},{16,8},{20,12},{24,0},{28,4},{1,25},{... | collective-permute-start | bytes 516104 | tf_op jit(solution)/shard_map/ppermute | solution.py:486
  465.6 21.3 %collective-permute-start.58 = (f32[56,768]{1,0:T(8,128)S(1)}, f32[56,768]{1,0:T(8,128)S(1)}, u32[]{:S(2)}, u32[]{:S(2)}) collective-permute-start(f32[56,768]{1,0:T(8,128)S(1)} %get-tuple-element.205), channel_id=1, source_target_pairs={{0,16},{4,20},{8,24},{12,28},{16,0},{20,4},{24,8},{28,12},{1,17},{... | collective-permute-start | bytes 516104 | tf_op jit(solution)/shard_map/ppermute | solution.py:486
  473.9 12.9 %collective-permute-start.57 = (f32[56,768]{1,0:T(8,128)S(1)}, f32[56,768]{1,0:T(8,128)S(1)}, u32[]{:S(2)}, u32[]{:S(2)}) collective-permute-start(f32[56,768]{1,0:T(8,128)S(1)} %get-tuple-element.204), channel_id=1, source_target_pairs={{0,8},{4,12},{8,0},{12,4},{16,24},{20,28},{24,16},{28,20},{1,9},{5... | collective-permute-start | bytes 516104 | tf_op jit(solution)/shard_map/ppermute | solution.py:486
  486.8 18.4 %collective-permute-start.68 = (f32[2,128,768]{2,1,0:T(8,128)}, f32[2,128,768]{2,1,0:T(8,128)}, u32[]{:S(2)}, u32[]{:S(2)}) collective-permute-start(f32[2,128,768]{2,1,0:T(8,128)} %get-tuple-element.210.refs_0_), channel_id=1, source_target_pairs={{0,2},{1,3},{2,0},{3,1},{4,6},{5,7},{6,4},{7,5},{8,10},{9,11},{10,... | collective-permute-start | bytes 2359304 | tf_op jit(solution)/shard_map/ppermute | solution.py:486
  488.9 7.2 %collective-permute-start.64 = (f32[56,768]{1,0:T(8,128)S(1)}, f32[56,768]{1,0:T(8,128)S(1)}, u32[]{:S(2)}, u32[]{:S(2)}) collective-permute-start(f32[56,768]{1,0:T(8,128)S(1)} %get-tuple-element.211), channel_id=1, source_target_pairs={{0,8},{4,12},{8,0},{12,4},{16,24},{20,28},{24,16},{28,20},{1,9},{5... | collective-permute-start | bytes 516104 | tf_op jit(solution)/shard_map/ppermute | solution.py:486
  488.9 15.0 %collective-permute-start.65 = (f32[56,768]{1,0:T(8,128)S(1)}, f32[56,768]{1,0:T(8,128)S(1)}, u32[]{:S(2)}, u32[]{:S(2)}) collective-permute-start(f32[56,768]{1,0:T(8,128)S(1)} %get-tuple-element.211), channel_id=1, source_target_pairs={{0,16},{4,20},{8,24},{12,28},{16,0},{20,4},{24,8},{28,12},{1,17},{... | collective-permute-start | bytes 516104 | tf_op jit(solution)/shard_map/ppermute | solution.py:486
  491.1 13.5 %collective-permute-start.66 = (f32[56,768]{1,0:T(8,128)S(1)}, f32[56,768]{1,0:T(8,128)S(1)}, u32[]{:S(2)}, u32[]{:S(2)}) collective-permute-start(f32[56,768]{1,0:T(8,128)S(1)} %get-tuple-element.211), channel_id=1, source_target_pairs={{0,24},{4,28},{8,16},{12,20},{16,8},{20,12},{24,0},{28,4},{1,25},{... | collective-permute-start | bytes 516104 | tf_op jit(solution)/shard_map/ppermute | solution.py:486
  493.4 24.3 %collective-permute-start.70 = (f32[2,128,768]{2,1,0:T(8,128)}, f32[2,128,768]{2,1,0:T(8,128)}, u32[]{:S(2)}, u32[]{:S(2)}) collective-permute-start(f32[2,128,768]{2,1,0:T(8,128)} %get-tuple-element.210.refs_0_), channel_id=1, source_target_pairs={{0,1},{1,0},{2,3},{3,2},{4,5},{5,4},{6,7},{7,6},{8,9},{9,8},{10,11... | collective-permute-start | bytes 2359304 | tf_op jit(solution)/shard_map/ppermute | solution.py:486
  496.1 15.1 %collective-permute-start.67 = (f32[192,768]{1,0:T(8,128)S(1)}, f32[192,768]{1,0:T(8,128)S(1)}, u32[]{:S(2)}, u32[]{:S(2)}) collective-permute-start(f32[192,768]{1,0:T(8,128)S(1)} %constant_dynamic-update-slice_fusion.8), channel_id=1, source_target_pairs={{0,4},{4,0},{8,12},{12,8},{16,20},{20,16},{24,28},{28,24},{1,5},{5... | collective-permute-start | bytes 1769480 | tf_op jit(solution)/shard_map/ppermute | solution.py:486
  505.3 12.4 %collective-permute-start.71 = (f32[2,128,768]{2,1,0:T(8,128)}, f32[2,128,768]{2,1,0:T(8,128)}, u32[]{:S(2)}, u32[]{:S(2)}) collective-permute-start(f32[2,128,768]{2,1,0:T(8,128)} %collective-permute-done.68.refs_2_), channel_id=1, source_target_pairs={{0,1},{1,0},{2,3},{3,2},{4,5},{5,4},{6,7},{7,6},{8,9},{9,8},{10,11... | collective-permute-start | bytes 2359304 | tf_op jit(solution)/shard_map/ppermute | solution.py:486
  511.2 18.7 %collective-permute-start.73 = (f32[224,768]{1,0:T(8,128)}, f32[224,768]{1,0:T(8,128)}, u32[]{:S(2)}, u32[]{:S(2)}) collective-permute-start(f32[224,768]{1,0:T(8,128)} %constant_dynamic-update-slice_fusion.4), channel_id=1, source_target_pairs={{0,4},{4,0},{8,12},{12,8},{16,20},{20,16},{24,28},{28,24},{1,5},{5... | collective-permute-start | bytes 2064392 | tf_op jit(solution)/shard_map/ppermute | solution.py:486
  513.5 19.8 %collective-permute-start.69 = (f32[2,128,768]{2,1,0:T(8,128)S(1)}, f32[2,128,768]{2,1,0:T(8,128)}, u32[]{:S(2)}, u32[]{:S(2)}) collective-permute-start(f32[2,128,768]{2,1,0:T(8,128)S(1)} %get-tuple-element.214.refs_0_), channel_id=1, source_target_pairs={{0,2},{1,3},{2,0},{3,1},{4,6},{5,7},{6,4},{7,5},{8,10},{9,11},{10,... | collective-permute-start | bytes 2359304 | tf_op jit(solution)/shard_map/ppermute | solution.py:486
  515.1 25.6 %collective-permute-start.56 = (f32[2,128,768]{2,1,0:T(8,128)S(1)}, f32[2,128,768]{2,1,0:T(8,128)}, u32[]{:S(2)}, u32[]{:S(2)}) collective-permute-start(f32[2,128,768]{2,1,0:T(8,128)S(1)} %get-tuple-element.214.refs_0_), channel_id=1, source_target_pairs={{0,1},{1,0},{2,3},{3,2},{4,5},{5,4},{6,7},{7,6},{8,9},{9,8},{10,11... | collective-permute-start | bytes 2359304 | tf_op jit(solution)/shard_map/ppermute | solution.py:486
  533.3 7.4 %collective-permute-start.72 = (f32[2,128,768]{2,1,0:T(8,128)}, f32[2,128,768]{2,1,0:T(8,128)}, u32[]{:S(2)}, u32[]{:S(2)}) collective-permute-start(f32[2,128,768]{2,1,0:T(8,128)} %collective-permute-done.69.refs_2_), channel_id=1, source_target_pairs={{0,1},{1,0},{2,3},{3,2},{4,5},{5,4},{6,7},{7,6},{8,9},{9,8},{10,11... | collective-permute-start | bytes 2359304 | tf_op jit(solution)/shard_map/ppermute | solution.py:486
  (95 other events, 941.4 us)
Sparse Core Ops, SparseCore 0:
  209.5 109.3 reduce-scatter.1
  355.1 84.2 all-gather.1

commit v5 on v4

--- a/solution.py
+++ b/solution.py
@@ -698,7 +698,9 @@
         hidden = hidden.astype(BF)
         d_hidden = product("btd,fd->btf", d_out, down_weight)
         d_up = pull(d_hidden)[0].astype(BF)
-        return hidden, d_up, product("btf,df->btd", d_up, up_weight)
+        return hidden, d_up, [
+            product("btf,df->btd", rows, up_weight) for rows in jnp.split(d_up, 2, axis=0)
+        ]
 
     def scaled(*two):
         return (jnp.concatenate(two, axis=0) * second_gain).astype(BF)
@@ -737,7 +739,10 @@
             link.last = (far,)
         sums.append((far_total(fed[2 * u][2]), far))
     early = lax.psum_scatter(early, "seq", scatter_dimension=0, tiled=True)
-    lowered = [product("btf,fd->btd", hidden, down_weight) for hidden in hiddens]
+    lowered = [
+        [product("btf,fd->btd", rows, down_weight) for rows in jnp.split(hidden, 2, axis=0)]
+        for hidden in hiddens
+    ]
     grad_second = 0.0
     d_norms = []
     lows = []

time: 558 us -> 554 us (level)
  starting transfers between devices: 78.7 us -> 70.5 us
  waiting for transfers between devices: 223 us -> 231 us
  local copies, waits for them, and re-layouts: 48.2 us -> 40.3 us
    split x12 -> x4, local copies, waits for them, and re-layouts: 11 us -> 2.16 us  [far_total(): jnp.split(part, 2, axis=0)]
    ppermute x70, waiting for transfers between devices: 188 us -> 196 us  [swapped(): lax.ppermute(x, axis, [(i, i ^ bit) for i in range(lax.axis_size(axis))])]
    ppermute x70, starting transfers between devices: 59.8 us -> 51.7 us  [swapped(): lax.ppermute(x, axis, [(i, i ^ bit) for i in range(lax.axis_size(axis))])]
    dot_general x26 -> x34, matrix products: 39.2 us -> 44.2 us  [product(): return jnp.einsum(form, left, right, preferred_element_type=F32)]
    unnamed x168 -> x182, local copies, waits for them, and re-layouts: 12.6 us -> 11.6 us
  transfers between devices with their start and end apart: 78 -> 78, of which waited for: 34 -> 35; matrix products, arithmetic and copies ran while one was open for 22% -> 22% of each run, Pallas kernels for 10% -> 10%
where the time goes in v5:
time: 554 us; the launch traced here: 548 us
  waiting for transfers between devices  231 us (42%)
  Pallas kernels  90.6 us (16%)
  starting transfers between devices  70.5 us (13%)
  other arithmetic  55.5 us (10%)
  matrix products  44.2 us (8%)
  local copies, waits for them, and re-layouts  40.3 us (7%)
  between operations  15.9 us (3%)
    ppermute x70, waiting for transfers between devices, swapped(): lax.ppermute(x, axis, [(i, i ^ bit) for i in range(lax.axis_size(axis))])  196 us
    ppermute x70, starting transfers between devices, swapped(): lax.ppermute(x, axis, [(i, i ^ bit) for i in range(lax.axis_size(axis))])  51.7 us
    pallas_call x5, Pallas kernels, call(): pl.pallas_call(kernel, grid=(channels // GROUP,), in_specs=ins, out_specs...  44.3 us
    dot_general x34, matrix products, product(): return jnp.einsum(form, left, right, preferred_element_type=F32)  44.2 us
    ppermute x6, waiting for transfers between devices, passed_along(): return lax.ppermute(x, axis, pairs)  35.3 us
    pallas_call x4, Pallas kernels, place_call(): pl.pallas_call(functools.partial(place_kernel, count=count), grid_spec=pl...  19.1 us
    ppermute x6, starting transfers between devices, passed_along(): return lax.ppermute(x, axis, pairs)  18.5 us
    pallas_call x1, Pallas kernels, last_call(): pl.pallas_call(last_kernel, grid=(pieces,), in_specs=[act, act, act, pl.B...  14.8 us
  transfers between devices with their start and end apart: 78, of which 35 were waited for; matrix products, arithmetic and copies ran while one was open for 22% of the time, Pallas kernels for 10%

profile of v5, /device:TPU:0, one launch (start us, length us, event | category | flops | bytes accessed | tf_op | source)
XLA Modules:
  0.0 548.2 jit_solution(13905706643533671235)
XLA Ops:
  9.8 12.4 %shard_map.254 = (bf16[16,128,768]{2,1,0:T(8,128)(2,1)}, bf16[16,128,768]{2,1,0:T(8,128)(2,1)}, f32[16,192,128]{2,1,0:T(8,128)}, f32[16,192,128]{2,1,0:T(8,128)}...) custom-call(s32[18]{0:T(128)} %pad_add_fusion.1.at_ref, bf16[16,128,768]{2,1,0:T(8,128)(2,1)} %x_ref.1, ...), custom_call_target="tpu_custom_call" | custom-call | tf_op jit(solution)/shard_map/pallas_call | solution.py:318
  22.2 4.9 collective-permute-start
  27.3 4.6 multiply_reduce_fusion.kern_ref
  34.1 10.7 %shard_map.255 = (f32[16,192,128]{2,1,0:T(8,128)}, f32[16,192,128]{2,1,0:T(8,128)}, f32[96,16,128]{2,1,0:T(8,128)}) custom-call(f32[16,192,128]{2,1,0:T(8,128)} %get-tuple-element.124.k_ref, f32[16,192,128]{2,1,0:T(8,128)} %get-tuple-element.125.v_ref, f32[192,128]{1,0:T(8,128)} %copy-done.66, f32[192,4]{1,0:T(8,128)} %bitcast.140, ...), custom_call_target="tpu_custom_call" | custom-call | tf_op jit(solution)/shard_map/pallas_call | solution.py:423
  48.3 8.5 %collective-permute-done.1 = f32[48,16,128]{2,1,0:T(8,128)S(1)} collective-permute-done((f32[48,16,128]{2,1,0:T(8,128)S(1)}, f32[48,16,128]{2,1,0:T(8,128)S(1)}, u32[]{:S(2)}, u32[]{:S(2)}) %collective-permute-start.1) | collective-permute-done | bytes 393248 | tf_op jit(solution)/shard_map/ppermute | solution.py:486
  56.8 3.5 collective-permute-start.2
  60.4 7.2 %collective-permute-done.2 = f32[48,16,128]{2,1,0:T(8,128)S(1)} collective-permute-done((f32[48,16,128]{2,1,0:T(8,128)S(1)}, f32[48,16,128]{2,1,0:T(8,128)S(1)}, u32[]{:S(2)}, u32[]{:S(2)}) %collective-permute-start.2) | collective-permute-done | bytes 393248 | tf_op jit(solution)/shard_map/ppermute | solution.py:482
  67.7 5.4 collective-permute-start.3
  73.1 6.3 %collective-permute-done.3 = f32[48,16,128]{2,1,0:T(8,128)S(1)} collective-permute-done((f32[48,16,128]{2,1,0:T(8,128)S(1)}, f32[48,16,128]{2,1,0:T(8,128)S(1)}, u32[]{:S(2)}, u32[]{:S(2)}) %collective-permute-start.3) | collective-permute-done | bytes 393248 | tf_op jit(solution)/shard_map/ppermute | solution.py:482
  83.3 5.1 collective-permute-done.4
  89.8 6.5 %shard_map.256 = (f32[16,192,128]{2,1,0:T(8,128)}, bf16[16,192,128]{2,1,0:T(8,128)(2,1)}) custom-call(f32[16,192,128]{2,1,0:T(8,128)} %get-tuple-element.127.y_ref, f32[96,16,128]{2,1,0:T(8,128)} %pad_maximum_fusion.2.hin_ref, f32[96,128]{1,0:T(8,128)} %reshape.190.coef_ref, f32[96,128]{1,0:T(8,128)} %reshape.189.rate_ref, ...), custom_call_target="tpu_custom_call" | custom-call | tf_op jit(solution)/shard_map/pallas_call | solution.py:423
  106.4 13.6 %collective-permute-done.8 = f32[2,128,768]{2,1,0:T(8,128)S(1)} collective-permute-done((f32[2,128,768]{2,1,0:T(8,128)S(1)}, f32[2,128,768]{2,1,0:T(8,128)S(1)}, u32[]{:S(2)}, u32[]{:S(2)}) %collective-permute-start.8) | collective-permute-done | bytes 786464 | tf_op jit(solution)/shard_map/ppermute | solution.py:486
  123.2 15.8 %collective-permute-done.9 = f32[2,128,768]{2,1,0:T(8,128)} collective-permute-done((f32[2,128,768]{2,1,0:T(8,128)}, f32[2,128,768]{2,1,0:T(8,128)}, u32[]{:S(2)}, u32[]{:S(2)}) %collective-permute-start.9) | collective-permute-done | bytes 786464 | tf_op jit(solution)/shard_map/ppermute | solution.py:486
  139.1 3.5 fusion.131
  152.4 10.6 %collective-permute-done.13 = f32[2,128,768]{2,1,0:T(8,128)S(1)} collective-permute-done((f32[2,128,768]{2,1,0:T(8,128)S(1)}, f32[2,128,768]{2,1,0:T(8,128)S(1)}, u32[]{:S(2)}, u32[]{:S(2)}) %collective-permute-start.13) | collective-permute-done | bytes 786464 | tf_op jit(solution)/shard_map/ppermute | solution.py:486
  174.7 8.3 %collective-permute-done.10 = f32[2,128,768]{2,1,0:T(8,128)S(1)} collective-permute-done((f32[2,128,768]{2,1,0:T(8,128)S(1)}, f32[2,128,768]{2,1,0:T(8,128)S(1)}, u32[]{:S(2)}, u32[]{:S(2)}) %collective-permute-start.10) | collective-permute-done | bytes 786464 | tf_op jit(solution)/shard_map/ppermute | solution.py:486
  190.2 2.8 fusion.32
  193.1 2.8 fusion.29
  196.0 2.5 pad_maximum_fusion
  198.5 10.5 %collective-permute-done.20 = f32[2,128,768]{2,1,0:T(8,128)} collective-permute-done((f32[2,128,768]{2,1,0:T(8,128)}, f32[2,128,768]{2,1,0:T(8,128)}, u32[]{:S(2)}, u32[]{:S(2)}) %collective-permute-start.20) | collective-permute-done | bytes 786464 | tf_op jit(solution)/shard_map/ppermute | solution.py:486
  209.8 2.4 fusion.86
  222.4 15.3 %collective-permute-done.21 = f32[2,128,768]{2,1,0:T(8,128)S(1)} collective-permute-done((f32[2,128,768]{2,1,0:T(8,128)S(1)}, f32[2,128,768]{2,1,0:T(8,128)S(1)}, u32[]{:S(2)}, u32[]{:S(2)}) %collective-permute-start.21) | collective-permute-done | bytes 786464 | tf_op jit(solution)/shard_map/ppermute | solution.py:486
  242.5 14.8 %collective-permute-done.23 = f32[2,128,768]{2,1,0:T(8,128)S(1)} collective-permute-done((f32[2,128,768]{2,1,0:T(8,128)S(1)}, f32[2,128,768]{2,1,0:T(8,128)S(1)}, u32[]{:S(2)}, u32[]{:S(2)}) %collective-permute-start.23) | collective-permute-done | bytes 786464 | tf_op jit(solution)/shard_map/ppermute | solution.py:486
  263.4 15.2 %collective-permute-done.24 = f32[2,128,768]{2,1,0:T(8,128)} collective-permute-done((f32[2,128,768]{2,1,0:T(8,128)}, f32[2,128,768]{2,1,0:T(8,128)}, u32[]{:S(2)}, u32[]{:S(2)}) %collective-permute-start.24) | collective-permute-done | bytes 786464 | tf_op jit(solution)/shard_map/ppermute | solution.py:486
  281.3 2.7 fusion.24
  286.0 7.4 %shard_map.257 = (bf16[16,192,128]{2,1,0:T(8,128)(2,1)}, f32[16,192,128]{2,1,0:T(8,128)}, f32[16,192,128]{2,1,0:T(8,128)}, f32[96,16,128]{2,1,0:T(8,128)}) custom-call(f32[16,192,128]{2,1,0:T(8,128)} %pad_maximum_fusion.1.dg_ref, f32[16,192,128]{2,1,0:T(8,128)} %get-tuple-element.130.q_ref, f32[16,192,128]{2,1,0:T(8,128)} %get-tuple-element.171.state_ref, ...), custom_call_target="tpu_custom_call" | custom-call | tf_op jit(solution)/shard_map/pallas_call | solution.py:423
  293.4 2.3 slice_select_fusion
  301.6 9.5 %collective-permute-done.33 = f32[48,16,128]{2,1,0:T(8,128)S(1)} collective-permute-done((f32[48,16,128]{2,1,0:T(8,128)}, f32[48,16,128]{2,1,0:T(8,128)S(1)}, u32[]{:S(2)}, u32[]{:S(2)}) %collective-permute-start.33) | collective-permute-done | bytes 393248 | tf_op jit(solution)/shard_map/ppermute | solution.py:486
  312.9 2.1 add.432
  316.6 3.9 collective-permute-done.32
  320.5 10.4 %collective-permute-done.34 = f32[48,16,128]{2,1,0:T(8,128)S(1)} collective-permute-done((f32[48,16,128]{2,1,0:T(8,128)S(1)}, f32[48,16,128]{2,1,0:T(8,128)S(1)}, u32[]{:S(2)}, u32[]{:S(2)}) %collective-permute-start.34) | collective-permute-done | bytes 393248 | tf_op jit(solution)/shard_map/ppermute | solution.py:482
  335.0 11.3 %shard_map.258 = (f32[96,16,128]{2,1,0:T(8,128)}, f32[96,16,128]{2,1,0:T(8,128)}, f32[192,128]{1,0:T(8,128)}, f32[96,128]{1,0:T(8,128)}, f32[96,128]{1,0:T(8,128)}) custom-call(f32[16,192,128]{2,1,0:T(8,128)} %get-tuple-element.179.d_ref, f32[16,192,128]{2,1,0:T(8,128)} %get-tuple-element.129.mixed_ref, f32[96,128]{1,0:T(8,128)} %reshape.189.rate_ref), custom_call_target="tpu_custom_call" | custom-call | tf_op jit(solution)/shard_map/pallas_call | solution.py:423
  346.3 2.7 add_select_fusion.refs_0_
  349.0 4.5 collective-permute-done.38
  354.6 2.9 convolution_bitcast_fusion.2
  358.9 2.4 add_select_fusion.1.refs_0_
  361.3 9.0 %collective-permute-done.40 = f32[48,16,128]{2,1,0:T(8,128)S(1)} collective-permute-done((f32[48,16,128]{2,1,0:T(8,128)S(1)}, f32[48,16,128]{2,1,0:T(8,128)S(1)}, u32[]{:S(2)}, u32[]{:S(2)}) %collective-permute-start.40) | collective-permute-done | bytes 393248 | tf_op jit(solution)/shard_map/ppermute | solution.py:486
  377.0 8.4 %shard_map.261 = (bf16[16,192,128]{2,1,0:T(8,128)(2,1)}, f32[16,192,128]{2,1,0:T(8,128)}, f32[192,128]{1,0:T(8,128)}, f32[192,128]{1,0:T(8,128)}) custom-call(f32[16,192,128]{2,1,0:T(8,128)} %get-tuple-element.192.dx_ref, f32[96,16,128]{2,1,0:T(8,128)} %get-tuple-element.313.gin_ref, f32[96,128]{1,0:T(8,128)} %reshape.190.coef_ref, ...), custom_call_target="tpu_custom_call" | custom-call | tf_op jit(solution)/shard_map/pallas_call | solution.py:423
  387.0 6.9 %collective-permute-done.45.spill_ref = f32[192,128]{1,0:T(8,128)S(1)} collective-permute-done((f32[192,128]{1,0:T(8,128)}, f32[192,128]{1,0:T(8,128)S(1)}, u32[]{:S(2)}, u32[]{:S(2)}) %collective-permute-start.45) | collective-permute-done | bytes 98336 | tf_op jit(solution)/shard_map/ppermute | solution.py:482
  394.9 14.8 %shard_map.262 = (f32[2,128,768]{2,1,0:T(8,128)}, f32[2,128,768]{2,1,0:T(8,128)}, f32[2,128,768]{2,1,0:T(8,128)}, f32[2,128,768]{2,1,0:T(8,128)}, f32[2,128,768]...) custom-call(bf16[16,192,128]{2,1,0:T(8,128)(2,1)} %get-tuple-element, ...), custom_call_target="tpu_custom_call" | custom-call | tf_op jit(solution)/shard_map/pallas_call | solution.py:357
  414.1 2.1 constant_dynamic-slice_fusion.3
  416.2 2.3 add.453
  418.6 3.5 collective-permute-start.50
  422.1 2.3 collective-permute-start.53
  425.8 9.8 %collective-permute-done.50 = f32[48,768]{1,0:T(8,128)S(1)} collective-permute-done((f32[48,768]{1,0:T(8,128)S(1)}, f32[48,768]{1,0:T(8,128)S(1)}, u32[]{:S(2)}, u32[]{:S(2)}) %collective-permute-start.50) | collective-permute-done | bytes 147488 | tf_op jit(solution)/shard_map/ppermute | solution.py:486
  435.6 3.1 collective-permute-start.52
  438.7 4.8 shard_map.259.refs_4_
  443.5 2.1 add.448
  445.6 4.8 shard_map.260
  453.2 1.9 collective-permute-start.62
  455.2 2.5 collective-permute-start.63
  457.6 2.2 fusion.127
  460.4 1.8 collective-permute-start.59
  462.3 10.2 %collective-permute-done.55 = f32[2,128,768]{2,1,0:T(8,128)S(1)} collective-permute-done((f32[2,128,768]{2,1,0:T(8,128)S(1)}, f32[2,128,768]{2,1,0:T(8,128)S(1)}, u32[]{:S(2)}, u32[]{:S(2)}) %collective-permute-start.55) | collective-permute-done | bytes 786464 | tf_op jit(solution)/shard_map/ppermute | solution.py:486
  473.6 2.8 fusion.130
  476.5 7.6 %collective-permute-done.58 = f32[56,768]{1,0:T(8,128)S(1)} collective-permute-done((f32[56,768]{1,0:T(8,128)S(1)}, f32[56,768]{1,0:T(8,128)S(1)}, u32[]{:S(2)}, u32[]{:S(2)}) %collective-permute-start.58) | collective-permute-done | bytes 172064 | tf_op jit(solution)/shard_map/ppermute | solution.py:486
  487.4 2.1 collective-permute-start.65
  489.5 2.4 collective-permute-start.66
  491.9 2.7 collective-permute-done.64
  496.9 5.5 %collective-permute-done.65 = f32[56,768]{1,0:T(8,128)S(1)} collective-permute-done((f32[56,768]{1,0:T(8,128)S(1)}, f32[56,768]{1,0:T(8,128)S(1)}, u32[]{:S(2)}, u32[]{:S(2)}) %collective-permute-start.65) | collective-permute-done | bytes 172064 | tf_op jit(solution)/shard_map/ppermute | solution.py:486
  503.8 4.9 fusion.158
  513.1 4.7 shard_map.263.refs_4_
  517.8 9.0 %collective-permute-done.73 = f32[224,768]{1,0:T(8,128)} collective-permute-done((f32[224,768]{1,0:T(8,128)}, f32[224,768]{1,0:T(8,128)}, u32[]{:S(2)}, u32[]{:S(2)}) %collective-permute-start.73) | collective-permute-done | bytes 688160 | tf_op jit(solution)/shard_map/ppermute | solution.py:486
  536.4 4.8 shard_map.264
  (454 shorter events, 138.1 us)
Async XLA Ops:
  7.2 346.3 %reduce-scatter.2.cloned.1.call-start = ((), (), s32[]{:S(2)}) async-start(), calls=%async_computation.1 | async-start | bytes 5308416 | tf_op jit(solution)/shard_map/reduce_scatter | solution.py:741
  22.2 11.3 %collective-permute-start = (f32[192,128]{1,0:T(8,128)}, f32[192,128]{1,0:T(8,128)S(1)}, u32[]{:S(2)}, u32[]{:S(2)}) collective-permute-start(f32[192,128]{1,0:T(8,128)} %get-tuple-element.126), channel_id=1, source_target_pairs={{0,4},{4,8},{8,12},{12,16},{16,20},{20,24},{24,28},{1,5},{5,9},{9,... | collective-permute-start | bytes 294920 | tf_op jit(solution)/shard_map/ppermute | solution.py:482
  46.0 10.7 %collective-permute-start.1 = (f32[48,16,128]{2,1,0:T(8,128)S(1)}, f32[48,16,128]{2,1,0:T(8,128)S(1)}, u32[]{:S(2)}, u32[]{:S(2)}) collective-permute-start(f32[48,16,128]{2,1,0:T(8,128)S(1)} %slice_select_fusion.2), channel_id=1, source_target_pairs={{0,4},{4,0},{8,12},{12,8},{16,20},{20,16},{24,28},{28,24},{1,5},{5... | collective-permute-start | bytes 1179656 | tf_op jit(solution)/shard_map/ppermute | solution.py:486
  56.8 10.7 %collective-permute-start.2 = (f32[48,16,128]{2,1,0:T(8,128)S(1)}, f32[48,16,128]{2,1,0:T(8,128)S(1)}, u32[]{:S(2)}, u32[]{:S(2)}) collective-permute-start(f32[48,16,128]{2,1,0:T(8,128)S(1)} %get-tuple-element.297), channel_id=1, source_target_pairs={{0,8},{4,12},{8,16},{12,20},{16,24},{20,28},{1,9},{5,13},{9,17},{1... | collective-permute-start | bytes 1179656 | tf_op jit(solution)/shard_map/ppermute | solution.py:482
  67.7 11.8 %collective-permute-start.3 = (f32[48,16,128]{2,1,0:T(8,128)S(1)}, f32[48,16,128]{2,1,0:T(8,128)S(1)}, u32[]{:S(2)}, u32[]{:S(2)}) collective-permute-start(f32[48,16,128]{2,1,0:T(8,128)S(1)} %multiply_add_fusion.5), channel_id=1, source_target_pairs={{0,16},{4,20},{8,24},{12,28},{1,17},{5,21},{9,25},{13,29},{2,18},{... | collective-permute-start | bytes 1179656 | tf_op jit(solution)/shard_map/ppermute | solution.py:482
  80.3 8.2 %collective-permute-start.4 = (f32[48,16,128]{2,1,0:T(8,128)}, f32[48,16,128]{2,1,0:T(8,128)S(1)}, u32[]{:S(2)}, u32[]{:S(2)}) collective-permute-start(f32[48,16,128]{2,1,0:T(8,128)} %fusion.138), channel_id=1, source_target_pairs={{0,4},{4,0},{8,12},{12,8},{16,20},{20,16},{24,28},{28,24},{1,5},{5... | collective-permute-start | bytes 1179656 | tf_op jit(solution)/shard_map/ppermute | solution.py:486
  100.3 19.6 %collective-permute-start.8 = (f32[2,128,768]{2,1,0:T(8,128)S(1)}, f32[2,128,768]{2,1,0:T(8,128)S(1)}, u32[]{:S(2)}, u32[]{:S(2)}) collective-permute-start(f32[2,128,768]{2,1,0:T(8,128)S(1)} %slice_add_fusion.1), channel_id=1, source_target_pairs={{0,2},{1,3},{2,0},{3,1},{4,6},{5,7},{6,4},{7,5},{8,10},{9,11},{10,... | collective-permute-start | bytes 2359304 | tf_op jit(solution)/shard_map/ppermute | solution.py:486
  103.1 19.3 %collective-permute-start.5 = (f32[2,128,768]{2,1,0:T(8,128)}, f32[2,128,768]{2,1,0:T(8,128)S(1)}, u32[]{:S(2)}, u32[]{:S(2)}) collective-permute-start(f32[2,128,768]{2,1,0:T(8,128)} %split.97), channel_id=1, source_target_pairs={{0,1},{1,0},{2,3},{3,2},{4,5},{5,4},{6,7},{7,6},{8,9},{9,8},{10,11... | collective-permute-start | bytes 2359304 | tf_op jit(solution)/shard_map/ppermute | solution.py:486
  104.9 17.4 %collective-permute-start.12 = (f32[2,128,768]{2,1,0:T(8,128)}, f32[2,128,768]{2,1,0:T(8,128)}, u32[]{:S(2)}, u32[]{:S(2)}) collective-permute-start(f32[2,128,768]{2,1,0:T(8,128)} %split.103), channel_id=1, source_target_pairs={{0,1},{1,0},{2,3},{3,2},{4,5},{5,4},{6,7},{7,6},{8,9},{9,8},{10,11... | collective-permute-start | bytes 2359304 | tf_op jit(solution)/shard_map/ppermute | solution.py:486
  120.0 19.1 %collective-permute-start.9 = (f32[2,128,768]{2,1,0:T(8,128)}, f32[2,128,768]{2,1,0:T(8,128)}, u32[]{:S(2)}, u32[]{:S(2)}) collective-permute-start(f32[2,128,768]{2,1,0:T(8,128)} %slice_add_fusion.2), channel_id=1, source_target_pairs={{0,2},{1,3},{2,0},{3,1},{4,6},{5,7},{6,4},{7,5},{8,10},{9,11},{10,... | collective-permute-start | bytes 2359304 | tf_op jit(solution)/shard_map/ppermute | solution.py:486
  143.0 20.0 %collective-permute-start.13 = (f32[2,128,768]{2,1,0:T(8,128)S(1)}, f32[2,128,768]{2,1,0:T(8,128)S(1)}, u32[]{:S(2)}, u32[]{:S(2)}) collective-permute-start(f32[2,128,768]{2,1,0:T(8,128)S(1)} %subtract_multiply_fusion.2), channel_id=1, source_target_pairs={{0,2},{1,3},{2,0},{3,1},{4,6},{5,7},{6,4},{7,5},{8,10},{9,11},{10,... | collective-permute-start | bytes 2359304 | tf_op jit(solution)/shard_map/ppermute | solution.py:486
  144.7 19.5 %collective-permute-start.11 = (f32[2,128,768]{2,1,0:T(8,128)S(1)}, f32[2,128,768]{2,1,0:T(8,128)S(1)}, u32[]{:S(2)}, u32[]{:S(2)}) collective-permute-start(f32[2,128,768]{2,1,0:T(8,128)S(1)} %subtract_multiply_fusion.3), channel_id=1, source_target_pairs={{0,1},{1,0},{2,3},{3,2},{4,5},{5,4},{6,7},{7,6},{8,9},{9,8},{10,11... | collective-permute-start | bytes 2359304 | tf_op jit(solution)/shard_map/ppermute | solution.py:486
  163.0 20.0 %collective-permute-start.10 = (f32[2,128,768]{2,1,0:T(8,128)S(1)}, f32[2,128,768]{2,1,0:T(8,128)S(1)}, u32[]{:S(2)}, u32[]{:S(2)}) collective-permute-start(f32[2,128,768]{2,1,0:T(8,128)S(1)} %subtract_multiply_fusion.3), channel_id=1, source_target_pairs={{0,2},{1,3},{2,0},{3,1},{4,6},{5,7},{6,4},{7,5},{8,10},{9,11},{10,... | collective-permute-start | bytes 2359304 | tf_op jit(solution)/shard_map/ppermute | solution.py:486
  189.0 19.9 %collective-permute-start.20 = (f32[2,128,768]{2,1,0:T(8,128)}, f32[2,128,768]{2,1,0:T(8,128)}, u32[]{:S(2)}, u32[]{:S(2)}) collective-permute-start(f32[2,128,768]{2,1,0:T(8,128)} %add.426), channel_id=1, source_target_pairs={{0,2},{1,3},{2,0},{3,1},{4,6},{5,7},{6,4},{7,5},{8,10},{9,11},{10,... | collective-permute-start | bytes 2359304 | tf_op jit(solution)/shard_map/ppermute | solution.py:486
  209.0 294.8 %all-gather.2.cloned.1.call-start = ((), (), s32[]{:S(2)}) async-start(), calls=%async_computation.2 | async-start | bytes 5308416 | tf_op jit(solution)/shard_map/all_gather | solution.py:804
  209.2 13.2 %collective-permute-start.16 = (f32[2,128,768]{2,1,0:T(8,128)}, f32[2,128,768]{2,1,0:T(8,128)S(1)}, u32[]{:S(2)}, u32[]{:S(2)}) collective-permute-start(f32[2,128,768]{2,1,0:T(8,128)} %fusion.109), channel_id=1, source_target_pairs={{0,1},{1,0},{2,3},{3,2},{4,5},{5,4},{6,7},{7,6},{8,9},{9,8},{10,11... | collective-permute-start | bytes 2359304 | tf_op jit(solution)/shard_map/ppermute | solution.py:486
  209.3 11.4 %collective-permute-start.22 = (f32[2,128,768]{2,1,0:T(8,128)}, f32[2,128,768]{2,1,0:T(8,128)S(1)}, u32[]{:S(2)}, u32[]{:S(2)}) collective-permute-start(f32[2,128,768]{2,1,0:T(8,128)} %fusion.103), channel_id=1, source_target_pairs={{0,1},{1,0},{2,3},{3,2},{4,5},{5,4},{6,7},{7,6},{8,9},{9,8},{10,11... | collective-permute-start | bytes 2359304 | tf_op jit(solution)/shard_map/ppermute | solution.py:486
  218.1 19.6 %collective-permute-start.21 = (f32[2,128,768]{2,1,0:T(8,128)S(1)}, f32[2,128,768]{2,1,0:T(8,128)S(1)}, u32[]{:S(2)}, u32[]{:S(2)}) collective-permute-start(f32[2,128,768]{2,1,0:T(8,128)S(1)} %convolution_add_fusion), channel_id=1, source_target_pairs={{0,2},{1,3},{2,0},{3,1},{4,6},{5,7},{6,4},{7,5},{8,10},{9,11},{10,... | collective-permute-start | bytes 2359304 | tf_op jit(solution)/shard_map/ppermute | solution.py:486
  238.4 18.9 %collective-permute-start.23 = (f32[2,128,768]{2,1,0:T(8,128)S(1)}, f32[2,128,768]{2,1,0:T(8,128)S(1)}, u32[]{:S(2)}, u32[]{:S(2)}) collective-permute-start(f32[2,128,768]{2,1,0:T(8,128)S(1)} %get-tuple-element.161), channel_id=1, source_target_pairs={{0,2},{1,3},{2,0},{3,1},{4,6},{5,7},{6,4},{7,5},{8,10},{9,11},{10,... | collective-permute-start | bytes 2359304 | tf_op jit(solution)/shard_map/ppermute | solution.py:486
  242.5 18.7 %collective-permute-start.25 = (f32[2,128,768]{2,1,0:T(8,128)S(1)}, f32[2,128,768]{2,1,0:T(8,128)S(1)}, u32[]{:S(2)}, u32[]{:S(2)}) collective-permute-start(f32[2,128,768]{2,1,0:T(8,128)S(1)} %get-tuple-element.161), channel_id=1, source_target_pairs={{0,1},{1,0},{2,3},{3,2},{4,5},{5,4},{6,7},{7,6},{8,9},{9,8},{10,11... | collective-permute-start | bytes 2359304 | tf_op jit(solution)/shard_map/ppermute | solution.py:486
  258.4 20.3 %collective-permute-start.24 = (f32[2,128,768]{2,1,0:T(8,128)}, f32[2,128,768]{2,1,0:T(8,128)}, u32[]{:S(2)}, u32[]{:S(2)}) collective-permute-start(f32[2,128,768]{2,1,0:T(8,128)} %subtract_multiply_fusion.1), channel_id=1, source_target_pairs={{0,2},{1,3},{2,0},{3,1},{4,6},{5,7},{6,4},{7,5},{8,10},{9,11},{10,... | collective-permute-start | bytes 2359304 | tf_op jit(solution)/shard_map/ppermute | solution.py:486
  260.9 19.1 %collective-permute-start.30 = (f32[2,128,768]{2,1,0:T(8,128)}, f32[2,128,768]{2,1,0:T(8,128)}, u32[]{:S(2)}, u32[]{:S(2)}) collective-permute-start(f32[2,128,768]{2,1,0:T(8,128)} %subtract_multiply_fusion.1), channel_id=1, source_target_pairs={{0,1},{1,0},{2,3},{3,2},{4,5},{5,4},{6,7},{7,6},{8,9},{9,8},{10,11... | collective-permute-start | bytes 2359304 | tf_op jit(solution)/shard_map/ppermute | solution.py:486
  279.6 19.6 %collective-permute-start.29 = (f32[2,128,768]{2,1,0:T(8,128)}, f32[2,128,768]{2,1,0:T(8,128)}, u32[]{:S(2)}, u32[]{:S(2)}) collective-permute-start(f32[2,128,768]{2,1,0:T(8,128)} %fusion.80), channel_id=1, source_target_pairs={{0,1},{1,0},{2,3},{3,2},{4,5},{5,4},{6,7},{7,6},{8,9},{9,8},{10,11... | collective-permute-start | bytes 2359304 | tf_op jit(solution)/shard_map/ppermute | solution.py:486
  295.7 15.4 %collective-permute-start.33 = (f32[48,16,128]{2,1,0:T(8,128)}, f32[48,16,128]{2,1,0:T(8,128)S(1)}, u32[]{:S(2)}, u32[]{:S(2)}) collective-permute-start(f32[48,16,128]{2,1,0:T(8,128)} %slice_select_fusion), channel_id=1, source_target_pairs={{0,4},{4,0},{8,12},{12,8},{16,20},{20,16},{24,28},{28,24},{1,5},{5... | collective-permute-start | bytes 1179656 | tf_op jit(solution)/shard_map/ppermute | solution.py:486
  297.1 15.8 %collective-permute-start.28 = (f32[2,128,768]{2,1,0:T(8,128)}, f32[2,128,768]{2,1,0:T(8,128)}, u32[]{:S(2)}, u32[]{:S(2)}) collective-permute-start(f32[2,128,768]{2,1,0:T(8,128)} %fusion.72), channel_id=1, source_target_pairs={{0,1},{1,0},{2,3},{3,2},{4,5},{5,4},{6,7},{7,6},{8,9},{9,8},{10,11... | collective-permute-start | bytes 2359304 | tf_op jit(solution)/shard_map/ppermute | solution.py:486
  300.5 20.0 %collective-permute-start.32 = (f32[2,128,768]{2,1,0:T(8,128)S(1)}, f32[2,128,768]{2,1,0:T(8,128)S(1)}, u32[]{:S(2)}, u32[]{:S(2)}) collective-permute-start(f32[2,128,768]{2,1,0:T(8,128)S(1)} %add.433), channel_id=1, source_target_pairs={{0,2},{1,3},{2,0},{3,1},{4,6},{5,7},{6,4},{7,5},{8,10},{9,11},{10,... | collective-permute-start | bytes 2359304 | tf_op jit(solution)/shard_map/ppermute | solution.py:486
  311.2 19.7 %collective-permute-start.34 = (f32[48,16,128]{2,1,0:T(8,128)S(1)}, f32[48,16,128]{2,1,0:T(8,128)S(1)}, u32[]{:S(2)}, u32[]{:S(2)}) collective-permute-start(f32[48,16,128]{2,1,0:T(8,128)S(1)} %select_add_fusion), channel_id=1, source_target_pairs={{8,0},{12,4},{16,8},{20,12},{24,16},{28,20},{9,1},{13,5},{17,9},{2... | collective-permute-start | bytes 1179656 | tf_op jit(solution)/shard_map/ppermute | solution.py:482
  312.8 33.5 %collective-permute-start.37 = (f32[2,128,768]{2,1,0:T(8,128)}, f32[2,128,768]{2,1,0:T(8,128)}, u32[]{:S(2)}, u32[]{:S(2)}) collective-permute-start(f32[2,128,768]{2,1,0:T(8,128)} %fusion.84), channel_id=1, source_target_pairs={{0,1},{1,0},{2,3},{3,2},{4,5},{5,4},{6,7},{7,6},{8,9},{9,8},{10,11... | collective-permute-start | bytes 2359304 | tf_op jit(solution)/shard_map/ppermute | solution.py:486
  330.9 22.6 %collective-permute-start.35 = (f32[2,128,768]{2,1,0:T(8,128)}, f32[2,128,768]{2,1,0:T(8,128)}, u32[]{:S(2)}, u32[]{:S(2)}) collective-permute-start(f32[2,128,768]{2,1,0:T(8,128)} %add.432), channel_id=1, source_target_pairs={{0,2},{1,3},{2,0},{3,1},{4,6},{5,7},{6,4},{7,5},{8,10},{9,11},{10,... | collective-permute-start | bytes 2359304 | tf_op jit(solution)/shard_map/ppermute | solution.py:486
  332.8 20.7 %collective-permute-start.38 = (f32[48,16,128]{2,1,0:T(8,128)}, f32[48,16,128]{2,1,0:T(8,128)S(1)}, u32[]{:S(2)}, u32[]{:S(2)}) collective-permute-start(f32[48,16,128]{2,1,0:T(8,128)} %multiply_add_fusion.2), channel_id=1, source_target_pairs={{16,0},{20,4},{24,8},{28,12},{17,1},{21,5},{25,9},{29,13},{18,2},{... | collective-permute-start | bytes 1179656 | tf_op jit(solution)/shard_map/ppermute | solution.py:482
  335.0 23.9 %collective-permute-start.27 = (f32[2,128,768]{2,1,0:T(8,128)}, f32[2,128,768]{2,1,0:T(8,128)}, u32[]{:S(2)}, u32[]{:S(2)}) collective-permute-start(f32[2,128,768]{2,1,0:T(8,128)} %fusion.76), channel_id=1, source_target_pairs={{0,1},{1,0},{2,3},{3,2},{4,5},{5,4},{6,7},{7,6},{8,9},{9,8},{10,11... | collective-permute-start | bytes 2359304 | tf_op jit(solution)/shard_map/ppermute | solution.py:486
  353.5 17.2 %collective-permute-start.39 = (f32[2,128,768]{2,1,0:T(8,128)}, f32[2,128,768]{2,1,0:T(8,128)}, u32[]{:S(2)}, u32[]{:S(2)}) collective-permute-start(f32[2,128,768]{2,1,0:T(8,128)} %add_select_fusion.refs_0_), channel_id=1, source_target_pairs={{0,2},{1,3},{2,0},{3,1},{4,6},{5,7},{6,4},{7,5},{8,10},{9,11},{10,... | collective-permute-start | bytes 2359304 | tf_op jit(solution)/shard_map/ppermute | solution.py:486
  357.8 12.6 %collective-permute-start.40 = (f32[48,16,128]{2,1,0:T(8,128)S(1)}, f32[48,16,128]{2,1,0:T(8,128)S(1)}, u32[]{:S(2)}, u32[]{:S(2)}) collective-permute-start(f32[48,16,128]{2,1,0:T(8,128)S(1)} %fusion.136), channel_id=1, source_target_pairs={{0,4},{4,0},{8,12},{12,8},{16,20},{20,16},{24,28},{28,24},{1,5},{5... | collective-permute-start | bytes 1179656 | tf_op jit(solution)/shard_map/ppermute | solution.py:486
  372.4 21.5 %collective-permute-start.41 = (f32[2,128,768]{2,1,0:T(8,128)}, f32[2,128,768]{2,1,0:T(8,128)S(1)}, u32[]{:S(2)}, u32[]{:S(2)}) collective-permute-start(f32[2,128,768]{2,1,0:T(8,128)} %add_select_fusion.1.refs_0_), channel_id=1, source_target_pairs={{0,2},{1,3},{2,0},{3,1},{4,6},{5,7},{6,4},{7,5},{8,10},{9,11},{10,... | collective-permute-start | bytes 2359304 | tf_op jit(solution)/shard_map/ppermute | solution.py:486
  374.6 19.3 %collective-permute-start.46 = (f32[192,768]{1,0:T(8,128)S(1)}, f32[192,768]{1,0:T(8,128)S(1)}, u32[]{:S(2)}, u32[]{:S(2)}) collective-permute-start(f32[192,768]{1,0:T(8,128)S(1)} %constant_dynamic-slice_fusion.7), channel_id=1, source_target_pairs={{0,4},{4,0},{8,12},{12,8},{16,20},{20,16},{24,28},{28,24},{1,5},{5... | collective-permute-start | bytes 1769480 | tf_op jit(solution)/shard_map/ppermute | solution.py:486
  376.5 42.1 %collective-permute-start.43 = (f32[2,128,768]{2,1,0:T(8,128)S(1)}, f32[2,128,768]{2,1,0:T(8,128)}, u32[]{:S(2)}, u32[]{:S(2)}) collective-permute-start(f32[2,128,768]{2,1,0:T(8,128)S(1)} %copy-done.25), channel_id=1, source_target_pairs={{0,1},{1,0},{2,3},{3,2},{4,5},{5,4},{6,7},{7,6},{8,9},{9,8},{10,11... | collective-permute-start | bytes 2359304 | tf_op jit(solution)/shard_map/ppermute | solution.py:486
  376.5 45.6 %collective-permute-start.36 = (f32[2,128,768]{2,1,0:T(8,128)}, f32[2,128,768]{2,1,0:T(8,128)}, u32[]{:S(2)}, u32[]{:S(2)}) collective-permute-start(f32[2,128,768]{2,1,0:T(8,128)} %add_select_fusion.1.refs_0_), channel_id=1, source_target_pairs={{0,1},{1,0},{2,3},{3,2},{4,5},{5,4},{6,7},{7,6},{8,9},{9,8},{10,11... | collective-permute-start | bytes 2359304 | tf_op jit(solution)/shard_map/ppermute | solution.py:486
  385.4 8.5 %collective-permute-start.45 = (f32[192,128]{1,0:T(8,128)}, f32[192,128]{1,0:T(8,128)S(1)}, u32[]{:S(2)}, u32[]{:S(2)}) collective-permute-start(f32[192,128]{1,0:T(8,128)} %get-tuple-element.195), channel_id=1, source_target_pairs={{4,0},{8,4},{12,8},{16,12},{20,16},{24,20},{28,24},{5,1},{9,5},{13... | collective-permute-start | bytes 294920 | tf_op jit(solution)/shard_map/ppermute | solution.py:482
  410.0 15.6 %collective-permute-start.44 = (f32[2,128,768]{2,1,0:T(8,128)}, f32[2,128,768]{2,1,0:T(8,128)}, u32[]{:S(2)}, u32[]{:S(2)}) collective-permute-start(f32[2,128,768]{2,1,0:T(8,128)} %collective-permute-done.39.refs_2_), channel_id=1, source_target_pairs={{0,1},{1,0},{2,3},{3,2},{4,5},{5,4},{6,7},{7,6},{8,9},{9,8},{10,11... | collective-permute-start | bytes 2359304 | tf_op jit(solution)/shard_map/ppermute | solution.py:486
  410.6 15.1 %collective-permute-start.48 = (f32[2,128,768]{2,1,0:T(8,128)}, f32[2,128,768]{2,1,0:T(8,128)}, u32[]{:S(2)}, u32[]{:S(2)}) collective-permute-start(f32[2,128,768]{2,1,0:T(8,128)} %get-tuple-element.203), channel_id=1, source_target_pairs={{0,1},{1,0},{2,3},{3,2},{4,5},{5,4},{6,7},{7,6},{8,9},{9,8},{10,11... | collective-permute-start | bytes 2359304 | tf_op jit(solution)/shard_map/ppermute | solution.py:486
  412.3 13.4 %collective-permute-start.42 = (f32[2,128,768]{2,1,0:T(8,128)}, f32[2,128,768]{2,1,0:T(8,128)S(1)}, u32[]{:S(2)}, u32[]{:S(2)}) collective-permute-start(f32[2,128,768]{2,1,0:T(8,128)} %copy-done.43), channel_id=1, source_target_pairs={{0,1},{1,0},{2,3},{3,2},{4,5},{5,4},{6,7},{7,6},{8,9},{9,8},{10,11... | collective-permute-start | bytes 2359304 | tf_op jit(solution)/shard_map/ppermute | solution.py:486
  418.6 17.0 %collective-permute-start.50 = (f32[48,768]{1,0:T(8,128)S(1)}, f32[48,768]{1,0:T(8,128)S(1)}, u32[]{:S(2)}, u32[]{:S(2)}) collective-permute-start(f32[48,768]{1,0:T(8,128)S(1)} %get-tuple-element.207), channel_id=1, source_target_pairs={{0,8},{4,12},{8,0},{12,4},{16,24},{20,28},{24,16},{28,20},{1,9},{5... | collective-permute-start | bytes 442376 | tf_op jit(solution)/shard_map/ppermute | solution.py:486
  422.1 28.5 %collective-permute-start.53 = (f32[224,768]{1,0:T(8,128)}, f32[224,768]{1,0:T(8,128)}, u32[]{:S(2)}, u32[]{:S(2)}) collective-permute-start(f32[224,768]{1,0:T(8,128)} %constant_dynamic-slice_fusion.3), channel_id=1, source_target_pairs={{0,4},{4,0},{8,12},{12,8},{16,20},{20,16},{24,28},{28,24},{1,5},{5... | collective-permute-start | bytes 2064392 | tf_op jit(solution)/shard_map/ppermute | solution.py:486
  425.6 29.5 %collective-permute-start.60 = (f32[2,128,768]{2,1,0:T(8,128)}, f32[2,128,768]{2,1,0:T(8,128)}, u32[]{:S(2)}, u32[]{:S(2)}) collective-permute-start(f32[2,128,768]{2,1,0:T(8,128)} %get-tuple-element.224), channel_id=1, source_target_pairs={{0,1},{1,0},{2,3},{3,2},{4,5},{5,4},{6,7},{7,6},{8,9},{9,8},{10,11... | collective-permute-start | bytes 2359304 | tf_op jit(solution)/shard_map/ppermute | solution.py:486
  425.7 27.4 %collective-permute-start.54 = (f32[2,128,768]{2,1,0:T(8,128)}, f32[2,128,768]{2,1,0:T(8,128)}, u32[]{:S(2)}, u32[]{:S(2)}) collective-permute-start(f32[2,128,768]{2,1,0:T(8,128)} %add.453), channel_id=1, source_target_pairs={{0,2},{1,3},{2,0},{3,1},{4,6},{5,7},{6,4},{7,5},{8,10},{9,11},{10,... | collective-permute-start | bytes 2359304 | tf_op jit(solution)/shard_map/ppermute | solution.py:486
  425.7 24.7 %collective-permute-start.51 = (f32[48,768]{1,0:T(8,128)S(1)}, f32[48,768]{1,0:T(8,128)S(1)}, u32[]{:S(2)}, u32[]{:S(2)}) collective-permute-start(f32[48,768]{1,0:T(8,128)S(1)} %get-tuple-element.208), channel_id=1, source_target_pairs={{0,16},{4,20},{8,24},{12,28},{16,0},{20,4},{24,8},{28,12},{1,17},{... | collective-permute-start | bytes 442376 | tf_op jit(solution)/shard_map/ppermute | solution.py:486
  435.6 14.8 %collective-permute-start.52 = (f32[48,768]{1,0:T(8,128)S(1)}, f32[48,768]{1,0:T(8,128)S(1)}, u32[]{:S(2)}, u32[]{:S(2)}) collective-permute-start(f32[48,768]{1,0:T(8,128)S(1)} %get-tuple-element.209), channel_id=1, source_target_pairs={{0,24},{4,28},{8,16},{12,20},{16,8},{20,12},{24,0},{28,4},{1,25},{... | collective-permute-start | bytes 442376 | tf_op jit(solution)/shard_map/ppermute | solution.py:486
  450.4 11.7 %collective-permute-start.47 = (f32[2,128,768]{2,1,0:T(8,128)}, f32[2,128,768]{2,1,0:T(8,128)S(1)}, u32[]{:S(2)}, u32[]{:S(2)}) collective-permute-start(f32[2,128,768]{2,1,0:T(8,128)} %get-tuple-element.201), channel_id=1, source_target_pairs={{0,1},{1,0},{2,3},{3,2},{4,5},{5,4},{6,7},{7,6},{8,9},{9,8},{10,11... | collective-permute-start | bytes 2359304 | tf_op jit(solution)/shard_map/ppermute | solution.py:486
  453.1 19.4 %collective-permute-start.55 = (f32[2,128,768]{2,1,0:T(8,128)S(1)}, f32[2,128,768]{2,1,0:T(8,128)S(1)}, u32[]{:S(2)}, u32[]{:S(2)}) collective-permute-start(f32[2,128,768]{2,1,0:T(8,128)S(1)} %copy-done.57), channel_id=1, source_target_pairs={{0,2},{1,3},{2,0},{3,1},{4,6},{5,7},{6,4},{7,5},{8,10},{9,11},{10,... | collective-permute-start | bytes 2359304 | tf_op jit(solution)/shard_map/ppermute | solution.py:486
  453.2 23.2 %collective-permute-start.62 = (f32[48,768]{1,0:T(8,128)S(1)}, f32[48,768]{1,0:T(8,128)S(1)}, u32[]{:S(2)}, u32[]{:S(2)}) collective-permute-start(f32[48,768]{1,0:T(8,128)S(1)} %get-tuple-element.225), channel_id=1, source_target_pairs={{0,16},{4,20},{8,24},{12,28},{16,0},{20,4},{24,8},{28,12},{1,17},{... | collective-permute-start | bytes 442376 | tf_op jit(solution)/shard_map/ppermute | solution.py:486
  455.2 21.3 %collective-permute-start.63 = (f32[48,768]{1,0:T(8,128)S(1)}, f32[48,768]{1,0:T(8,128)S(1)}, u32[]{:S(2)}, u32[]{:S(2)}) collective-permute-start(f32[48,768]{1,0:T(8,128)S(1)} %get-tuple-element.225), channel_id=1, source_target_pairs={{0,24},{4,28},{8,16},{12,20},{16,8},{20,12},{24,0},{28,4},{1,25},{... | collective-permute-start | bytes 442376 | tf_op jit(solution)/shard_map/ppermute | solution.py:486
  460.4 16.1 %collective-permute-start.59 = (f32[56,768]{1,0:T(8,128)S(1)}, f32[56,768]{1,0:T(8,128)S(1)}, u32[]{:S(2)}, u32[]{:S(2)}) collective-permute-start(f32[56,768]{1,0:T(8,128)S(1)} %get-tuple-element.222), channel_id=1, source_target_pairs={{0,24},{4,28},{8,16},{12,20},{16,8},{20,12},{24,0},{28,4},{1,25},{... | collective-permute-start | bytes 516104 | tf_op jit(solution)/shard_map/ppermute | solution.py:486
  462.2 21.9 %collective-permute-start.58 = (f32[56,768]{1,0:T(8,128)S(1)}, f32[56,768]{1,0:T(8,128)S(1)}, u32[]{:S(2)}, u32[]{:S(2)}) collective-permute-start(f32[56,768]{1,0:T(8,128)S(1)} %get-tuple-element.221), channel_id=1, source_target_pairs={{0,16},{4,20},{8,24},{12,28},{16,0},{20,4},{24,8},{28,12},{1,17},{... | collective-permute-start | bytes 516104 | tf_op jit(solution)/shard_map/ppermute | solution.py:486
  472.5 11.6 %collective-permute-start.57 = (f32[56,768]{1,0:T(8,128)S(1)}, f32[56,768]{1,0:T(8,128)S(1)}, u32[]{:S(2)}, u32[]{:S(2)}) collective-permute-start(f32[56,768]{1,0:T(8,128)S(1)} %get-tuple-element.220), channel_id=1, source_target_pairs={{0,8},{4,12},{8,0},{12,4},{16,24},{20,28},{24,16},{28,20},{1,9},{5... | collective-permute-start | bytes 516104 | tf_op jit(solution)/shard_map/ppermute | solution.py:486
  484.1 19.6 %collective-permute-start.68 = (f32[2,128,768]{2,1,0:T(8,128)}, f32[2,128,768]{2,1,0:T(8,128)}, u32[]{:S(2)}, u32[]{:S(2)}) collective-permute-start(f32[2,128,768]{2,1,0:T(8,128)} %get-tuple-element.226.refs_0_), channel_id=1, source_target_pairs={{0,2},{1,3},{2,0},{3,1},{4,6},{5,7},{6,4},{7,5},{8,10},{9,11},{10,... | collective-permute-start | bytes 2359304 | tf_op jit(solution)/shard_map/ppermute | solution.py:486
  487.3 7.2 %collective-permute-start.64 = (f32[56,768]{1,0:T(8,128)S(1)}, f32[56,768]{1,0:T(8,128)S(1)}, u32[]{:S(2)}, u32[]{:S(2)}) collective-permute-start(f32[56,768]{1,0:T(8,128)S(1)} %get-tuple-element.227), channel_id=1, source_target_pairs={{0,8},{4,12},{8,0},{12,4},{16,24},{20,28},{24,16},{28,20},{1,9},{5... | collective-permute-start | bytes 516104 | tf_op jit(solution)/shard_map/ppermute | solution.py:486
  487.4 15.0 %collective-permute-start.65 = (f32[56,768]{1,0:T(8,128)S(1)}, f32[56,768]{1,0:T(8,128)S(1)}, u32[]{:S(2)}, u32[]{:S(2)}) collective-permute-start(f32[56,768]{1,0:T(8,128)S(1)} %get-tuple-element.227), channel_id=1, source_target_pairs={{0,16},{4,20},{8,24},{12,28},{16,0},{20,4},{24,8},{28,12},{1,17},{... | collective-permute-start | bytes 516104 | tf_op jit(solution)/shard_map/ppermute | solution.py:486
  489.5 13.6 %collective-permute-start.66 = (f32[56,768]{1,0:T(8,128)S(1)}, f32[56,768]{1,0:T(8,128)S(1)}, u32[]{:S(2)}, u32[]{:S(2)}) collective-permute-start(f32[56,768]{1,0:T(8,128)S(1)} %get-tuple-element.227), channel_id=1, source_target_pairs={{0,24},{4,28},{8,16},{12,20},{16,8},{20,12},{24,0},{28,4},{1,25},{... | collective-permute-start | bytes 516104 | tf_op jit(solution)/shard_map/ppermute | solution.py:486
  491.9 21.3 %collective-permute-start.70 = (f32[2,128,768]{2,1,0:T(8,128)}, f32[2,128,768]{2,1,0:T(8,128)}, u32[]{:S(2)}, u32[]{:S(2)}) collective-permute-start(f32[2,128,768]{2,1,0:T(8,128)} %get-tuple-element.226.refs_0_), channel_id=1, source_target_pairs={{0,1},{1,0},{2,3},{3,2},{4,5},{5,4},{6,7},{7,6},{8,9},{9,8},{10,11... | collective-permute-start | bytes 2359304 | tf_op jit(solution)/shard_map/ppermute | solution.py:486
  494.6 14.1 %collective-permute-start.67 = (f32[192,768]{1,0:T(8,128)S(1)}, f32[192,768]{1,0:T(8,128)S(1)}, u32[]{:S(2)}, u32[]{:S(2)}) collective-permute-start(f32[192,768]{1,0:T(8,128)S(1)} %constant_dynamic-update-slice_fusion.8), channel_id=1, source_target_pairs={{0,4},{4,0},{8,12},{12,8},{16,20},{20,16},{24,28},{28,24},{1,5},{5... | collective-permute-start | bytes 1769480 | tf_op jit(solution)/shard_map/ppermute | solution.py:486
  503.8 9.4 %collective-permute-start.71 = (f32[2,128,768]{2,1,0:T(8,128)}, f32[2,128,768]{2,1,0:T(8,128)}, u32[]{:S(2)}, u32[]{:S(2)}) collective-permute-start(f32[2,128,768]{2,1,0:T(8,128)} %collective-permute-done.68.refs_2_), channel_id=1, source_target_pairs={{0,1},{1,0},{2,3},{3,2},{4,5},{5,4},{6,7},{7,6},{8,9},{9,8},{10,11... | collective-permute-start | bytes 2359304 | tf_op jit(solution)/shard_map/ppermute | solution.py:486
  508.6 18.2 %collective-permute-start.73 = (f32[224,768]{1,0:T(8,128)}, f32[224,768]{1,0:T(8,128)}, u32[]{:S(2)}, u32[]{:S(2)}) collective-permute-start(f32[224,768]{1,0:T(8,128)} %constant_dynamic-update-slice_fusion.4), channel_id=1, source_target_pairs={{0,4},{4,0},{8,12},{12,8},{16,20},{20,16},{24,28},{28,24},{1,5},{5... | collective-permute-start | bytes 2064392 | tf_op jit(solution)/shard_map/ppermute | solution.py:486
  509.9 19.8 %collective-permute-start.69 = (f32[2,128,768]{2,1,0:T(8,128)S(1)}, f32[2,128,768]{2,1,0:T(8,128)}, u32[]{:S(2)}, u32[]{:S(2)}) collective-permute-start(f32[2,128,768]{2,1,0:T(8,128)S(1)} %get-tuple-element.230.refs_0_), channel_id=1, source_target_pairs={{0,2},{1,3},{2,0},{3,1},{4,6},{5,7},{6,4},{7,5},{8,10},{9,11},{10,... | collective-permute-start | bytes 2359304 | tf_op jit(solution)/shard_map/ppermute | solution.py:486
  510.6 25.8 %collective-permute-start.56 = (f32[2,128,768]{2,1,0:T(8,128)S(1)}, f32[2,128,768]{2,1,0:T(8,128)}, u32[]{:S(2)}, u32[]{:S(2)}) collective-permute-start(f32[2,128,768]{2,1,0:T(8,128)S(1)} %get-tuple-element.230.refs_0_), channel_id=1, source_target_pairs={{0,1},{1,0},{2,3},{3,2},{4,5},{5,4},{6,7},{7,6},{8,9},{9,8},{10,11... | collective-permute-start | bytes 2359304 | tf_op jit(solution)/shard_map/ppermute | solution.py:486
  (102 other events, 999.1 us)
Sparse Core Ops, SparseCore 0:
  209.1 108.9 reduce-scatter.1
  354.7 83.7 all-gather.1
